TPU v7x, 32 devices: a whole 2x2x4 slice. The times are simulated.
32 devices in a mesh: group: 2 (over y), tm: 4 (over z), tensor: 2 (over x), dp: 2 (over core).
Axes of the slice: x: 2, y: 2, z: 4, core: 2. Of those that a mesh axis runs over, the one named last changes fastest.
Arguments:
- frames_in: bfloat16 [4, 3072, 1024], P(('group', 'dp'), 'tm', 'tensor'), parts along dimension 0, may hold values from -6 to 6
- in_proj: bfloat16 [2, 1024, 1024], P(None, None, 'tensor'), may hold values from -0.1875 to 0.1875
- log_rates: float32 [8, 8], P(None, 'tensor'), as said below
- angles: float32 [8, 8], P(None, 'tensor'), may hold values from -3.140625 to 3.140625
- residues: float32 [2, 8, 1024], P(None, None, 'tensor'), may hold values from -3 to 3
- skip_gain: float32 [1024], P('tensor'), may hold values from -3 to 3
- lengths: int32 [4, 4], P(('group', 'dp')), parts along dimension 0, may hold values from 1 to 1536, 3072 in all within a row
- grad_out: bfloat16 [4, 3072, 1024], P(('group', 'dp'), 'tm', 'tensor'), parts along dimension 0, may hold values from -6 to 6
Outputs:
- mixed: bfloat16 [4, 3072, 1024], P(('group', 'dp'), 'tm', 'tensor'), parts along dimension 0
- input_grad: bfloat16 [4, 3072, 1024], P(('group', 'dp'), 'tm', 'tensor'), parts along dimension 0
- proj_grad: float32 [4, 1024, 1024], P('group', None, 'tensor'), parts along dimension 0
- residue_grad: float32 [4, 8, 1024], P('group', None, 'tensor'), parts along dimension 0
- skip_grad: float32 [2048], P(('group', 'tensor')), parts along dimension 0
There are 2 independent parts, one for each index of `group`. A program takes and returns all parts, laid end to end along the dimension named above; an argument that names none is the same for every part. Nothing has to cross between parts.
Inputs may be any that keep to these rules, and one draw needn't show every extreme that they name: Each clip has at least one frame; the lengths of a stream sum to 3072. `log_rates`: each entry lies between the logarithms of 0.1 / 3072 and 0.08.
All inputs are finite; a program needn't handle non-finite values.
Results may differ from a plain program's by a relative error of at most 0.0058.
Values may be sent and summed in bfloat16 or wider, within the bound.
A program may use at most 128 MiB of HBM per device.

v0:
```python
import math

import jax
import jax.numpy as jnp
from jax import lax
from jax.sharding import PartitionSpec as P

BLOCK_LEN = 128


def carried_in(value, axis, join, neutral, backward):
    count, mine = (lax.axis_size(axis), lax.axis_index(axis))
    pieces = jax.tree.map(lambda part: lax.all_gather(part, axis), value)
    if backward:
        pieces = jax.tree.map(lambda part: part[::-1], pieces)
        mine = count - 1 - mine
    total = jax.tree.map(
        lambda part, zero: jnp.full_like(part, 0) + jnp.asarray(zero, part.dtype), value, neutral
    )

    def lap(position, total):
        longer = join(total, jax.tree.map(lambda part: part[position], pieces))
        return jax.tree.map(lambda new, old: jnp.where(position < mine, new, old), longer, total)

    return lax.fori_loop(0, count - 1, lap, total)


def compose(earlier_map, later_map):
    early_re, early_im, early_sre, early_sim = earlier_map
    late_re, late_im, late_sre, late_sim = later_map
    return (
        late_re * early_re - late_im * early_im,
        late_re * early_im + late_im * early_re,
        late_re[..., None] * early_sre - late_im[..., None] * early_sim + late_sre,
        late_re[..., None] * early_sim + late_im[..., None] * early_sre + late_sim,
    )


def shards(frames_in, in_proj, log_rates, angles, residues, skip_gain, lengths, grad_out):
    rows_dev = frames_in.shape[1]
    channels = frames_in.shape[2]
    modes_dev, heads_dev = log_rates.shape
    head_width = channels // heads_dev
    block_count = rows_dev // BLOCK_LEN
    largest_value = lax.Precision.HIGHEST
    features = lax.all_gather(frames_in, "tensor", axis=2, tiled=True)[0]
    projected = jnp.einsum("ld,kdc->klc", features, in_proj, preferred_element_type=jnp.float32)
    query_rows = projected[0].astype(jnp.bfloat16)
    signal = projected[1].astype(jnp.bfloat16)
    decay_rate = jnp.exp(log_rates)
    weight = jnp.sqrt(-jnp.expm1(-2.0 * decay_rate))
    later_idx = lax.broadcasted_iota(jnp.int32, (BLOCK_LEN, BLOCK_LEN), 0)
    earlier_idx = lax.broadcasted_iota(jnp.int32, (BLOCK_LEN, BLOCK_LEN), 1)
    causal = later_idx >= earlier_idx
    lag_steps = jnp.maximum(later_idx - earlier_idx, 0).astype(jnp.float32)
    damping = jnp.where(causal, jnp.exp(-decay_rate[:, :, None, None] * lag_steps), 0.0)
    kern_re = damping * jnp.cos(angles[:, :, None, None] * lag_steps)
    kern_im = damping * jnp.sin(angles[:, :, None, None] * lag_steps)
    exponents = jnp.arange(1, rows_dev + 1, dtype=jnp.int32).astype(jnp.float32)
    exponent_real = jnp.exp(-decay_rate[:, :, None] * exponents) * jnp.cos(
        angles[:, :, None] * exponents
    )
    exponent_imaginary = jnp.exp(-decay_rate[:, :, None] * exponents) * jnp.sin(
        angles[:, :, None] * exponents
    )
    block_re = exponent_real[:, :, :BLOCK_LEN]
    block_im = exponent_imaginary[:, :, :BLOCK_LEN]
    clip_start = jnp.cumsum(lengths[0]) - lengths[0]
    first_frame = lax.axis_index("tm") * rows_dev
    frame_ids = first_frame + jnp.arange(rows_dev, dtype=jnp.int32)
    segment = jnp.sum((frame_ids[:, None] >= clip_start[None, :]).astype(jnp.int32), axis=1) - 1
    segment_before = jnp.sum((first_frame - 1 >= clip_start).astype(jnp.int32)) - 1
    seg_blocks = segment.reshape(block_count, BLOCK_LEN)
    seg_prior = jnp.concatenate([segment_before[None], seg_blocks[:-1, -1]])
    alive_dev = (segment == segment_before).astype(jnp.float32)
    carry_re = exponent_real[:, :, -1] * alive_dev[-1]
    carry_im = exponent_imaginary[:, :, -1] * alive_dev[-1]

    def split_coeffs(coeffs):
        coefficient_real = coeffs[0].reshape(modes_dev, heads_dev, head_width) * weight[:, :, None]
        coefficient_imaginary = (
            coeffs[1].reshape(modes_dev, heads_dev, head_width) * weight[:, :, None]
        )
        return (coefficient_real, coefficient_imaginary)

    def intra(signal32, coeffs, skip_vec):
        coefficient_real, coefficient_imaginary = split_coeffs(coeffs)
        skip_row = skip_vec.reshape(heads_dev, head_width)

        def block_step(carried, element):
            state_re, state_im = carried
            block_in, block_seg, prior_seg = element
            same_clip = (block_seg[:, None] == block_seg[None, :]).astype(jnp.float32)
            alive_mask = (block_seg == prior_seg).astype(jnp.float32)[None, None, :, None]
            inner_re = jnp.einsum(
                "mhts,shd->mhtd", kern_re * same_clip, block_in, precision=largest_value
            )
            inner_im = jnp.einsum(
                "mhts,shd->mhtd", kern_im * same_clip, block_in, precision=largest_value
            )
            aggregate_real = inner_re + alive_mask * (
                block_re[..., None] * state_re[:, :, None, :]
                - block_im[..., None] * state_im[:, :, None, :]
            )
            aggregate_imaginary = inner_im + alive_mask * (
                block_re[..., None] * state_im[:, :, None, :]
                + block_im[..., None] * state_re[:, :, None, :]
            )
            output = (
                skip_row * block_in
                + jnp.einsum(
                    "ywo,ywlo->lwo", coefficient_real, aggregate_real, precision=largest_value
                )
                - jnp.einsum(
                    "ywo,ywlo->lwo",
                    coefficient_imaginary,
                    aggregate_imaginary,
                    precision=largest_value,
                )
            )
            return ((aggregate_real[:, :, -1, :], aggregate_imaginary[:, :, -1, :]), output)

        initial = jnp.zeros((modes_dev, heads_dev, head_width), jnp.float32)
        blocks_in = signal32.reshape(block_count, BLOCK_LEN, heads_dev, head_width)
        final_state, outputs = lax.scan(
            jax.checkpoint(block_step), (initial, initial), (blocks_in, seg_blocks, seg_prior)
        )
        return (outputs.reshape(rows_dev, heads_dev, head_width), final_state)

    def carry_part(coeffs, enter_re, enter_im):
        coefficient_real, coefficient_imaginary = split_coeffs(coeffs)
        blended_real = coefficient_real * enter_re - coefficient_imaginary * enter_im
        blended_imaginary = coefficient_real * enter_im + coefficient_imaginary * enter_re
        carried_contribution = jnp.einsum(
            "zan,zas->nas", exponent_real, blended_real, precision=largest_value
        ) - jnp.einsum(
            "zan,zas->nas", exponent_imaginary, blended_imaginary, precision=largest_value
        )
        carried_contribution = carried_contribution * alive_dev[:, None, None]
        leave_re = carry_re[:, :, None] * enter_re - carry_im[:, :, None] * enter_im
        leave_im = carry_re[:, :, None] * enter_im + carry_im[:, :, None] * enter_re
        return (carried_contribution, (leave_re, leave_im))

    signal32 = signal.astype(jnp.float32)
    (local_out, local_end), pull_local = jax.vjp(intra, signal32, residues, skip_gain)
    identity = (
        jnp.ones_like(carry_re),
        jnp.zeros_like(carry_re),
        jnp.zeros_like(local_end[0]),
        jnp.zeros_like(local_end[0]),
    )
    entering = carried_in(
        (carry_re, carry_im, local_end[0], local_end[1]), "tm", compose, identity, False
    )
    enter_re, enter_im = (entering[2], entering[3])
    carry_result, pull_carry = jax.vjp(carry_part, residues, enter_re, enter_im)
    long_out = (local_out + carry_result[0]).reshape(rows_dev, channels)
    query32 = query_rows.astype(jnp.float32)
    upstream = grad_out[0].astype(jnp.float32)
    mixed = (query32 * long_out).astype(jnp.bfloat16)
    grad_long = (upstream * query32).reshape(rows_dev, heads_dev, head_width)
    grad_query = (upstream * long_out).astype(jnp.bfloat16)
    zero_state = jnp.zeros_like(enter_re)
    _, adjoint_re, adjoint_im = pull_carry((grad_long, (zero_state, zero_state)))
    leaving = carried_in(
        (carry_re, -carry_im, adjoint_re, adjoint_im), "tm", compose, identity, True
    )
    end_re, end_im = (leaving[2], leaving[3])
    coeff_carry, _, _ = pull_carry((grad_long, (end_re, end_im)))
    grad_signal, coeff_local, skip_local = pull_local((grad_long, (end_re, end_im)))
    grad_value = grad_signal.astype(jnp.bfloat16)
    stacked = jnp.stack([grad_query, grad_value])
    partial_in = jnp.einsum("klc,kdc->ld", stacked, in_proj, preferred_element_type=jnp.float32)
    input_grad = lax.psum_scatter(
        partial_in[None], "tensor", scatter_dimension=2, tiled=True
    ).astype(jnp.bfloat16)
    norm_scale = 1.0 / math.sqrt(rows_dev * lax.axis_size("tm") * lax.axis_size("dp"))
    proj_term = (
        jnp.einsum("ld,klc->kdc", features, stacked, preferred_element_type=jnp.float32)
        * norm_scale
    )
    coeff_term = (coeff_local + coeff_carry) * norm_scale
    skip_term = skip_local * norm_scale
    proj_sum, coeff_sum, skip_sum = lax.psum((proj_term, coeff_term, skip_term), ("tm", "dp"))
    return (mixed[None], input_grad, proj_sum, coeff_sum, skip_sum)


def solution(mesh):
    in_specs = (
        P(("group", "dp"), "tm", "tensor"),
        P(None, None, "tensor"),
        P(None, "tensor"),
        P(None, "tensor"),
        P(None, None, "tensor"),
        P("tensor"),
        P(("group", "dp"), None),
        P(("group", "dp"), "tm", "tensor"),
    )
    out_specs = (
        P(("group", "dp"), "tm", "tensor"),
        P(("group", "dp"), "tm", "tensor"),
        P("group", None, "tensor"),
        P("group", None, "tensor"),
        P(("group", "tensor")),
    )
    return jax.shard_map(shards, mesh=mesh, in_specs=in_specs, out_specs=out_specs, check_vma=False)
```

profile of v0, /device:TPU:0, one launch (start us, length us, event | category | flops | bytes accessed | tf_op | source)
XLA Modules:
  0.0 767.0 jit_solution(7219482252016499978)
XLA Ops:
  13.0 14.9 %all-gather = f32[32,4,1]{2,0,1:T(8,128)S(1)} all-gather(f32[8,4,1]{2,0,1:T(8,128)S(1)} %get-tuple-element.1668), channel_id=2, replica_groups=mesh['group'=2,'tm'=4,'tensor'=2,'dp'=2] {'tm'}, dimensions={0}, use_global_device_ids=true | all-gather | bytes 640 | tf_op jit(solution)/shard_map/all_gather | solution.py:13
  28.0 13.3 %all-gather.1 = f32[32,4,1]{2,0,1:T(8,128)S(1)} all-gather(f32[8,4,1]{2,0,1:T(8,128)S(1)} %get-tuple-element.1667), channel_id=3, replica_groups=mesh['group'=2,'tm'=4,'tensor'=2,'dp'=2] {'tm'}, dimensions={0}, use_global_device_ids=true | all-gather | bytes 640 | tf_op jit(solution)/shard_map/all_gather | solution.py:13
  41.6 13.2 %all-gather.6 = f32[32,4,1]{2,0,1:T(8,128)S(1)} all-gather(f32[8,4,1]{2,0,1:T(8,128)S(1)} %neg.55), channel_id=8, replica_groups=mesh['group'=2,'tm'=4,'tensor'=2,'dp'=2] {'tm'}, dimensions={0}, use_global_device_ids=true | all-gather | bytes 640 | tf_op jit(solution)/shard_map/all_gather | solution.py:13
  79.1 145.3 %while.82 = (s32[]{:T(128)}, f32[8,4,128]{2,0,1:T(8,128)S(1)}, f32[8,4,128]{2,0,1:T(8,128)S(1)}, f32[6,128,4,128]{3,1,0,2:T(8,128)}, f32[6,8,4,128]{3,1,2,0:T(8,...) while((s32[]{:T(128)}, f32[8,4,128]{2,0,1:T(8,128)S(1)}, ...), condition=%wide.region_4.5_spmd.clone.clone, body=%wide.region_3.4_spmd.clone.clone.sunk | while | flops 1623294208 | bytes 7542485 | solution.py:125
  82.1 10.2 %multiply_reduce_fusion.11 = (f32[4,128,128]{1,2,0:T(8,128)S(1)}, f32[8,4,128,128]{3,2,0,1:T(8,128)S(1)}) fusion(f32[4,128,8]{1,2,0:T(8,128)S(1)} %copy.360, f32[8,4,128]{2,0,1:T(8,128)S(1)} %get-tuple-element.2158, f32[8,4,128]{2,0,1:T(8,128)S(1)} %bitcast.427, f32[8,4,128]{2,0,1:T(8,128)S(1)} %get-tuple-element.2159, ...), kind=kOutput, calls=%fused_computation.88.clone.1 | convolution fusion | flops 811532288 | bytes 2851584 | tf_op jit(solution)/shard_map/jvp()/while/body/eval_jaxpr/mhts,shd->mhtd/dot_general | solution.py:98
  92.3 10.3 %multiply_reduce_fusion.10 = (f32[4,128,128]{1,2,0:T(8,128)S(1)}, f32[8,4,128,128]{3,2,0,1:T(8,128)S(1)}) fusion(f32[4,128,8]{1,2,0:T(8,128)S(1)} %copy.359, f32[8,4,128]{2,0,1:T(8,128)S(1)} %get-tuple-element.2159, f32[8,4,128]{2,0,1:T(8,128)S(1)} %bitcast.428, f32[8,4,128]{2,0,1:T(8,128)S(1)} %get-tuple-element.2158, ...), kind=kOutput, calls=%fused_computation.89.clone.1 | convolution fusion | flops 811532288 | bytes 2851584 | tf_op jit(solution)/shard_map/jvp()/while/body/eval_jaxpr/mhts,shd->mhtd/dot_general | solution.py:95
  106.2 10.2 %multiply_reduce_fusion.11 = (f32[4,128,128]{1,2,0:T(8,128)S(1)}, f32[8,4,128,128]{3,2,0,1:T(8,128)S(1)}) fusion(f32[4,128,8]{1,2,0:T(8,128)S(1)} %copy.360, f32[8,4,128]{2,0,1:T(8,128)S(1)} %get-tuple-element.2158, f32[8,4,128]{2,0,1:T(8,128)S(1)} %bitcast.427, f32[8,4,128]{2,0,1:T(8,128)S(1)} %get-tuple-element.2159, ...), kind=kOutput, calls=%fused_computation.88.clone.1 | convolution fusion | flops 811532288 | bytes 2851584 | tf_op jit(solution)/shard_map/jvp()/while/body/eval_jaxpr/mhts,shd->mhtd/dot_general | solution.py:98
  116.4 10.3 %multiply_reduce_fusion.10 = (f32[4,128,128]{1,2,0:T(8,128)S(1)}, f32[8,4,128,128]{3,2,0,1:T(8,128)S(1)}) fusion(f32[4,128,8]{1,2,0:T(8,128)S(1)} %copy.359, f32[8,4,128]{2,0,1:T(8,128)S(1)} %get-tuple-element.2159, f32[8,4,128]{2,0,1:T(8,128)S(1)} %bitcast.428, f32[8,4,128]{2,0,1:T(8,128)S(1)} %get-tuple-element.2158, ...), kind=kOutput, calls=%fused_computation.89.clone.1 | convolution fusion | flops 811532288 | bytes 2851584 | tf_op jit(solution)/shard_map/jvp()/while/body/eval_jaxpr/mhts,shd->mhtd/dot_general | solution.py:95
  130.4 10.2 %multiply_reduce_fusion.11 = (f32[4,128,128]{1,2,0:T(8,128)S(1)}, f32[8,4,128,128]{3,2,0,1:T(8,128)S(1)}) fusion(f32[4,128,8]{1,2,0:T(8,128)S(1)} %copy.360, f32[8,4,128]{2,0,1:T(8,128)S(1)} %get-tuple-element.2158, f32[8,4,128]{2,0,1:T(8,128)S(1)} %bitcast.427, f32[8,4,128]{2,0,1:T(8,128)S(1)} %get-tuple-element.2159, ...), kind=kOutput, calls=%fused_computation.88.clone.1 | convolution fusion | flops 811532288 | bytes 2851584 | tf_op jit(solution)/shard_map/jvp()/while/body/eval_jaxpr/mhts,shd->mhtd/dot_general | solution.py:98
  140.6 10.3 %multiply_reduce_fusion.10 = (f32[4,128,128]{1,2,0:T(8,128)S(1)}, f32[8,4,128,128]{3,2,0,1:T(8,128)S(1)}) fusion(f32[4,128,8]{1,2,0:T(8,128)S(1)} %copy.359, f32[8,4,128]{2,0,1:T(8,128)S(1)} %get-tuple-element.2159, f32[8,4,128]{2,0,1:T(8,128)S(1)} %bitcast.428, f32[8,4,128]{2,0,1:T(8,128)S(1)} %get-tuple-element.2158, ...), kind=kOutput, calls=%fused_computation.89.clone.1 | convolution fusion | flops 811532288 | bytes 2851584 | tf_op jit(solution)/shard_map/jvp()/while/body/eval_jaxpr/mhts,shd->mhtd/dot_general | solution.py:95
  154.5 10.2 %multiply_reduce_fusion.11 = (f32[4,128,128]{1,2,0:T(8,128)S(1)}, f32[8,4,128,128]{3,2,0,1:T(8,128)S(1)}) fusion(f32[4,128,8]{1,2,0:T(8,128)S(1)} %copy.360, f32[8,4,128]{2,0,1:T(8,128)S(1)} %get-tuple-element.2158, f32[8,4,128]{2,0,1:T(8,128)S(1)} %bitcast.427, f32[8,4,128]{2,0,1:T(8,128)S(1)} %get-tuple-element.2159, ...), kind=kOutput, calls=%fused_computation.88.clone.1 | convolution fusion | flops 811532288 | bytes 2851584 | tf_op jit(solution)/shard_map/jvp()/while/body/eval_jaxpr/mhts,shd->mhtd/dot_general | solution.py:98
  164.7 10.3 %multiply_reduce_fusion.10 = (f32[4,128,128]{1,2,0:T(8,128)S(1)}, f32[8,4,128,128]{3,2,0,1:T(8,128)S(1)}) fusion(f32[4,128,8]{1,2,0:T(8,128)S(1)} %copy.359, f32[8,4,128]{2,0,1:T(8,128)S(1)} %get-tuple-element.2159, f32[8,4,128]{2,0,1:T(8,128)S(1)} %bitcast.428, f32[8,4,128]{2,0,1:T(8,128)S(1)} %get-tuple-element.2158, ...), kind=kOutput, calls=%fused_computation.89.clone.1 | convolution fusion | flops 811532288 | bytes 2851584 | tf_op jit(solution)/shard_map/jvp()/while/body/eval_jaxpr/mhts,shd->mhtd/dot_general | solution.py:95
  178.6 10.2 %multiply_reduce_fusion.11 = (f32[4,128,128]{1,2,0:T(8,128)S(1)}, f32[8,4,128,128]{3,2,0,1:T(8,128)S(1)}) fusion(f32[4,128,8]{1,2,0:T(8,128)S(1)} %copy.360, f32[8,4,128]{2,0,1:T(8,128)S(1)} %get-tuple-element.2158, f32[8,4,128]{2,0,1:T(8,128)S(1)} %bitcast.427, f32[8,4,128]{2,0,1:T(8,128)S(1)} %get-tuple-element.2159, ...), kind=kOutput, calls=%fused_computation.88.clone.1 | convolution fusion | flops 811532288 | bytes 2851584 | tf_op jit(solution)/shard_map/jvp()/while/body/eval_jaxpr/mhts,shd->mhtd/dot_general | solution.py:98
  188.8 10.3 %multiply_reduce_fusion.10 = (f32[4,128,128]{1,2,0:T(8,128)S(1)}, f32[8,4,128,128]{3,2,0,1:T(8,128)S(1)}) fusion(f32[4,128,8]{1,2,0:T(8,128)S(1)} %copy.359, f32[8,4,128]{2,0,1:T(8,128)S(1)} %get-tuple-element.2159, f32[8,4,128]{2,0,1:T(8,128)S(1)} %bitcast.428, f32[8,4,128]{2,0,1:T(8,128)S(1)} %get-tuple-element.2158, ...), kind=kOutput, calls=%fused_computation.89.clone.1 | convolution fusion | flops 811532288 | bytes 2851584 | tf_op jit(solution)/shard_map/jvp()/while/body/eval_jaxpr/mhts,shd->mhtd/dot_general | solution.py:95
  202.7 10.2 %multiply_reduce_fusion.11 = (f32[4,128,128]{1,2,0:T(8,128)S(1)}, f32[8,4,128,128]{3,2,0,1:T(8,128)S(1)}) fusion(f32[4,128,8]{1,2,0:T(8,128)S(1)} %copy.360, f32[8,4,128]{2,0,1:T(8,128)S(1)} %get-tuple-element.2158, f32[8,4,128]{2,0,1:T(8,128)S(1)} %bitcast.427, f32[8,4,128]{2,0,1:T(8,128)S(1)} %get-tuple-element.2159, ...), kind=kOutput, calls=%fused_computation.88.clone.1 | convolution fusion | flops 811532288 | bytes 2851584 | tf_op jit(solution)/shard_map/jvp()/while/body/eval_jaxpr/mhts,shd->mhtd/dot_general | solution.py:98
  212.9 10.3 %multiply_reduce_fusion.10 = (f32[4,128,128]{1,2,0:T(8,128)S(1)}, f32[8,4,128,128]{3,2,0,1:T(8,128)S(1)}) fusion(f32[4,128,8]{1,2,0:T(8,128)S(1)} %copy.359, f32[8,4,128]{2,0,1:T(8,128)S(1)} %get-tuple-element.2159, f32[8,4,128]{2,0,1:T(8,128)S(1)} %bitcast.428, f32[8,4,128]{2,0,1:T(8,128)S(1)} %get-tuple-element.2158, ...), kind=kOutput, calls=%fused_computation.89.clone.1 | convolution fusion | flops 811532288 | bytes 2851584 | tf_op jit(solution)/shard_map/jvp()/while/body/eval_jaxpr/mhts,shd->mhtd/dot_general | solution.py:95
  227.4 13.2 %all-gather.2 = f32[32,4,128]{2,0,1:T(8,128)S(1)} all-gather(f32[8,4,128]{2,0,1:T(8,128)S(1)} %get-tuple-element.821), channel_id=4, replica_groups=mesh['group'=2,'tm'=4,'tensor'=2,'dp'=2] {'tm'}, dimensions={0}, use_global_device_ids=true | all-gather | bytes 81920 | tf_op jit(solution)/shard_map/all_gather | solution.py:13
  240.6 13.2 %all-gather.3 = f32[32,4,128]{2,0,1:T(8,128)S(1)} all-gather(f32[8,4,128]{2,0,1:T(8,128)S(1)} %get-tuple-element.822), channel_id=5, replica_groups=mesh['group'=2,'tm'=4,'tensor'=2,'dp'=2] {'tm'}, dimensions={0}, use_global_device_ids=true | all-gather | bytes 81920 | tf_op jit(solution)/shard_map/all_gather | solution.py:13
  260.5 13.2 %all-gather.4 = f32[32,4,128]{2,0,1:T(8,128)S(1)} all-gather(f32[8,4,128]{2,0,1:T(8,128)S(1)} %get-tuple-element.1700), channel_id=6, replica_groups=mesh['group'=2,'tm'=4,'tensor'=2,'dp'=2] {'tm'}, dimensions={0}, use_global_device_ids=true | all-gather | bytes 81920 | tf_op jit(solution)/shard_map/all_gather | solution.py:13
  273.7 13.2 %all-gather.5 = f32[32,4,128]{2,0,1:T(8,128)S(1)} all-gather(f32[8,4,128]{2,0,1:T(8,128)S(1)} %get-tuple-element.1664), channel_id=7, replica_groups=mesh['group'=2,'tm'=4,'tensor'=2,'dp'=2] {'tm'}, dimensions={0}, use_global_device_ids=true | all-gather | bytes 81920 | tf_op jit(solution)/shard_map/all_gather | solution.py:13
  290.1 313.4 %while.83 = (s32[]{:T(128)}, f32[4,128]{1,0:T(4,128)S(1)}, f32[8,4,128]{2,1,0:T(4,128)}, f32[8,4,128]{2,1,0:T(4,128)}, f32[8,4,128]{2,0,1:T(8,128)}, /*index=5*/...) while((s32[]{:T(128)}, f32[4,128]{1,0:T(4,128)S(1)}, ...), condition=%wide.region_15.16_spmd.clone.clone.clone, body=%wide.region_9.15_spmd.clone.clone.clone.sunk | while | flops 3254166272 | bytes 45512152 | solution.py:125
  290.3 10.1 %fusion.192 = (f32[8,4,128,128]{3,2,0,1:T(8,128)}, f32[8,4,128,128]{3,2,0,1:T(8,128)}) fusion(f32[8,4]{0,1:T(4,128)S(1)} %get-tuple-element.2326, f32[128,128]{1,0:T(8,128)} %get-tuple-element.2325, f32[8,4]{0,1:T(4,128)S(1)} %get-tuple-element.2323, pred[128,128]{1,0:T(8,128)(4,1)S(1)} %get-tuple-element.2324), kind=kLoop, calls=%fused_computation.23.clone.1 | loop fusion | flops 2621440 | bytes 4276480 | tf_op jit(solution)/shard_map/mul | solution.py:58
  307.0 4.1 bitcast_add_fusion.17
  311.1 4.5 fusion.194
  315.7 4.2 bitcast_add_fusion.18
  320.0 4.5 fusion.195
  328.7 6.1 multiply_reduce_fusion.12
  338.8 3.6 fusion.197
  342.5 10.1 %fusion.192 = (f32[8,4,128,128]{3,2,0,1:T(8,128)}, f32[8,4,128,128]{3,2,0,1:T(8,128)}) fusion(f32[8,4]{0,1:T(4,128)S(1)} %get-tuple-element.2326, f32[128,128]{1,0:T(8,128)} %get-tuple-element.2325, f32[8,4]{0,1:T(4,128)S(1)} %get-tuple-element.2323, pred[128,128]{1,0:T(8,128)(4,1)S(1)} %get-tuple-element.2324), kind=kLoop, calls=%fused_computation.23.clone.1 | loop fusion | flops 2621440 | bytes 4276480 | tf_op jit(solution)/shard_map/mul | solution.py:58
  359.2 4.1 bitcast_add_fusion.17
  363.3 4.5 fusion.194
  367.9 4.2 bitcast_add_fusion.18
  372.1 4.5 fusion.195
  380.9 6.1 multiply_reduce_fusion.12
  394.7 10.1 %fusion.192 = (f32[8,4,128,128]{3,2,0,1:T(8,128)}, f32[8,4,128,128]{3,2,0,1:T(8,128)}) fusion(f32[8,4]{0,1:T(4,128)S(1)} %get-tuple-element.2326, f32[128,128]{1,0:T(8,128)} %get-tuple-element.2325, f32[8,4]{0,1:T(4,128)S(1)} %get-tuple-element.2323, pred[128,128]{1,0:T(8,128)(4,1)S(1)} %get-tuple-element.2324), kind=kLoop, calls=%fused_computation.23.clone.1 | loop fusion | flops 2621440 | bytes 4276480 | tf_op jit(solution)/shard_map/mul | solution.py:58
  411.3 4.1 bitcast_add_fusion.17
  415.5 4.5 fusion.194
  420.1 4.2 bitcast_add_fusion.18
  424.3 4.5 fusion.195
  433.1 6.1 multiply_reduce_fusion.12
  446.9 10.1 %fusion.192 = (f32[8,4,128,128]{3,2,0,1:T(8,128)}, f32[8,4,128,128]{3,2,0,1:T(8,128)}) fusion(f32[8,4]{0,1:T(4,128)S(1)} %get-tuple-element.2326, f32[128,128]{1,0:T(8,128)} %get-tuple-element.2325, f32[8,4]{0,1:T(4,128)S(1)} %get-tuple-element.2323, pred[128,128]{1,0:T(8,128)(4,1)S(1)} %get-tuple-element.2324), kind=kLoop, calls=%fused_computation.23.clone.1 | loop fusion | flops 2621440 | bytes 4276480 | tf_op jit(solution)/shard_map/mul | solution.py:58
  463.5 4.1 bitcast_add_fusion.17
  467.6 4.5 fusion.194
  472.2 4.2 bitcast_add_fusion.18
  476.5 4.5 fusion.195
  485.3 6.1 multiply_reduce_fusion.12
  499.1 10.1 %fusion.192 = (f32[8,4,128,128]{3,2,0,1:T(8,128)}, f32[8,4,128,128]{3,2,0,1:T(8,128)}) fusion(f32[8,4]{0,1:T(4,128)S(1)} %get-tuple-element.2326, f32[128,128]{1,0:T(8,128)} %get-tuple-element.2325, f32[8,4]{0,1:T(4,128)S(1)} %get-tuple-element.2323, pred[128,128]{1,0:T(8,128)(4,1)S(1)} %get-tuple-element.2324), kind=kLoop, calls=%fused_computation.23.clone.1 | loop fusion | flops 2621440 | bytes 4276480 | tf_op jit(solution)/shard_map/mul | solution.py:58
  515.7 4.1 bitcast_add_fusion.17
  519.8 4.5 fusion.194
  524.4 4.2 bitcast_add_fusion.18
  528.7 4.5 fusion.195
  537.4 6.1 multiply_reduce_fusion.12
  551.3 10.1 %fusion.192 = (f32[8,4,128,128]{3,2,0,1:T(8,128)}, f32[8,4,128,128]{3,2,0,1:T(8,128)}) fusion(f32[8,4]{0,1:T(4,128)S(1)} %get-tuple-element.2326, f32[128,128]{1,0:T(8,128)} %get-tuple-element.2325, f32[8,4]{0,1:T(4,128)S(1)} %get-tuple-element.2323, pred[128,128]{1,0:T(8,128)(4,1)S(1)} %get-tuple-element.2324), kind=kLoop, calls=%fused_computation.23.clone.1 | loop fusion | flops 2621440 | bytes 4276480 | tf_op jit(solution)/shard_map/mul | solution.py:58
  567.9 4.1 bitcast_add_fusion.17
  572.0 4.5 fusion.194
  576.6 4.2 bitcast_add_fusion.18
  580.9 4.5 fusion.195
  589.6 6.1 multiply_reduce_fusion.12
  607.7 5.7 multiply_bitcast_fusion
  614.5 4.7 convolution_bitcast_fusion
  621.7 29.1 %all-reduce.6 = (f32[2,8,512]{2,1,0:T(8,128)}, f32[512]{0:T(512)}) all-reduce(f32[2,8,512]{2,1,0:T(8,128)S(1)} %add_multiply_fusion, f32[512]{0:T(512)S(1)} %multiply_bitcast_fusion.3), channel_id=1, replica_groups=mesh['group'=2,'tm'=4,'tensor'=2,'dp'=2] {'tm','dp'}, use_global_device_ids=true, to_apply=%region_18.19 | all-reduce | flops 8704 | bytes 69632 | tf_op jit(solution)/shard_map/psum | solution.py:184
  650.8 61.4 %all-reduce.9.cloned.1.call-done = f32[2,1024,512]{1,2,0:T(8,128)} async-done(((f32[2,1024,512]{1,2,0:T(8,128)}), f32[2,1024,512]{1,2,0:T(8,128)}) %all-reduce.9.cloned.1.call-update) | async-done | bytes 4194320 | tf_op jit(solution)/shard_map/psum | solution.py:184
  712.2 5.4 copy.231
  717.5 40.3 %reduce-scatter.2.cloned.1.call-done = f32[1,768,512]{2,1,0:T(8,128)} async-done(((f32[1,768,1024]{2,1,0:T(8,128)}), f32[1,768,512]{2,1,0:T(8,128)}) %reduce-scatter.2.cloned.1.call-update) | async-done | bytes 1572880 | tf_op jit(solution)/shard_map/reduce_scatter | solution.py:174
  (647 shorter events, 181.7 us)
Async XLA Ops:
  7.2 48.8 %copy-start = (bf16[2,1024,512]{2,1,0:T(8,128)(2,1)S(1)}, bf16[2,1024,512]{2,1,0:T(8,128)(2,1)}, u32[]{:S(2)}) copy-start(bf16[2,1024,512]{2,1,0:T(8,128)(2,1)} %param.17) | copy-start | bytes 6291460
  7.2 48.7 %all-gather.9.cloned.1.call-start = ((), (), s32[]{:S(2)}) async-start(), calls=%async_computation.1 | async-start | bytes 2359296 | tf_op jit(solution)/shard_map/all_gather | solution.py:46
  7.9 704.2 %all-reduce.9.cloned.1.call-start = ((), (), s32[]{:S(2)}) async-start(), calls=%async_computation.3 | async-start | bytes 8388608 | tf_op jit(solution)/shard_map/psum | solution.py:184
  11.7 248.1 %copy-start.38 = (f32[8,4]{0,1:T(4,128)}, f32[8,4]{0,1:T(4,128)S(1)}, u32[]{:S(2)}) copy-start(f32[8,4]{0,1:T(4,128)S(1)} %get-tuple-element.1705) | copy-start | bytes 388
  259.8 30.4 %copy-start.31 = (f32[4,128]{1,0:T(4,128)S(1)}, f32[4,128]{1,0:T(4,128)}, u32[]{:S(2)}) copy-start(f32[4,128]{1,0:T(4,128)} %custom-call.4) | copy-start | bytes 6148
  290.3 10.2 %copy-start.11 = (pred[128,128]{1,0:T(8,128)(4,1)}, pred[128,128]{1,0:T(8,128)(4,1)S(1)}, u32[]{:S(2)}) copy-start(pred[128,128]{1,0:T(8,128)(4,1)S(1)} %get-tuple-element.2324) | copy-start | bytes 49156 | tf_op jit(solution)/shard_map/transpose(jvp())/while
  290.3 10.1 %copy-start.21 = (f32[8,4]{0,1:T(4,128)}, f32[8,4]{0,1:T(4,128)S(1)}, u32[]{:S(2)}) copy-start(f32[8,4]{0,1:T(4,128)S(1)} %get-tuple-element.2323) | copy-start | bytes 388 | tf_op jit(solution)/shard_map/transpose(jvp())/while
  290.3 10.1 %copy-start.24 = (f32[8,4]{0,1:T(4,128)}, f32[8,4]{0,1:T(4,128)S(1)}, u32[]{:S(2)}) copy-start(f32[8,4]{0,1:T(4,128)S(1)} %get-tuple-element.2326) | copy-start | bytes 388 | tf_op jit(solution)/shard_map/transpose(jvp())/while
  290.3 10.1 %copy-start.27 = (f32[4,128]{1,0:T(4,128)}, f32[4,128]{1,0:T(4,128)S(1)}, u32[]{:S(2)}) copy-start(f32[4,128]{1,0:T(4,128)S(1)} %get-tuple-element.2137) | copy-start | bytes 6148 | tf_op jit(solution)/shard_map/transpose(jvp())/while
  290.3 12.7 %copy-start.40 = (s32[6,128]{1,0:T(8,128)}, s32[6,128]{1,0:T(8,128)S(1)}, u32[]{:S(2)}) copy-start(s32[6,128]{1,0:T(8,128)S(1)} %get-tuple-element.2315) | copy-start | bytes 9220 | tf_op jit(solution)/shard_map/transpose(jvp())/while
  290.3 12.7 %copy-start.45 = (s32[6]{0:T(128)}, s32[6]{0:T(128)S(1)}, u32[]{:S(2)}) copy-start(s32[6]{0:T(128)S(1)} %get-tuple-element.2316) | copy-start | bytes 76 | tf_op jit(solution)/shard_map/transpose(jvp())/while
  328.7 7.3 copy-start.1
  328.7 7.3 copy-start.2
  328.7 7.3 copy-start.28
  342.5 10.2 %copy-start.11 = (pred[128,128]{1,0:T(8,128)(4,1)}, pred[128,128]{1,0:T(8,128)(4,1)S(1)}, u32[]{:S(2)}) copy-start(pred[128,128]{1,0:T(8,128)(4,1)S(1)} %get-tuple-element.2324) | copy-start | bytes 49156 | tf_op jit(solution)/shard_map/transpose(jvp())/while
  342.5 10.1 %copy-start.21 = (f32[8,4]{0,1:T(4,128)}, f32[8,4]{0,1:T(4,128)S(1)}, u32[]{:S(2)}) copy-start(f32[8,4]{0,1:T(4,128)S(1)} %get-tuple-element.2323) | copy-start | bytes 388 | tf_op jit(solution)/shard_map/transpose(jvp())/while
  342.5 10.1 %copy-start.24 = (f32[8,4]{0,1:T(4,128)}, f32[8,4]{0,1:T(4,128)S(1)}, u32[]{:S(2)}) copy-start(f32[8,4]{0,1:T(4,128)S(1)} %get-tuple-element.2326) | copy-start | bytes 388 | tf_op jit(solution)/shard_map/transpose(jvp())/while
  342.5 10.1 %copy-start.27 = (f32[4,128]{1,0:T(4,128)}, f32[4,128]{1,0:T(4,128)S(1)}, u32[]{:S(2)}) copy-start(f32[4,128]{1,0:T(4,128)S(1)} %get-tuple-element.2137) | copy-start | bytes 6148 | tf_op jit(solution)/shard_map/transpose(jvp())/while
  342.5 12.7 %copy-start.40 = (s32[6,128]{1,0:T(8,128)}, s32[6,128]{1,0:T(8,128)S(1)}, u32[]{:S(2)}) copy-start(s32[6,128]{1,0:T(8,128)S(1)} %get-tuple-element.2315) | copy-start | bytes 9220 | tf_op jit(solution)/shard_map/transpose(jvp())/while
  342.5 12.7 %copy-start.45 = (s32[6]{0:T(128)}, s32[6]{0:T(128)S(1)}, u32[]{:S(2)}) copy-start(s32[6]{0:T(128)S(1)} %get-tuple-element.2316) | copy-start | bytes 76 | tf_op jit(solution)/shard_map/transpose(jvp())/while
  372.1 6.7 copy-start.13
  380.9 7.3 copy-start.1
  380.9 7.3 copy-start.2
  380.9 7.3 copy-start.28
  394.7 10.2 %copy-start.11 = (pred[128,128]{1,0:T(8,128)(4,1)}, pred[128,128]{1,0:T(8,128)(4,1)S(1)}, u32[]{:S(2)}) copy-start(pred[128,128]{1,0:T(8,128)(4,1)S(1)} %get-tuple-element.2324) | copy-start | bytes 49156 | tf_op jit(solution)/shard_map/transpose(jvp())/while
  394.7 10.1 %copy-start.21 = (f32[8,4]{0,1:T(4,128)}, f32[8,4]{0,1:T(4,128)S(1)}, u32[]{:S(2)}) copy-start(f32[8,4]{0,1:T(4,128)S(1)} %get-tuple-element.2323) | copy-start | bytes 388 | tf_op jit(solution)/shard_map/transpose(jvp())/while
  394.7 10.1 %copy-start.24 = (f32[8,4]{0,1:T(4,128)}, f32[8,4]{0,1:T(4,128)S(1)}, u32[]{:S(2)}) copy-start(f32[8,4]{0,1:T(4,128)S(1)} %get-tuple-element.2326) | copy-start | bytes 388 | tf_op jit(solution)/shard_map/transpose(jvp())/while
  394.7 10.1 %copy-start.27 = (f32[4,128]{1,0:T(4,128)}, f32[4,128]{1,0:T(4,128)S(1)}, u32[]{:S(2)}) copy-start(f32[4,128]{1,0:T(4,128)S(1)} %get-tuple-element.2137) | copy-start | bytes 6148 | tf_op jit(solution)/shard_map/transpose(jvp())/while
  394.7 12.7 %copy-start.40 = (s32[6,128]{1,0:T(8,128)}, s32[6,128]{1,0:T(8,128)S(1)}, u32[]{:S(2)}) copy-start(s32[6,128]{1,0:T(8,128)S(1)} %get-tuple-element.2315) | copy-start | bytes 9220 | tf_op jit(solution)/shard_map/transpose(jvp())/while
  394.7 12.7 %copy-start.45 = (s32[6]{0:T(128)}, s32[6]{0:T(128)S(1)}, u32[]{:S(2)}) copy-start(s32[6]{0:T(128)S(1)} %get-tuple-element.2316) | copy-start | bytes 76 | tf_op jit(solution)/shard_map/transpose(jvp())/while
  424.3 6.7 copy-start.13
  433.1 7.3 copy-start.1
  433.1 7.3 copy-start.2
  433.1 7.3 copy-start.28
  446.8 10.2 %copy-start.11 = (pred[128,128]{1,0:T(8,128)(4,1)}, pred[128,128]{1,0:T(8,128)(4,1)S(1)}, u32[]{:S(2)}) copy-start(pred[128,128]{1,0:T(8,128)(4,1)S(1)} %get-tuple-element.2324) | copy-start | bytes 49156 | tf_op jit(solution)/shard_map/transpose(jvp())/while
  446.8 10.1 %copy-start.21 = (f32[8,4]{0,1:T(4,128)}, f32[8,4]{0,1:T(4,128)S(1)}, u32[]{:S(2)}) copy-start(f32[8,4]{0,1:T(4,128)S(1)} %get-tuple-element.2323) | copy-start | bytes 388 | tf_op jit(solution)/shard_map/transpose(jvp())/while
  446.9 10.1 %copy-start.24 = (f32[8,4]{0,1:T(4,128)}, f32[8,4]{0,1:T(4,128)S(1)}, u32[]{:S(2)}) copy-start(f32[8,4]{0,1:T(4,128)S(1)} %get-tuple-element.2326) | copy-start | bytes 388 | tf_op jit(solution)/shard_map/transpose(jvp())/while
  446.9 10.1 %copy-start.27 = (f32[4,128]{1,0:T(4,128)}, f32[4,128]{1,0:T(4,128)S(1)}, u32[]{:S(2)}) copy-start(f32[4,128]{1,0:T(4,128)S(1)} %get-tuple-element.2137) | copy-start | bytes 6148 | tf_op jit(solution)/shard_map/transpose(jvp())/while
  446.9 12.7 %copy-start.40 = (s32[6,128]{1,0:T(8,128)}, s32[6,128]{1,0:T(8,128)S(1)}, u32[]{:S(2)}) copy-start(s32[6,128]{1,0:T(8,128)S(1)} %get-tuple-element.2315) | copy-start | bytes 9220 | tf_op jit(solution)/shard_map/transpose(jvp())/while
  446.9 12.7 %copy-start.45 = (s32[6]{0:T(128)}, s32[6]{0:T(128)S(1)}, u32[]{:S(2)}) copy-start(s32[6]{0:T(128)S(1)} %get-tuple-element.2316) | copy-start | bytes 76 | tf_op jit(solution)/shard_map/transpose(jvp())/while
  476.5 6.7 copy-start.13
  485.2 7.3 copy-start.1
  485.2 7.3 copy-start.2
  485.3 7.3 copy-start.28
  499.0 10.2 %copy-start.11 = (pred[128,128]{1,0:T(8,128)(4,1)}, pred[128,128]{1,0:T(8,128)(4,1)S(1)}, u32[]{:S(2)}) copy-start(pred[128,128]{1,0:T(8,128)(4,1)S(1)} %get-tuple-element.2324) | copy-start | bytes 49156 | tf_op jit(solution)/shard_map/transpose(jvp())/while
  499.0 10.1 %copy-start.21 = (f32[8,4]{0,1:T(4,128)}, f32[8,4]{0,1:T(4,128)S(1)}, u32[]{:S(2)}) copy-start(f32[8,4]{0,1:T(4,128)S(1)} %get-tuple-element.2323) | copy-start | bytes 388 | tf_op jit(solution)/shard_map/transpose(jvp())/while
  499.0 10.1 %copy-start.24 = (f32[8,4]{0,1:T(4,128)}, f32[8,4]{0,1:T(4,128)S(1)}, u32[]{:S(2)}) copy-start(f32[8,4]{0,1:T(4,128)S(1)} %get-tuple-element.2326) | copy-start | bytes 388 | tf_op jit(solution)/shard_map/transpose(jvp())/while
  499.0 10.1 %copy-start.27 = (f32[4,128]{1,0:T(4,128)}, f32[4,128]{1,0:T(4,128)S(1)}, u32[]{:S(2)}) copy-start(f32[4,128]{1,0:T(4,128)S(1)} %get-tuple-element.2137) | copy-start | bytes 6148 | tf_op jit(solution)/shard_map/transpose(jvp())/while
  499.1 12.7 %copy-start.40 = (s32[6,128]{1,0:T(8,128)}, s32[6,128]{1,0:T(8,128)S(1)}, u32[]{:S(2)}) copy-start(s32[6,128]{1,0:T(8,128)S(1)} %get-tuple-element.2315) | copy-start | bytes 9220 | tf_op jit(solution)/shard_map/transpose(jvp())/while
  499.1 12.7 %copy-start.45 = (s32[6]{0:T(128)}, s32[6]{0:T(128)S(1)}, u32[]{:S(2)}) copy-start(s32[6]{0:T(128)S(1)} %get-tuple-element.2316) | copy-start | bytes 76 | tf_op jit(solution)/shard_map/transpose(jvp())/while
  528.7 6.7 copy-start.13
  537.4 7.3 copy-start.1
  537.4 7.3 copy-start.2
  537.4 7.3 copy-start.28
  551.2 10.2 %copy-start.11 = (pred[128,128]{1,0:T(8,128)(4,1)}, pred[128,128]{1,0:T(8,128)(4,1)S(1)}, u32[]{:S(2)}) copy-start(pred[128,128]{1,0:T(8,128)(4,1)S(1)} %get-tuple-element.2324) | copy-start | bytes 49156 | tf_op jit(solution)/shard_map/transpose(jvp())/while
  551.2 10.1 %copy-start.21 = (f32[8,4]{0,1:T(4,128)}, f32[8,4]{0,1:T(4,128)S(1)}, u32[]{:S(2)}) copy-start(f32[8,4]{0,1:T(4,128)S(1)} %get-tuple-element.2323) | copy-start | bytes 388 | tf_op jit(solution)/shard_map/transpose(jvp())/while
  551.2 10.1 %copy-start.24 = (f32[8,4]{0,1:T(4,128)}, f32[8,4]{0,1:T(4,128)S(1)}, u32[]{:S(2)}) copy-start(f32[8,4]{0,1:T(4,128)S(1)} %get-tuple-element.2326) | copy-start | bytes 388 | tf_op jit(solution)/shard_map/transpose(jvp())/while
  551.2 10.1 %copy-start.27 = (f32[4,128]{1,0:T(4,128)}, f32[4,128]{1,0:T(4,128)S(1)}, u32[]{:S(2)}) copy-start(f32[4,128]{1,0:T(4,128)S(1)} %get-tuple-element.2137) | copy-start | bytes 6148 | tf_op jit(solution)/shard_map/transpose(jvp())/while
  551.2 12.7 %copy-start.40 = (s32[6,128]{1,0:T(8,128)}, s32[6,128]{1,0:T(8,128)S(1)}, u32[]{:S(2)}) copy-start(s32[6,128]{1,0:T(8,128)S(1)} %get-tuple-element.2315) | copy-start | bytes 9220 | tf_op jit(solution)/shard_map/transpose(jvp())/while
  551.2 12.7 %copy-start.45 = (s32[6]{0:T(128)}, s32[6]{0:T(128)S(1)}, u32[]{:S(2)}) copy-start(s32[6]{0:T(128)S(1)} %get-tuple-element.2316) | copy-start | bytes 76 | tf_op jit(solution)/shard_map/transpose(jvp())/while
  589.6 7.3 copy-start.1
  589.6 7.3 copy-start.2
  589.6 7.3 copy-start.28
  613.4 144.4 %reduce-scatter.2.cloned.1.call-start = ((), (), s32[]{:S(2)}) async-start(), calls=%async_computation.2 | async-start | bytes 4718592 | tf_op jit(solution)/shard_map/reduce_scatter | solution.py:174
  (121 other events, 415.1 us)
Sparse Core Ops, SparseCore 0:
  9.6 29.8 all-gather.8
  613.5 98.6 all-reduce.8
  714.4 43.3 reduce-scatter.1
where the time goes:
time: 777 us; the launch traced here: 767 us
  matrix products  288 us (37%)
  other arithmetic  130 us (17%)
  blocking collectives  123 us (16%)
  local copies, waits for them, and re-layouts  104 us (13%)
  waiting for transfers between devices  102 us (13%)
  between operations  15.1 us (2%)
    dot_general x18, matrix products, block_step(): jnp.einsum('mhts,shd->mhtd', kern_re * same_clip, block_in, precision=lar...  108 us
    dot_general x18, matrix products, block_step(): jnp.einsum('mhts,shd->mhtd', kern_im * same_clip, block_in, precision=lar...  102 us
    all_gather x7, blocking collectives, carried_in(): pieces = jax.tree.map(lambda part: lax.all_gather(part, axis), value)  94.2 us
    psum x1, waiting for transfers between devices, shards(): lax.psum((proj_term, coeff_term, skip_term), ('tm', 'dp'))  61.4 us
    mul x6, other arithmetic, shards(): kern_im = damping * jnp.sin(angles[:, :, None, None] * lag_steps)  60.6 us
    reduce_scatter x1, waiting for transfers between devices, shards(): lax.psum_scatter(partial_in[None], 'tensor', scatter_dimension=2, tiled=T...  40.3 us
    reduce_sum x6, other arithmetic, block_step(): block_re[..., None] * state_im[:, :, None, :]  36.6 us
    dynamic_slice x36, local copies, waits for them, and re-layouts, intra(): lax.scan(jax.checkpoint(block_step), (initial, initial), (blocks_in, seg_...  30.9 us
  transfers between devices with their start and end apart: 3, of which 2 were waited for; matrix products, arithmetic and copies ran while one was open for 2% of the time, Pallas kernels for 0%

commit v1 on v0

v1 whole, which is shorter than its diff:
```python
import functools
import math

import jax
import jax.numpy as jnp
from jax import lax
from jax.experimental import pallas as pl
from jax.experimental.pallas import tpu as pltpu
from jax.sharding import PartitionSpec as P

BLOCK_LEN = 128
F32 = jnp.float32
BF16 = jnp.bfloat16


def dot(a, b):
    return jnp.dot(a, b, preferred_element_type=F32)


def segment_of(starts_ref, clips, frame):
    total = jnp.where(frame >= starts_ref[1], 1, 0)
    for k in range(1, clips):
        total = total + jnp.where(frame >= starts_ref[1 + k], 1, 0)
    return total


def project_kernel(clips, modes, starts_ref, feat_ref, proj_ref, up_ref, table_ref, q_ref, x_ref, ends_ref):
    rows, width = q_ref.shape
    first = starts_ref[0]
    lane = lax.broadcasted_iota(jnp.int32, (1, rows), 1) + first
    seg = segment_of(starts_ref, clips, lane)
    at_end = jnp.where(seg == segment_of(starts_ref, clips, first + rows - 1), 1.0, 0.0)
    at_start = jnp.where(seg == segment_of(starts_ref, clips, first), 1.0, 0.0)
    query = dot(feat_ref[...], proj_ref[0]).astype(BF16)
    q_ref[...] = query
    signal = dot(feat_ref[...], proj_ref[1]).astype(BF16)
    x_ref[...] = signal
    grad = (query.astype(F32) * up_ref[...].astype(F32)).astype(BF16)
    for h in range(width // 128):
        cols = slice(h * 128, h * 128 + 128)
        fwd = (table_ref[h, : 2 * modes, :] * at_end).astype(BF16)
        bwd = (table_ref[h, 2 * modes :, :] * at_start).astype(BF16)
        ends_ref[h, : 2 * modes, :] = dot(fwd, signal[:, cols])
        ends_ref[h, 2 * modes :, :] = dot(bwd, grad[:, cols])


def conv_kernel(
    clips, modes, starts_ref, cols_ref, rows_ref, w_ref, carry_ref, q_ref, x_ref, up_ref,
    mixed_ref, stack_ref, sums_ref, kf, kb, tx,
):
    rows = q_ref.shape[0]
    blocks = rows // BLOCK_LEN
    M = modes
    first = starts_ref[0]
    i0 = lax.broadcasted_iota(jnp.int32, (BLOCK_LEN, BLOCK_LEN), 0)
    i1 = lax.broadcasted_iota(jnp.int32, (BLOCK_LEN, BLOCK_LEN), 1)
    for m in range(M):
        re, im = m, M + m
        er, ei = cols_ref[0, :, re : re + 1], cols_ref[0, :, im : im + 1]
        fr = rows_ref[0, 2 * M + re : 2 * M + re + 1, :]
        fi = rows_ref[0, 2 * M + im : 2 * M + im + 1, :]
        kf[:, re * 128 : re * 128 + 128] = jnp.where(i0 >= i1, er * fr - ei * fi, 0.0).astype(BF16)
        kf[:, im * 128 : im * 128 + 128] = jnp.where(i0 >= i1, -(er * fi + ei * fr), 0.0).astype(BF16)
        fr, fi = cols_ref[0, :, 2 * M + re : 2 * M + re + 1], cols_ref[0, :, 2 * M + im : 2 * M + im + 1]
        er, ei = rows_ref[0, re : re + 1, :], rows_ref[0, im : im + 1, :]
        kb[re * 128 : re * 128 + 128, :] = jnp.where(i1 >= i0, er * fr - ei * fi, 0.0).astype(BF16)
        kb[im * 128 : im * 128 + 128, :] = jnp.where(i1 >= i0, -(er * fi + ei * fr), 0.0).astype(BF16)

    w = w_ref[0, : 2 * M, :]
    wr, wi = w[:M], w[M:]
    skip = w_ref[0, 2 * M : 2 * M + 1, :]
    pr = rows_ref[0, 6 * M : 7 * M, :]
    pi = rows_ref[0, 7 * M : 8 * M, :]
    col_p = cols_ref[0, :, : 2 * M].astype(BF16)
    col_h = cols_ref[0, :, 4 * M : 6 * M].astype(BF16)

    def flag(cond):
        return jnp.where(cond, 1.0, 0.0).astype(F32)

    def weigh(sr, si):
        return jnp.concatenate([wr * sr - wi * si, -(wr * si + wi * sr)], axis=0).astype(BF16)

    def masks(b):
        begin = first + b * BLOCK_LEN
        seg0 = segment_of(starts_ref, clips, i0 + begin)
        seg1 = segment_of(starts_ref, clips, i1 + begin)
        prior = segment_of(starts_ref, clips, begin - 1)
        head = segment_of(starts_ref, clips, begin)
        last = segment_of(starts_ref, clips, begin + BLOCK_LEN - 1)
        after = segment_of(starts_ref, clips, begin + BLOCK_LEN)
        return seg0, seg1, flag(seg0 == seg1).astype(BF16), prior, head, last, after

    def forward(b, carried):
        ur, ui = carried
        seg0, seg1, same, prior, head, last, after = masks(b)
        at = pl.ds(pl.multiple_of(b * BLOCK_LEN, BLOCK_LEN), BLOCK_LEN)
        x = x_ref[at, :]
        xf = x.astype(F32)
        same2 = jnp.concatenate([same, same], axis=1)
        acc = flag(seg0 == prior) * dot(col_p, weigh(ur, ui))
        for j in range(M):
            scaled = jnp.concatenate(
                [(w[2 * j : 2 * j + 1] * xf).astype(BF16), (w[2 * j + 1 : 2 * j + 2] * xf).astype(BF16)], axis=0
            )
            acc = acc + dot(kf[:, j * 256 : j * 256 + 256] * same2, scaled)
        out = skip * xf + acc
        mixed_ref[at, :] = (q_ref[at, :].astype(F32) * out).astype(BF16)
        stack_ref[0, at, :] = (up_ref[at, :].astype(F32) * out).astype(BF16)
        reach = (rows_ref[0, 4 * M : 6 * M, :] * flag(seg1[: 2 * M] == last)).astype(BF16)
        total = dot(reach, x)
        tx[b] = total
        keep = flag(last == prior)
        return (
            total[:M] + keep * (pr * ur - pi * ui),
            total[M:] + keep * (pr * ui + pi * ur),
        )

    lax.fori_loop(0, blocks, forward, (carry_ref[0, :M, :], carry_ref[0, M : 2 * M, :]))
    sums_ref[...] = jnp.zeros_like(sums_ref)

    def backward(step, carried):
        gr, gi = carried
        b = blocks - 1 - step
        seg0, seg1, same, prior, head, last, after = masks(b)
        at = pl.ds(pl.multiple_of(b * BLOCK_LEN, BLOCK_LEN), BLOCK_LEN)
        xf = x_ref[at, :].astype(F32)
        g = up_ref[at, :].astype(F32) * q_ref[at, :].astype(F32)
        gb = g.astype(BF16)
        gx = skip * g + flag(seg0 == after) * dot(col_h, weigh(gr, gi))
        for m in range(2 * M):
            part = dot(kb[m * 128 : m * 128 + 128, :] * same, gb)
            gx = gx + w[m : m + 1] * part
            sums_ref[0, m : m + 1, :] += jnp.sum(xf * part, axis=0, keepdims=True)
        stack_ref[1, at, :] = gx.astype(BF16)
        sums_ref[0, 2 * M : 2 * M + 1, :] += jnp.sum(xf * g, axis=0, keepdims=True)
        total = tx[b]
        join = flag(last == after)
        sums_ref[0, :M, :] += join * (total[:M] * gr - total[M:] * gi)
        sums_ref[0, M : 2 * M, :] -= join * (total[:M] * gi + total[M:] * gr)
        reach = (rows_ref[0, : 2 * M, :] * flag(seg1[: 2 * M] == head)).astype(BF16)
        lead = dot(reach, gb)
        keep = flag(head == after)
        return (
            lead[:M] + keep * (pr * gr - pi * gi),
            lead[M:] + keep * (pr * gi + pi * gr),
        )

    lax.fori_loop(0, blocks, backward, (carry_ref[0, 2 * M : 3 * M, :], carry_ref[0, 3 * M :, :]))


def shards(frames_in, in_proj, log_rates, angles, residues, skip_gain, lengths, grad_out):
    rows = frames_in.shape[1]
    channels = frames_in.shape[2]
    width = in_proj.shape[1]
    M, heads = log_rates.shape
    clips = lengths.shape[1]
    count, mine = lax.axis_size("tm"), lax.axis_index("tm")
    features = lax.all_gather(frames_in, "tensor", axis=2, tiled=True)[0]
    upstream = grad_out[0]
    decay = jnp.exp(log_rates).T
    turn = angles.T
    weight = jnp.sqrt(-jnp.expm1(-2.0 * decay))

    def powers(exponents):
        exponents = jnp.asarray(exponents, F32)
        size = jnp.exp(-decay[:, :, None] * exponents)
        arg = turn[:, :, None] * exponents
        return jnp.concatenate([size * jnp.cos(arg), size * jnp.sin(arg)], axis=1)

    lags = jnp.arange(BLOCK_LEN, dtype=jnp.int32)
    ahead, back, rest = powers(lags), powers(-lags), powers(BLOCK_LEN - lags)
    full = jnp.broadcast_to(powers(jnp.full((1,), BLOCK_LEN)), (heads, 2 * M, BLOCK_LEN))
    row_table = jnp.concatenate([ahead, back, rest, full], axis=1)
    col_table = jnp.concatenate([ahead, back, rest], axis=1).transpose(0, 2, 1)
    span = jnp.arange(rows, dtype=jnp.int32)
    long_table = jnp.concatenate([powers(rows - span), powers(span)], axis=1)
    coeffs = residues.reshape(2, M, heads, 128).transpose(2, 0, 1, 3) * weight[:, None, :, None]
    pad = jnp.zeros((heads, 7, 128), F32)
    w_table = jnp.concatenate(
        [coeffs.reshape(heads, 2 * M, 128), skip_gain.reshape(heads, 1, 128), pad], axis=1
    )
    clip_start = jnp.cumsum(lengths[0]) - lengths[0]
    starts = jnp.concatenate([(mine * rows)[None], clip_start]).astype(jnp.int32)

    pair = 2 if heads % 2 == 0 else 1
    wide = pair * 128
    query_rows, signal, ends = pl.pallas_call(
        functools.partial(project_kernel, clips, M),
        grid_spec=pltpu.PrefetchScalarGridSpec(
            num_scalar_prefetch=1,
            grid=(heads // pair,),
            in_specs=[
                pl.BlockSpec((rows, width), lambda i, s: (0, 0)),
                pl.BlockSpec((2, width, wide), lambda i, s: (0, 0, i)),
                pl.BlockSpec((rows, wide), lambda i, s: (0, i)),
                pl.BlockSpec((pair, 4 * M, rows), lambda i, s: (i, 0, 0)),
            ],
            out_specs=[
                pl.BlockSpec((rows, wide), lambda i, s: (0, i)),
                pl.BlockSpec((rows, wide), lambda i, s: (0, i)),
                pl.BlockSpec((pair, 4 * M, 128), lambda i, s: (i, 0, 0)),
            ],
        ),
        out_shape=[
            jax.ShapeDtypeStruct((rows, channels), BF16),
            jax.ShapeDtypeStruct((rows, channels), BF16),
            jax.ShapeDtypeStruct((heads, 4 * M, 128), F32),
        ],
        compiler_params=pltpu.CompilerParams(vmem_limit_bytes=40 << 20),
        name="project",
    )(starts, features, in_proj, upstream, long_table)

    gathered = lax.all_gather(ends, "tm")
    step = powers(jnp.full((1,), rows))
    step_re, step_im = step[:, :M], step[:, M:]

    def segment_at(frame):
        return jnp.sum((frame >= clip_start).astype(jnp.int32))

    ur = ui = gr = gi = jnp.zeros((heads, M, 128), F32)
    for d in range(count - 1):
        keep = (segment_at(d * rows - 1) == segment_at(d * rows + rows - 1)).astype(F32)
        nr = gathered[d, :, :M] + keep * (step_re * ur - step_im * ui)
        ni = gathered[d, :, M : 2 * M] + keep * (step_re * ui + step_im * ur)
        ur, ui = jnp.where(d < mine, nr, ur), jnp.where(d < mine, ni, ui)
    for d in range(count - 1, 0, -1):
        keep = (segment_at(d * rows) == segment_at(d * rows + rows)).astype(F32)
        nr = gathered[d, :, 2 * M : 3 * M] + keep * (step_re * gr - step_im * gi)
        ni = gathered[d, :, 3 * M :] + keep * (step_re * gi + step_im * gr)
        gr, gi = jnp.where(d > mine, nr, gr), jnp.where(d > mine, ni, gi)
    carries = jnp.concatenate([ur, ui, gr, gi], axis=1)

    per_head = lambda i, s: (i, 0, 0)
    column = lambda i, s: (0, i)
    mixed, stacked, sums = pl.pallas_call(
        functools.partial(conv_kernel, clips, M),
        grid_spec=pltpu.PrefetchScalarGridSpec(
            num_scalar_prefetch=1,
            grid=(heads,),
            in_specs=[
                pl.BlockSpec((1, BLOCK_LEN, 6 * M), per_head),
                pl.BlockSpec((1, 8 * M, BLOCK_LEN), per_head),
                pl.BlockSpec((1, 2 * M + 8, 128), per_head),
                pl.BlockSpec((1, 4 * M, 128), per_head),
                pl.BlockSpec((rows, 128), column),
                pl.BlockSpec((rows, 128), column),
                pl.BlockSpec((rows, 128), column),
            ],
            out_specs=[
                pl.BlockSpec((rows, 128), column),
                pl.BlockSpec((2, rows, 128), lambda i, s: (0, 0, i)),
                pl.BlockSpec((1, 2 * M + 8, 128), per_head),
            ],
            scratch_shapes=[
                pltpu.VMEM((BLOCK_LEN, 2 * M * BLOCK_LEN), BF16),
                pltpu.VMEM((2 * M * BLOCK_LEN, BLOCK_LEN), BF16),
                pltpu.VMEM((rows // BLOCK_LEN, 2 * M, 128), F32),
            ],
        ),
        out_shape=[
            jax.ShapeDtypeStruct((rows, channels), BF16),
            jax.ShapeDtypeStruct((2, rows, channels), BF16),
            jax.ShapeDtypeStruct((heads, 2 * M + 8, 128), F32),
        ],
        compiler_params=pltpu.CompilerParams(vmem_limit_bytes=40 << 20),
        name="conv",
    )(starts, col_table, row_table, w_table, carries, query_rows, signal, upstream)

    norm_scale = 1.0 / math.sqrt(rows * count * lax.axis_size("dp"))
    coeff_term = sums[:, : 2 * M].reshape(heads, 2, M, 128) * (weight[:, None, :, None] * norm_scale)
    coeff_term = coeff_term.transpose(1, 2, 0, 3).reshape(2, M, channels)
    skip_term = sums[:, 2 * M].reshape(channels) * norm_scale
    proj_term = jnp.einsum("ld,klc->kdc", features, stacked, preferred_element_type=F32) * norm_scale
    partial_in = jnp.einsum("klc,kdc->ld", stacked, in_proj, preferred_element_type=F32)
    proj_sum, coeff_sum, skip_sum = lax.psum((proj_term, coeff_term, skip_term), ("tm", "dp"))
    input_grad = lax.psum_scatter(
        partial_in.astype(BF16)[None], "tensor", scatter_dimension=2, tiled=True
    )
    return (mixed[None], input_grad, proj_sum, coeff_sum, skip_sum)


def solution(mesh):
    in_specs = (
        P(("group", "dp"), "tm", "tensor"),
        P(None, None, "tensor"),
        P(None, "tensor"),
        P(None, "tensor"),
        P(None, None, "tensor"),
        P("tensor"),
        P(("group", "dp"), None),
        P(("group", "dp"), "tm", "tensor"),
    )
    out_specs = (
        P(("group", "dp"), "tm", "tensor"),
        P(("group", "dp"), "tm", "tensor"),
        P("group", None, "tensor"),
        P("group", None, "tensor"),
        P(("group", "tensor")),
    )
    return jax.shard_map(shards, mesh=mesh, in_specs=in_specs, out_specs=out_specs, check_vma=False)
```

time: 777 us -> 219 us (0.28); the launches traced: 767 us -> 219 us
  matrix products: 288 us -> 8.26 us
  other arithmetic: 130 us -> 14.9 us
  local copies, waits for them, and re-layouts: 104 us -> 9.61 us
  blocking collectives: 123 us -> 43.4 us
  Pallas kernels: 0 us -> 24.5 us
    dot_general x55 -> x2, matrix products: 288 us -> 8.26 us  [the longest x1 4.42 us: shards(): jnp.einsum('klc,kdc->ld', stacked, in_proj, preferred_element_type=F32)]
    all_gather x7 -> x1, blocking collectives: 94.2 us -> 13.9 us  [shards(): gathered = lax.all_gather(ends, 'tm')]
    mul x10 -> x4, other arithmetic: 63.5 us -> 3.39 us  [the longest x1 1.47 us: powers(): return jnp.concatenate([size * jnp.cos(arg), size * jnp.sin(arg)], axis=1)]
    reduce_sum x8 -> x1, other arithmetic: 37.3 us -> 1.49 us  [segment_at(): return jnp.sum((frame >= clip_start).astype(jnp.int32))]
    dynamic_slice x45 -> x0, local copies, waits for them, and re-layouts: 31 us -> none  [the longest x36 30.9 us: intra(): lax.scan(jax.checkpoint(block_step), (initial, initial), (blocks_in, seg_...]
    pallas_call x0 -> x2, Pallas kernels: none -> 24.5 us  [the longest x1 21.3 us: shards(): pl.pallas_call(functools.partial(conv_kernel, clips, M), grid_spec=pltpu....]
    broadcast_in_dim x12 -> x1, local copies, waits for them, and re-layouts: 24.2 us -> 0.01 us  [shards(): pad = jnp.zeros((heads, 7, 128), F32)]
    reduce_scatter x1, waiting for transfers between devices: 40.3 us -> 23.6 us  [shards(): lax.psum_scatter(partial_in.astype(BF16)[None], 'tensor', scatter_dimensi...]
  transfers between devices with their start and end apart: 3 -> 3, of which waited for: 2 -> 3; matrix products, arithmetic and copies ran while one was open for 2% -> 12% of each run, Pallas kernels for 0% -> 0%
where the time goes in v1:
time: 219 us
  waiting for transfers between devices  96.4 us (44%)
  blocking collectives  43.4 us (20%)
  Pallas kernels  24.5 us (11%)
  between operations  21.6 us (10%)
  other arithmetic  14.9 us (7%)
  local copies, waits for them, and re-layouts  9.61 us (4%)
  matrix products  8.26 us (4%)
    psum x1, waiting for transfers between devices, shards(): lax.psum((proj_term, coeff_term, skip_term), ('tm', 'dp'))  63.8 us
    psum x1, blocking collectives, shards(): lax.psum((proj_term, coeff_term, skip_term), ('tm', 'dp'))  29.5 us
    reduce_scatter x1, waiting for transfers between devices, shards(): lax.psum_scatter(partial_in.astype(BF16)[None], 'tensor', scatter_dimensi...  23.6 us
    pallas_call x1, Pallas kernels, shards(): pl.pallas_call(functools.partial(conv_kernel, clips, M), grid_spec=pltpu....  21.3 us
    all_gather x1, blocking collectives, shards(): gathered = lax.all_gather(ends, 'tm')  13.9 us
    unnamed x21, local copies, waits for them, and re-layouts  8.62 us
    all_gather x1, waiting for transfers between devices, shards(): features = lax.all_gather(frames_in, 'tensor', axis=2, tiled=True)[0]  8.31 us
    unnamed x6, other arithmetic  4.96 us
  transfers between devices with their start and end apart: 3, of which 3 were waited for; matrix products, arithmetic and copies ran while one was open for 12% of the time, Pallas kernels for 0%

profile of v1, /device:TPU:0, one launch (start us, length us, event | category | flops | bytes accessed | tf_op | source)
XLA Modules:
  0.0 218.7 jit_solution(5149918859317335498)
XLA Ops:
  7.2 0.0 copy-start
  7.2 0.0 copy-start.2
  7.2 0.0 copy-start.1
  7.2 0.0 all-gather.3.cloned.1.call-start
  7.2 0.7 all-gather.3.cloned.1.call-update
  7.9 0.0 all-reduce.3.cloned.1.call-start
  8.0 0.9 reduce-window.9
  8.9 1.3 sqrt_bitcast_fusion
  10.2 1.5 fusion.39
  19.3 1.3 broadcast_multiply_fusion.4
  20.6 0.8 constant_dynamic-update-slice_fusion.12
  21.5 0.8 constant_dynamic-update-slice_fusion.11
  22.3 0.8 constant_dynamic-update-slice_fusion.10
  23.1 0.8 constant_dynamic-update-slice_fusion.9
  23.9 0.9 constant_dynamic-update-slice_fusion.8
  24.8 0.8 constant_dynamic-update-slice_fusion.7
  25.6 0.8 constant_dynamic-update-slice_fusion
  26.4 0.8 copy.19.cols_ref
  27.3 0.1 pad.10.clone
  27.4 0.1 pad_add_fusion.starts_ref
  27.4 0.1 maximum_bitcast_fusion
  27.5 1.5 fusion.2
  29.0 0.6 broadcast_multiply_fusion.3
  29.6 0.1 constant_dynamic-update-slice_fusion.6.rows_ref
  29.7 0.0 copy-done
  29.7 0.8 fusion.7
  30.5 0.8 maximum_maximum_fusion.w_ref
  31.2 8.3 %all-gather.3.cloned.1.call-done = bf16[1,768,1024]{2,1,0:T(8,128)(2,1)} async-done(((bf16[1,768,512]{2,1,0:T(8,128)(2,1)}), bf16[1,768,1024]{2,1,0:T(8,128)(2,1)}) %all-gather.3.cloned.1.call-update) | async-done | bytes 1572880 | tf_op jit(solution)/shard_map/all_gather | solution.py:158
  39.5 0.0 copy-done.2
  39.5 0.0 copy-done.1
  39.5 0.0 copy-start.3
  39.5 1.4 copy-done.3
  40.9 0.0 copy-start.7
  40.9 0.0 copy-start.8
  40.9 0.0 copy-start.5
  40.9 3.2 %project.1 = (bf16[768,512]{1,0:T(8,128)(2,1)S(1)}, bf16[768,512]{1,0:T(8,128)(2,1)S(1)}, f32[4,32,128]{2,1,0:T(8,128)S(1)}) custom-call(s32[5]{0:T(128)S(1)} %pad_add_fusion.starts_ref, bf16[768,1024]{1,0:T(8,128)(2,1)S(1)} %bitcast.179, bf16[2,1024,512]{2,1,0:T(8,128)(2,1)S(1)} %copy-done.2, bf16[768,512]{1,0:T(8,128)(2,1)S(1)} %bitcast.177, ...), custom_call_target="tpu_custom_call" | custom-call | tf_op jit(solution)/shard_map/project/pallas_call | solution.py:187
  44.1 13.9 %all-gather = f32[16,32,128]{2,1,0:T(8,128)S(1)} all-gather(f32[4,32,128]{2,1,0:T(8,128)S(1)} %get-tuple-element.11), channel_id=2, replica_groups=mesh['group'=2,'tm'=4,'tensor'=2,'dp'=2] {'tm'}, dimensions={0}, use_global_device_ids=true | all-gather | bytes 327680 | tf_op jit(solution)/shard_map/all_gather | solution.py:213
  58.1 0.1 fusion.37
  58.2 0.0 copy-done.7
  58.2 0.0 copy-done.8
  58.2 0.1 fusion.25
  58.3 0.0 copy-start.4
  58.3 0.1 fusion.15
  58.4 0.0 copy-done.5
  58.4 21.3 %conv.1 = (bf16[768,512]{1,0:T(8,128)(2,1)}, bf16[2,768,512]{2,1,0:T(8,128)(2,1)S(1)}, f32[4,24,128]{2,1,0:T(8,128)S(1)}) custom-call(s32[5]{0:T(128)S(1)} %pad_add_fusion.starts_ref, f32[4,128,48]{2,1,0:T(8,128)S(1)} %copy-done.5, f32[4,64,128]{2,1,0:T(8,128)S(1)} %constant_dynamic-update-slice_fusion.6.rows_ref, ...), custom_call_target="tpu_custom_call" | custom-call | tf_op jit(solution)/shard_map/conv/pallas_call | solution.py:235
  79.7 0.0 copy-start.6
  79.7 1.2 copy-done.6
  80.8 0.0 copy-done.4
  80.8 3.8 %multiply_bitcast_fusion = f32[2,1024,512]{1,2,0:T(8,128)} fusion(bf16[2,768,512]{2,1,0:T(8,128)(2,1)S(1)} %get-tuple-element.15, bf16[1,768,1024]{2,1,0:T(8,128)(2,1)S(1)} %copy-done.4), kind=kOutput, calls=%fused_computation | convolution fusion | flops 1611661312 | bytes 7340032 | tf_op jit(solution)/shard_map/ld,klc->kdc/dot_general | solution.py:273
  84.7 0.0 all-reduce.3.cloned.1.call-update
  84.7 0.0 reduce-scatter.2.cloned.1.call-start
  84.8 4.4 %fusion.1 = bf16[1,768,1024]{2,1,0:T(8,128)(2,1)} fusion(bf16[2,768,512]{2,1,0:T(8,128)(2,1)} %copy-done.6, bf16[2,1024,512]{2,1,0:T(8,128)(2,1)S(1)} %copy-done.2), kind=kOutput, calls=%fused_computation.3 | convolution fusion | flops 1611399168 | bytes 5242880 | tf_op jit(solution)/shard_map/klc,kdc->ld/dot_general | solution.py:274
  89.2 0.0 copy-start.9
  89.2 0.0 reduce-scatter.2.cloned.1.call-update
  89.2 0.6 copy-done.9
  89.9 0.1 copy_bitcast_fusion
  89.9 29.5 %all-reduce = (f32[2,8,512]{2,1,0:T(8,128)}, f32[512]{0:T(512)}) all-reduce(f32[2,8,512]{2,1,0:T(8,128)S(1)} %copy_bitcast_fusion, f32[512]{0:T(512)S(1)} %bitcast.192), channel_id=1, replica_groups=mesh['group'=2,'tm'=4,'tensor'=2,'dp'=2] {'tm','dp'}, use_global_device_ids=true, to_apply=%region_11.12 | all-reduce | flops 8704 | bytes 69632 | tf_op jit(solution)/shard_map/psum | solution.py:275
  119.4 63.8 %all-reduce.3.cloned.1.call-done = f32[2,1024,512]{1,2,0:T(8,128)} async-done(((f32[2,1024,512]{1,2,0:T(8,128)}), f32[2,1024,512]{1,2,0:T(8,128)}) %all-reduce.3.cloned.1.call-update) | async-done | bytes 4194320 | tf_op jit(solution)/shard_map/psum | solution.py:275
  183.2 5.4 %copy.22 = f32[2,1024,512]{2,1,0:T(8,128)} copy(f32[2,1024,512]{1,2,0:T(8,128)} %all-reduce.3.cloned.1.call-done) | data formatting | bytes 8388608
  188.6 23.6 %reduce-scatter.2.cloned.1.call-done = bf16[1,768,512]{2,1,0:T(8,128)(2,1)} async-done(((bf16[1,768,1024]{2,1,0:T(8,128)(2,1)}), bf16[1,768,512]{2,1,0:T(8,128)(2,1)}) %reduce-scatter.2.cloned.1.call-update) | async-done | bytes 786448 | tf_op jit(solution)/shard_map/reduce_scatter | solution.py:276
  (7 shorter events, 0.1 us)
Async XLA Ops:
  7.2 22.5 %copy-start = (f32[2,8,512]{2,1,0:T(8,128)S(1)}, f32[2,8,512]{2,1,0:T(8,128)}, u32[]{:S(2)}) copy-start(f32[2,8,512]{2,1,0:T(8,128)} %param.12) | copy-start | bytes 98308
  7.2 32.3 %copy-start.2 = (bf16[2,1024,512]{2,1,0:T(8,128)(2,1)S(1)}, bf16[2,1024,512]{2,1,0:T(8,128)(2,1)}, u32[]{:S(2)}) copy-start(bf16[2,1024,512]{2,1,0:T(8,128)(2,1)} %proj_ref.1) | copy-start | bytes 6291460
  7.2 32.3 %copy-start.1 = (bf16[1,768,512]{2,1,0:T(8,128)(2,1)S(1)}, bf16[1,768,512]{2,1,0:T(8,128)(2,1)}, u32[]{:S(2)}) copy-start(bf16[1,768,512]{2,1,0:T(8,128)(2,1)} %param.15) | copy-start | bytes 2359300
  7.2 32.3 %all-gather.3.cloned.1.call-start = ((), (), s32[]{:S(2)}) async-start(), calls=%async_computation.1 | async-start | bytes 2359296 | tf_op jit(solution)/shard_map/all_gather | solution.py:158
  7.9 175.3 %all-reduce.3.cloned.1.call-start = ((), (), s32[]{:S(2)}) async-start(), calls=%async_computation.3 | async-start | bytes 8388608 | tf_op jit(solution)/shard_map/psum | solution.py:275
  39.5 1.4 copy-start.3
  40.9 17.2 %copy-start.7 = (f32[4,8]{1,0:T(4,128)S(1)}, f32[4,8]{1,0:T(4,128)}, u32[]{:S(2)}) copy-start(f32[4,8]{1,0:T(4,128)} %get-tuple-element.61) | copy-start | bytes 388
  40.9 17.2 %copy-start.8 = (f32[4,8]{1,0:T(4,128)S(1)}, f32[4,8]{1,0:T(4,128)}, u32[]{:S(2)}) copy-start(f32[4,8]{1,0:T(4,128)} %get-tuple-element.62) | copy-start | bytes 388
  40.9 17.5 %copy-start.5 = (f32[4,128,48]{2,1,0:T(8,128)S(1)}, f32[4,128,48]{2,1,0:T(8,128)}, u32[]{:S(2)}) copy-start(f32[4,128,48]{2,1,0:T(8,128)} %copy.19.cols_ref) | copy-start | bytes 294916
  58.3 22.5 %copy-start.4 = (bf16[1,768,1024]{2,1,0:T(8,128)(2,1)S(1)}, bf16[1,768,1024]{2,1,0:T(8,128)(2,1)}, u32[]{:S(2)}) copy-start(bf16[1,768,1024]{2,1,0:T(8,128)(2,1)} %all-gather.3.cloned.1.call-done) | copy-start | bytes 4718596
  79.7 1.2 copy-start.6
  84.7 127.4 %reduce-scatter.2.cloned.1.call-start = ((), (), s32[]{:S(2)}) async-start(), calls=%async_computation.2 | async-start | bytes 2359296 | tf_op jit(solution)/shard_map/reduce_scatter | solution.py:276
  89.2 0.7 copy-start.9
Sparse Core Ops, SparseCore 0:
  9.6 29.8 all-gather.2
  84.8 98.3 all-reduce.2
  186.0 26.1 reduce-scatter.1

commit v2 on v1

--- a/solution.py
+++ b/solution.py
@@ -148,6 +148,17 @@
     lax.fori_loop(0, blocks, backward, (carry_ref[0, 2 * M : 3 * M, :], carry_ref[0, 3 * M :, :]))
 
 
+def summed_over(value, axis):
+    size = lax.axis_size(axis)
+    if size & (size - 1):
+        return lax.psum(value, axis)
+    stride = 1
+    while stride < size:
+        value = value + lax.ppermute(value, axis, [(i, i ^ stride) for i in range(size)])
+        stride *= 2
+    return value
+
+
 def shards(frames_in, in_proj, log_rates, angles, residues, skip_gain, lengths, grad_out):
     rows = frames_in.shape[1]
     channels = frames_in.shape[2]
@@ -272,10 +283,19 @@
     skip_term = sums[:, 2 * M].reshape(channels) * norm_scale
     proj_term = jnp.einsum("ld,klc->kdc", features, stacked, preferred_element_type=F32) * norm_scale
     partial_in = jnp.einsum("klc,kdc->ld", stacked, in_proj, preferred_element_type=F32)
-    proj_sum, coeff_sum, skip_sum = lax.psum((proj_term, coeff_term, skip_term), ("tm", "dp"))
-    input_grad = lax.psum_scatter(
-        partial_in.astype(BF16)[None], "tensor", scatter_dimension=2, tiled=True
-    )
+    small = jnp.concatenate([coeff_term.reshape(2 * M, channels), skip_term[None]], axis=0)
+    proj_sum = lax.psum(proj_term.astype(BF16), ("tm", "dp")).astype(F32)
+    small = summed_over(summed_over(small, "dp"), "tm")
+    coeff_sum = small[: 2 * M].reshape(2, M, channels)
+    skip_sum = small[2 * M]
+    own, size = lax.axis_index("tensor"), lax.axis_size("tensor")
+    share = width // size
+    total_in = lax.dynamic_slice_in_dim(partial_in, own * share, share, 1)
+    for k in range(1, size):
+        other = lax.rem(own + k, size)
+        piece = lax.dynamic_slice_in_dim(partial_in, other * share, share, 1).astype(BF16)
+        total_in += lax.ppermute(piece, "tensor", [(i, (i + k) % size) for i in range(size)]).astype(F32)
+    input_grad = total_in.astype(BF16)[None]
     return (mixed[None], input_grad, proj_sum, coeff_sum, skip_sum)
 
 

time: 219 us -> 165 us (0.75)
  blocking collectives: 43.4 us -> 13.9 us
  waiting for transfers between devices: 96.4 us -> 68.7 us
  starting transfers between devices: 0.12 us -> 5.24 us
    psum x1 -> x0, blocking collectives: 29.5 us -> none  [shards(): lax.psum((proj_term, coeff_term, skip_term), ('tm', 'dp'))]
    reduce_scatter x1 -> x0, waiting for transfers between devices: 23.6 us -> none  [shards(): lax.psum_scatter(partial_in.astype(BF16)[None], 'tensor', scatter_dimensi...]
    psum x1, waiting for transfers between devices: 63.8 us -> 45.6 us  [shards(): proj_sum = lax.psum(proj_term.astype(BF16), ('tm', 'dp')).astype(F32)]
    ppermute x0 -> x4, waiting for transfers between devices: none -> 11.1 us  [the longest x3 7.48 us: summed_over(): lax.ppermute(value, axis, [(i, i ^ stride) for i in range(size)])]
    ppermute x0 -> x4, starting transfers between devices: none -> 5.16 us  [the longest x3 4.56 us: summed_over(): lax.ppermute(value, axis, [(i, i ^ stride) for i in range(size)])]
    unnamed x21 -> x15, local copies, waits for them, and re-layouts: 8.62 us -> 5.55 us
    all_gather x1, waiting for transfers between devices: 8.31 us -> 11.3 us  [shards(): features = lax.all_gather(frames_in, 'tensor', axis=2, tiled=True)[0]]
    broadcast_in_dim x0 -> x1, other arithmetic: none -> 2.56 us  [shards(): input_grad = total_in.astype(BF16)[None]]
  transfers between devices with their start and end apart: 3 -> 6, of which waited for: 3 -> 6; matrix products, arithmetic and copies ran while one was open for 12% -> 11% of each run, Pallas kernels for 0% -> 0%
where the time goes in v2:
time: 165 us
  waiting for transfers between devices  68.7 us (42%)
  Pallas kernels  24.4 us (15%)
  between operations  22 us (13%)
  other arithmetic  14.3 us (9%)
  blocking collectives  13.9 us (8%)
  local copies, waits for them, and re-layouts  9.25 us (6%)
  matrix products  6.62 us (4%)
  starting transfers between devices  5.24 us (3%)
    psum x1, waiting for transfers between devices, shards(): proj_sum = lax.psum(proj_term.astype(BF16), ('tm', 'dp')).astype(F32)  45.6 us
    pallas_call x1, Pallas kernels, shards(): pl.pallas_call(functools.partial(conv_kernel, clips, M), grid_spec=pltpu....  21.3 us
    all_gather x1, blocking collectives, shards(): gathered = lax.all_gather(ends, 'tm')  13.9 us
    all_gather x1, waiting for transfers between devices, shards(): features = lax.all_gather(frames_in, 'tensor', axis=2, tiled=True)[0]  11.3 us
    ppermute x3, waiting for transfers between devices, summed_over(): lax.ppermute(value, axis, [(i, i ^ stride) for i in range(size)])  7.48 us
    unnamed x15, local copies, waits for them, and re-layouts  5.55 us
    unnamed x6, other arithmetic  4.97 us
    ppermute x3, starting transfers between devices, summed_over(): lax.ppermute(value, axis, [(i, i ^ stride) for i in range(size)])  4.56 us
  transfers between devices with their start and end apart: 6, of which 6 were waited for; matrix products, arithmetic and copies ran while one was open for 11% of the time, Pallas kernels for 0%

profile of v2, /device:TPU:0, one launch (start us, length us, event | category | flops | bytes accessed | tf_op | source)
XLA Modules:
  0.0 164.5 jit_solution(5744491664773734251)
XLA Ops:
  7.2 0.0 copy-start
  7.2 0.0 copy-start.6
  7.2 0.0 copy-start.2
  7.2 0.0 copy-start.1
  7.2 0.0 all-gather.3.cloned.1.call-start
  7.3 0.7 all-gather.3.cloned.1.call-update
  7.9 0.0 all-reduce.2.cloned.1.call-start
  8.0 0.9 reduce-window.9
  8.9 0.7 sqrt_bitcast_fusion
  9.6 1.5 fusion.40
  18.8 0.8 broadcast_multiply_fusion.4
  19.6 0.8 constant_dynamic-update-slice_fusion.12
  20.4 0.8 constant_dynamic-update-slice_fusion.11
  21.2 0.8 constant_dynamic-update-slice_fusion.10
  22.1 0.8 constant_dynamic-update-slice_fusion.9
  22.9 0.9 constant_dynamic-update-slice_fusion.8
  23.8 0.8 constant_dynamic-update-slice_fusion.7
  24.6 0.8 constant_dynamic-update-slice_fusion
  25.4 0.8 copy.23.cols_ref
  26.3 0.1 pad.12.clone
  26.3 0.1 pad_add_fusion.starts_ref
  26.4 0.1 maximum_bitcast_fusion
  26.5 1.5 fusion.3
  28.0 0.1 constant_dynamic-update-slice_fusion.6.rows_ref
  28.1 0.0 copy-done
  28.1 0.1 fusion.7
  28.2 0.0 copy-done.6
  28.2 0.1 maximum_maximum_fusion.w_ref
  28.2 11.3 %all-gather.3.cloned.1.call-done = bf16[1,768,1024]{2,1,0:T(8,128)(2,1)} async-done(((bf16[1,768,512]{2,1,0:T(8,128)(2,1)}), bf16[1,768,1024]{2,1,0:T(8,128)(2,1)}) %all-gather.3.cloned.1.call-update) | async-done | bytes 1572880 | tf_op jit(solution)/shard_map/all_gather | solution.py:169
  39.5 0.0 copy-done.2
  39.5 0.0 copy-done.1
  39.5 0.0 copy-start.3
  39.6 1.4 copy-done.3
  41.0 0.0 copy-start.5
  41.0 3.2 %project.1 = (bf16[768,512]{1,0:T(8,128)(2,1)S(1)}, bf16[768,512]{1,0:T(8,128)(2,1)S(1)}, f32[4,32,128]{2,1,0:T(8,128)S(1)}) custom-call(s32[5]{0:T(128)S(1)} %pad_add_fusion.starts_ref, bf16[768,1024]{1,0:T(8,128)(2,1)S(1)} %bitcast.178, bf16[2,1024,512]{2,1,0:T(8,128)(2,1)S(1)} %copy-done.2, bf16[768,512]{1,0:T(8,128)(2,1)S(1)} %bitcast.176, ...), custom_call_target="tpu_custom_call" | custom-call | tf_op jit(solution)/shard_map/project/pallas_call | solution.py:198
  44.2 13.9 %all-gather = f32[16,32,128]{2,1,0:T(8,128)S(1)} all-gather(f32[4,32,128]{2,1,0:T(8,128)S(1)} %get-tuple-element.11), channel_id=2, replica_groups=mesh['group'=2,'tm'=4,'tensor'=2,'dp'=2] {'tm'}, dimensions={0}, use_global_device_ids=true | all-gather | bytes 327680 | tf_op jit(solution)/shard_map/all_gather | solution.py:224
  58.1 0.1 fusion.38
  58.2 0.1 fusion.26
  58.3 0.1 fusion.16
  58.4 0.0 copy-done.5
  58.4 21.3 %conv.1 = (bf16[768,512]{1,0:T(8,128)(2,1)}, bf16[2,768,512]{2,1,0:T(8,128)(2,1)S(1)}, f32[4,24,128]{2,1,0:T(8,128)S(1)}) custom-call(s32[5]{0:T(128)S(1)} %pad_add_fusion.starts_ref, f32[4,128,48]{2,1,0:T(8,128)S(1)} %copy-done.5, f32[4,64,128]{2,1,0:T(8,128)S(1)} %constant_dynamic-update-slice_fusion.6.rows_ref, ...), custom_call_target="tpu_custom_call" | custom-call | tf_op jit(solution)/shard_map/conv/pallas_call | solution.py:246
  79.6 0.0 copy-start.4
  79.6 3.5 %convolution_bitcast_fusion = f32[768,1024]{1,0:T(8,128)} fusion(bf16[2,768,512]{2,1,0:T(8,128)(2,1)S(1)} %get-tuple-element.15, bf16[2,1024,512]{2,1,0:T(8,128)(2,1)S(1)} %copy-done.2), kind=kOutput, calls=%fused_computation.1 | convolution fusion | flops 1610612736 | bytes 6815744 | tf_op jit(solution)/shard_map/klc,kdc->ld/dot_general | solution.py:285
  83.1 0.0 copy-done.4
  83.1 3.1 %fusion = bf16[2,1024,512]{1,2,0:T(8,128)(2,1)} fusion(bf16[2,768,512]{2,1,0:T(8,128)(2,1)S(1)} %get-tuple-element.15, bf16[1,768,1024]{2,1,0:T(8,128)(2,1)S(1)} %copy-done.4), kind=kOutput, calls=%fused_computation.2 | convolution fusion | flops 1612709888 | bytes 5242880 | tf_op jit(solution)/shard_map/ld,klc->kdc/dot_general | solution.py:284
  86.3 0.0 all-reduce.2.cloned.1.call-update
  86.3 1.5 dynamic-slice_convert_fusion
  87.8 0.6 collective-permute-start
  88.4 0.1 fusion.8
  88.5 0.1 collective-permute-start.1
  88.6 1.2 collective-permute-done.1
  89.8 2.0 %collective-permute-start.2 = (f32[17,512]{1,0:T(8,128)S(1)}, f32[17,512]{1,0:T(8,128)S(1)}, u32[]{:S(2)}, u32[]{:S(2)}) collective-permute-start(f32[17,512]{1,0:T(8,128)S(1)} %fusion.47), channel_id=1, source_target_pairs={{0,4},{4,0},{8,12},{12,8},{1,5},{5,1},{9,13},{13,9},{2,6},{6,2},{1... | collective-permute-start | bytes 104456 | tf_op jit(solution)/shard_map/ppermute | solution.py:157
  91.8 2.4 %collective-permute-done.2 = f32[17,512]{1,0:T(8,128)S(1)} collective-permute-done((f32[17,512]{1,0:T(8,128)S(1)}, f32[17,512]{1,0:T(8,128)S(1)}, u32[]{:S(2)}, u32[]{:S(2)}) %collective-permute-start.2) | collective-permute-done | bytes 34848 | tf_op jit(solution)/shard_map/ppermute | solution.py:157
  94.3 2.5 %collective-permute-start.3 = (f32[17,512]{1,0:T(8,128)S(1)}, f32[17,512]{1,0:T(8,128)S(1)}, u32[]{:S(2)}, u32[]{:S(2)}) collective-permute-start(f32[17,512]{1,0:T(8,128)S(1)} %add.98), channel_id=1, source_target_pairs={{0,8},{4,12},{8,0},{12,4},{1,9},{5,13},{9,1},{13,5},{2,10},{6,14},... | collective-permute-start | bytes 104456 | tf_op jit(solution)/shard_map/ppermute | solution.py:157
  96.8 3.8 %collective-permute-done.3 = f32[17,512]{1,0:T(8,128)S(1)} collective-permute-done((f32[17,512]{1,0:T(8,128)S(1)}, f32[17,512]{1,0:T(8,128)S(1)}, u32[]{:S(2)}, u32[]{:S(2)}) %collective-permute-start.3) | collective-permute-done | bytes 34848 | tf_op jit(solution)/shard_map/ppermute | solution.py:157
  100.6 0.6 slice.77
  101.2 0.6 slice_bitcast_fusion
  101.8 3.7 %collective-permute-done = bf16[768,512]{1,0:T(8,128)(2,1)S(1)} collective-permute-done((bf16[768,512]{1,0:T(8,128)(2,1)S(1)}, bf16[768,512]{1,0:T(8,128)(2,1)S(1)}, u32[]{:S(2)}, u32[]{:S(2)}) %collective-permute-start) | collective-permute-done | bytes 786464 | tf_op jit(solution)/shard_map/ppermute | solution.py:297
  105.4 2.6 %fusion.2 = bf16[1,768,512]{2,1,0:T(8,128)(2,1)} fusion(bf16[768,512]{1,0:T(8,128)(2,1)S(1)} %collective-permute-done, f32[768,1024]{1,0:T(8,128)} %convolution_bitcast_fusion, s32[]{:T(128)S(6)} %select_n.86), kind=kLoop, calls=%fused_computation.6 | loop fusion | flops 1179648 | bytes 3145732 | tf_op jit(solution)/shard_map/broadcast_in_dim | solution.py:298
  108.0 45.6 %all-reduce.2.cloned.1.call-done = bf16[2,1024,512]{1,2,0:T(8,128)(2,1)} async-done(((bf16[2,1024,512]{1,2,0:T(8,128)(2,1)}), bf16[2,1024,512]{1,2,0:T(8,128)(2,1)}) %all-reduce.2.cloned.1.call-update) | async-done | bytes 2097168 | tf_op jit(solution)/shard_map/psum | solution.py:287
  153.6 4.1 %copy.26 = f32[2,1024,512]{2,1,0:T(8,128)} copy(bf16[2,1024,512]{1,2,0:T(8,128)(2,1)} %all-reduce.2.cloned.1.call-done) | data formatting | bytes 6291456
  (12 shorter events, 0.1 us)
Async XLA Ops:
  7.2 20.9 %copy-start = (f32[2,8,512]{2,1,0:T(8,128)S(1)}, f32[2,8,512]{2,1,0:T(8,128)}, u32[]{:S(2)}) copy-start(f32[2,8,512]{2,1,0:T(8,128)} %param.12) | copy-start | bytes 98308
  7.2 21.0 %copy-start.6 = (f32[512]{0:T(512)S(1)}, f32[512]{0:T(512)}, u32[]{:S(2)}) copy-start(f32[512]{0:T(512)} %param.13) | copy-start | bytes 6148
  7.2 32.4 %copy-start.2 = (bf16[2,1024,512]{2,1,0:T(8,128)(2,1)S(1)}, bf16[2,1024,512]{2,1,0:T(8,128)(2,1)}, u32[]{:S(2)}) copy-start(bf16[2,1024,512]{2,1,0:T(8,128)(2,1)} %proj_ref.1) | copy-start | bytes 6291460
  7.2 32.3 %copy-start.1 = (bf16[1,768,512]{2,1,0:T(8,128)(2,1)S(1)}, bf16[1,768,512]{2,1,0:T(8,128)(2,1)}, u32[]{:S(2)}) copy-start(bf16[1,768,512]{2,1,0:T(8,128)(2,1)} %param.15) | copy-start | bytes 2359300
  7.2 32.3 %all-gather.3.cloned.1.call-start = ((), (), s32[]{:S(2)}) async-start(), calls=%async_computation | async-start | bytes 2359296 | tf_op jit(solution)/shard_map/all_gather | solution.py:169
  7.9 145.6 %all-reduce.2.cloned.1.call-start = ((), (), s32[]{:S(2)}) async-start(), calls=%async_computation.1 | async-start | bytes 4194304 | tf_op jit(solution)/shard_map/psum | solution.py:287
  39.5 1.4 copy-start.3
  41.0 17.4 %copy-start.5 = (f32[4,128,48]{2,1,0:T(8,128)S(1)}, f32[4,128,48]{2,1,0:T(8,128)}, u32[]{:S(2)}) copy-start(f32[4,128,48]{2,1,0:T(8,128)} %copy.23.cols_ref) | copy-start | bytes 294916
  79.6 3.5 %copy-start.4 = (bf16[1,768,1024]{2,1,0:T(8,128)(2,1)S(1)}, bf16[1,768,1024]{2,1,0:T(8,128)(2,1)}, u32[]{:S(2)}) copy-start(bf16[1,768,1024]{2,1,0:T(8,128)(2,1)} %all-gather.3.cloned.1.call-done) | copy-start | bytes 4718596
  87.8 17.6 %collective-permute-start = (bf16[768,512]{1,0:T(8,128)(2,1)S(1)}, bf16[768,512]{1,0:T(8,128)(2,1)S(1)}, u32[]{:S(2)}, u32[]{:S(2)}) collective-permute-start(bf16[768,512]{1,0:T(8,128)(2,1)S(1)} %dynamic-slice_convert_fusion), channel_id=1, source_target_pairs={{0,2},{2,0},{1,3},{3,1},{4,6},{6,4},{5,7},{7,5},{8,10},{10,8},{9,1... | collective-permute-start | bytes 2359304 | tf_op jit(solution)/shard_map/ppermute | solution.py:297
  88.5 1.3 collective-permute-start.1
  89.8 4.5 %collective-permute-start.2 = (f32[17,512]{1,0:T(8,128)S(1)}, f32[17,512]{1,0:T(8,128)S(1)}, u32[]{:S(2)}, u32[]{:S(2)}) collective-permute-start(f32[17,512]{1,0:T(8,128)S(1)} %fusion.47), channel_id=1, source_target_pairs={{0,4},{4,0},{8,12},{12,8},{1,5},{5,1},{9,13},{13,9},{2,6},{6,2},{1... | collective-permute-start | bytes 104456 | tf_op jit(solution)/shard_map/ppermute | solution.py:157
  94.3 6.3 %collective-permute-start.3 = (f32[17,512]{1,0:T(8,128)S(1)}, f32[17,512]{1,0:T(8,128)S(1)}, u32[]{:S(2)}, u32[]{:S(2)}) collective-permute-start(f32[17,512]{1,0:T(8,128)S(1)} %add.98), channel_id=1, source_target_pairs={{0,8},{4,12},{8,0},{12,4},{1,9},{5,13},{9,1},{13,5},{2,10},{6,14},... | collective-permute-start | bytes 104456 | tf_op jit(solution)/shard_map/ppermute | solution.py:157
Sparse Core Ops, SparseCore 0:
  9.6 29.9 all-gather.2
  86.4 67.1 all-reduce.1

commit v3 on v2

--- a/solution.py
+++ b/solution.py
@@ -24,7 +24,7 @@
     return total
 
 
-def project_kernel(clips, modes, starts_ref, feat_ref, proj_ref, up_ref, table_ref, q_ref, x_ref, ends_ref):
+def project_kernel(clips, modes, starts_ref, feat_ref, proj_ref, up_ref, tre_ref, tim_ref, q_ref, x_ref, ends_ref):
     rows, width = q_ref.shape
     first = starts_ref[0]
     lane = lax.broadcasted_iota(jnp.int32, (1, rows), 1) + first
@@ -38,41 +38,45 @@
     grad = (query.astype(F32) * up_ref[...].astype(F32)).astype(BF16)
     for h in range(width // 128):
         cols = slice(h * 128, h * 128 + 128)
-        fwd = (table_ref[h, : 2 * modes, :] * at_end).astype(BF16)
-        bwd = (table_ref[h, 2 * modes :, :] * at_start).astype(BF16)
+        fwd = jnp.concatenate([tre_ref[h, :, :rows], tim_ref[h, :, :rows]], axis=0)
+        bwd = jnp.concatenate([tre_ref[h, :, rows : 2 * rows], tim_ref[h, :, rows : 2 * rows]], axis=0)
+        fwd = (fwd * at_end).astype(BF16)
+        bwd = (bwd * at_start).astype(BF16)
         ends_ref[h, : 2 * modes, :] = dot(fwd, signal[:, cols])
         ends_ref[h, 2 * modes :, :] = dot(bwd, grad[:, cols])
 
 
 def conv_kernel(
-    clips, modes, starts_ref, cols_ref, rows_ref, w_ref, carry_ref, q_ref, x_ref, up_ref,
+    clips, modes, starts_ref, cre_ref, cim_ref, tre_ref, tim_ref, w_ref, u_ref, g_ref, q_ref, x_ref, up_ref,
     mixed_ref, stack_ref, sums_ref, kf, kb, tx,
 ):
     rows = q_ref.shape[0]
     blocks = rows // BLOCK_LEN
     M = modes
+    L = 2 * rows
     first = starts_ref[0]
     i0 = lax.broadcasted_iota(jnp.int32, (BLOCK_LEN, BLOCK_LEN), 0)
     i1 = lax.broadcasted_iota(jnp.int32, (BLOCK_LEN, BLOCK_LEN), 1)
     for m in range(M):
         re, im = m, M + m
-        er, ei = cols_ref[0, :, re : re + 1], cols_ref[0, :, im : im + 1]
-        fr = rows_ref[0, 2 * M + re : 2 * M + re + 1, :]
-        fi = rows_ref[0, 2 * M + im : 2 * M + im + 1, :]
+        er, ei = cre_ref[0, :128, m : m + 1], cim_ref[0, :128, m : m + 1]
+        fr, fi = tre_ref[0, m : m + 1, L + 128 : L + 256], tim_ref[0, m : m + 1, L + 128 : L + 256]
         kf[:, re * 128 : re * 128 + 128] = jnp.where(i0 >= i1, er * fr - ei * fi, 0.0).astype(BF16)
         kf[:, im * 128 : im * 128 + 128] = jnp.where(i0 >= i1, -(er * fi + ei * fr), 0.0).astype(BF16)
-        fr, fi = cols_ref[0, :, 2 * M + re : 2 * M + re + 1], cols_ref[0, :, 2 * M + im : 2 * M + im + 1]
-        er, ei = rows_ref[0, re : re + 1, :], rows_ref[0, im : im + 1, :]
+        fr, fi = cre_ref[0, 128:256, m : m + 1], cim_ref[0, 128:256, m : m + 1]
+        er, ei = tre_ref[0, m : m + 1, L : L + 128], tim_ref[0, m : m + 1, L : L + 128]
         kb[re * 128 : re * 128 + 128, :] = jnp.where(i1 >= i0, er * fr - ei * fi, 0.0).astype(BF16)
         kb[im * 128 : im * 128 + 128, :] = jnp.where(i1 >= i0, -(er * fi + ei * fr), 0.0).astype(BF16)
 
     w = w_ref[0, : 2 * M, :]
     wr, wi = w[:M], w[M:]
     skip = w_ref[0, 2 * M : 2 * M + 1, :]
-    pr = rows_ref[0, 6 * M : 7 * M, :]
-    pi = rows_ref[0, 7 * M : 8 * M, :]
-    col_p = cols_ref[0, :, : 2 * M].astype(BF16)
-    col_h = cols_ref[0, :, 4 * M : 6 * M].astype(BF16)
+    pr = tre_ref[0, :, L + 384 : L + 512]
+    pi = tim_ref[0, :, L + 384 : L + 512]
+    col_p = jnp.concatenate([cre_ref[0, :128, :], cim_ref[0, :128, :]], axis=1).astype(BF16)
+    col_h = jnp.concatenate([cre_ref[0, 256:, :], cim_ref[0, 256:, :]], axis=1).astype(BF16)
+    row_h = jnp.concatenate([tre_ref[0, :, L + 256 : L + 384], tim_ref[0, :, L + 256 : L + 384]], axis=0)
+    row_p = jnp.concatenate([tre_ref[0, :, L : L + 128], tim_ref[0, :, L : L + 128]], axis=0)
 
     def flag(cond):
         return jnp.where(cond, 1.0, 0.0).astype(F32)
@@ -106,7 +110,7 @@
         out = skip * xf + acc
         mixed_ref[at, :] = (q_ref[at, :].astype(F32) * out).astype(BF16)
         stack_ref[0, at, :] = (up_ref[at, :].astype(F32) * out).astype(BF16)
-        reach = (rows_ref[0, 4 * M : 6 * M, :] * flag(seg1[: 2 * M] == last)).astype(BF16)
+        reach = (row_h * flag(seg1[: 2 * M] == last)).astype(BF16)
         total = dot(reach, x)
         tx[b] = total
         keep = flag(last == prior)
@@ -115,7 +119,7 @@
             total[M:] + keep * (pr * ui + pi * ur),
         )
 
-    lax.fori_loop(0, blocks, forward, (carry_ref[0, :M, :], carry_ref[0, M : 2 * M, :]))
+    lax.fori_loop(0, blocks, forward, (u_ref[0, :M, :], u_ref[0, M:, :]))
     sums_ref[...] = jnp.zeros_like(sums_ref)
 
     def backward(step, carried):
@@ -137,7 +141,7 @@
         join = flag(last == after)
         sums_ref[0, :M, :] += join * (total[:M] * gr - total[M:] * gi)
         sums_ref[0, M : 2 * M, :] -= join * (total[:M] * gi + total[M:] * gr)
-        reach = (rows_ref[0, : 2 * M, :] * flag(seg1[: 2 * M] == head)).astype(BF16)
+        reach = (row_p * flag(seg1[: 2 * M] == head)).astype(BF16)
         lead = dot(reach, gb)
         keep = flag(head == after)
         return (
@@ -145,7 +149,7 @@
             lead[M:] + keep * (pr * gi + pi * gr),
         )
 
-    lax.fori_loop(0, blocks, backward, (carry_ref[0, 2 * M : 3 * M, :], carry_ref[0, 3 * M :, :]))
+    lax.fori_loop(0, blocks, backward, (g_ref[0, :M, :], g_ref[0, M:, :]))
 
 
 def summed_over(value, axis):
@@ -159,6 +163,42 @@
     return value
 
 
+def summed_matrix(value):
+    stages = []
+    for axis, kind in (("dp", F32), ("tm", BF16)):
+        size, place = lax.axis_size(axis), lax.axis_index(axis)
+        stride = 1
+        while stride < size:
+            upper = lax.rem(place // stride, 2)
+            pairs = [(i, i ^ stride) for i in range(size)]
+            half = value.shape[0] // 2
+            away = lax.dynamic_slice_in_dim(value, (1 - upper) * half, half, 0).astype(kind)
+            kept = lax.dynamic_slice_in_dim(value, upper * half, half, 0)
+            value = kept + lax.ppermute(away, axis, pairs).astype(F32)
+            stages.append((axis, pairs, upper))
+            stride *= 2
+    value = value.astype(BF16)
+    for axis, pairs, upper in reversed(stages):
+        other = lax.ppermute(value, axis, pairs)
+        low, high = jnp.where(upper == 0, value, other), jnp.where(upper == 0, other, value)
+        value = jnp.concatenate([low, high], axis=0)
+    return value.astype(F32)
+
+
+def widened(value, axis):
+    size, place = lax.axis_size(axis), lax.axis_index(axis)
+    pieces = [value]
+    for k in range(1, size):
+        pieces.append(lax.ppermute(value, axis, [(i, (i + k) % size) for i in range(size)]))
+    columns = []
+    for j in range(size):
+        column = pieces[0]
+        for k in range(1, size):
+            column = jnp.where(lax.rem(place - j + size, size) == k, pieces[k], column)
+        columns.append(column)
+    return jnp.concatenate(columns, axis=1)
+
+
 def shards(frames_in, in_proj, log_rates, angles, residues, skip_gain, lengths, grad_out):
     rows = frames_in.shape[1]
     channels = frames_in.shape[2]
@@ -166,25 +206,22 @@
     M, heads = log_rates.shape
     clips = lengths.shape[1]
     count, mine = lax.axis_size("tm"), lax.axis_index("tm")
-    features = lax.all_gather(frames_in, "tensor", axis=2, tiled=True)[0]
+    features = widened(frames_in[0], "tensor")
     upstream = grad_out[0]
     decay = jnp.exp(log_rates).T
     turn = angles.T
     weight = jnp.sqrt(-jnp.expm1(-2.0 * decay))
 
-    def powers(exponents):
-        exponents = jnp.asarray(exponents, F32)
-        size = jnp.exp(-decay[:, :, None] * exponents)
-        arg = turn[:, :, None] * exponents
-        return jnp.concatenate([size * jnp.cos(arg), size * jnp.sin(arg)], axis=1)
-
     lags = jnp.arange(BLOCK_LEN, dtype=jnp.int32)
-    ahead, back, rest = powers(lags), powers(-lags), powers(BLOCK_LEN - lags)
-    full = jnp.broadcast_to(powers(jnp.full((1,), BLOCK_LEN)), (heads, 2 * M, BLOCK_LEN))
-    row_table = jnp.concatenate([ahead, back, rest, full], axis=1)
-    col_table = jnp.concatenate([ahead, back, rest], axis=1).transpose(0, 2, 1)
     span = jnp.arange(rows, dtype=jnp.int32)
-    long_table = jnp.concatenate([powers(rows - span), powers(span)], axis=1)
+    steps = jnp.concatenate(
+        [rows - span, span, lags, -lags, BLOCK_LEN - lags, jnp.full_like(lags, BLOCK_LEN)]
+    ).astype(F32)
+    size = jnp.exp(-decay[:, :, None] * steps)
+    table_re = size * jnp.cos(turn[:, :, None] * steps)
+    table_im = size * jnp.sin(turn[:, :, None] * steps)
+    col_re = table_re[:, :, 2 * rows : 2 * rows + 3 * BLOCK_LEN].transpose(0, 2, 1)
+    col_im = table_im[:, :, 2 * rows : 2 * rows + 3 * BLOCK_LEN].transpose(0, 2, 1)
     coeffs = residues.reshape(2, M, heads, 128).transpose(2, 0, 1, 3) * weight[:, None, :, None]
     pad = jnp.zeros((heads, 7, 128), F32)
     w_table = jnp.concatenate(
@@ -204,7 +241,8 @@
                 pl.BlockSpec((rows, width), lambda i, s: (0, 0)),
                 pl.BlockSpec((2, width, wide), lambda i, s: (0, 0, i)),
                 pl.BlockSpec((rows, wide), lambda i, s: (0, i)),
-                pl.BlockSpec((pair, 4 * M, rows), lambda i, s: (i, 0, 0)),
+                pl.BlockSpec((pair, M, steps.size), lambda i, s: (i, 0, 0)),
+                pl.BlockSpec((pair, M, steps.size), lambda i, s: (i, 0, 0)),
             ],
             out_specs=[
                 pl.BlockSpec((rows, wide), lambda i, s: (0, i)),
@@ -219,27 +257,37 @@
         ],
         compiler_params=pltpu.CompilerParams(vmem_limit_bytes=40 << 20),
         name="project",
-    )(starts, features, in_proj, upstream, long_table)
-
-    gathered = lax.all_gather(ends, "tm")
-    step = powers(jnp.full((1,), rows))
-    step_re, step_im = step[:, :M], step[:, M:]
+    )(starts, features, in_proj, upstream, table_re, table_im)
+
+    step_re, step_im = table_re[:, :, :1], table_im[:, :, :1]
 
     def segment_at(frame):
         return jnp.sum((frame >= clip_start).astype(jnp.int32))
 
-    ur = ui = gr = gi = jnp.zeros((heads, M, 128), F32)
-    for d in range(count - 1):
-        keep = (segment_at(d * rows - 1) == segment_at(d * rows + rows - 1)).astype(F32)
-        nr = gathered[d, :, :M] + keep * (step_re * ur - step_im * ui)
-        ni = gathered[d, :, M : 2 * M] + keep * (step_re * ui + step_im * ur)
-        ur, ui = jnp.where(d < mine, nr, ur), jnp.where(d < mine, ni, ui)
-    for d in range(count - 1, 0, -1):
-        keep = (segment_at(d * rows) == segment_at(d * rows + rows)).astype(F32)
-        nr = gathered[d, :, 2 * M : 3 * M] + keep * (step_re * gr - step_im * gi)
-        ni = gathered[d, :, 3 * M :] + keep * (step_re * gi + step_im * gr)
-        gr, gi = jnp.where(d > mine, nr, gr), jnp.where(d > mine, ni, gi)
-    carries = jnp.concatenate([ur, ui, gr, gi], axis=1)
+    def join(state, own, keep):
+        re, im = state[:, :M], state[:, M:]
+        turned = jnp.concatenate([step_re * re - step_im * im, step_re * im + step_im * re], axis=1)
+        return own + keep.astype(F32) * turned
+
+    entering = leaving = jnp.zeros((heads, 2 * M, 128), F32)
+    if count <= 8:
+        for k in range(count - 1, 0, -1):
+            before = lax.ppermute(ends[:, : 2 * M], "tm", [(i, i + k) for i in range(count - k)])
+            behind = lax.ppermute(ends[:, 2 * M :], "tm", [(i + k, i) for i in range(count - k)])
+            d = mine - k
+            entering = join(
+                entering, before, segment_at(d * rows - 1) == segment_at(d * rows + rows - 1)
+            )
+            d = mine + k
+            leaving = join(leaving, behind, segment_at(d * rows) == segment_at(d * rows + rows))
+    else:
+        gathered = lax.all_gather(ends, "tm")
+        for d in range(count - 1):
+            keep = segment_at(d * rows - 1) == segment_at(d * rows + rows - 1)
+            entering = jnp.where(d < mine, join(entering, gathered[d, :, : 2 * M], keep), entering)
+        for d in range(count - 1, 0, -1):
+            keep = segment_at(d * rows) == segment_at(d * rows + rows)
+            leaving = jnp.where(d > mine, join(leaving, gathered[d, :, 2 * M :], keep), leaving)
 
     per_head = lambda i, s: (i, 0, 0)
     column = lambda i, s: (0, i)
@@ -249,10 +297,13 @@
             num_scalar_prefetch=1,
             grid=(heads,),
             in_specs=[
-                pl.BlockSpec((1, BLOCK_LEN, 6 * M), per_head),
-                pl.BlockSpec((1, 8 * M, BLOCK_LEN), per_head),
+                pl.BlockSpec((1, 3 * BLOCK_LEN, M), per_head),
+                pl.BlockSpec((1, 3 * BLOCK_LEN, M), per_head),
+                pl.BlockSpec((1, M, steps.size), per_head),
+                pl.BlockSpec((1, M, steps.size), per_head),
                 pl.BlockSpec((1, 2 * M + 8, 128), per_head),
-                pl.BlockSpec((1, 4 * M, 128), per_head),
+                pl.BlockSpec((1, 2 * M, 128), per_head),
+                pl.BlockSpec((1, 2 * M, 128), per_head),
                 pl.BlockSpec((rows, 128), column),
                 pl.BlockSpec((rows, 128), column),
                 pl.BlockSpec((rows, 128), column),
@@ -275,16 +326,19 @@
         ],
         compiler_params=pltpu.CompilerParams(vmem_limit_bytes=40 << 20),
         name="conv",
-    )(starts, col_table, row_table, w_table, carries, query_rows, signal, upstream)
+    )(starts, col_re, col_im, table_re, table_im, w_table, entering, leaving, query_rows, signal, upstream)
 
     norm_scale = 1.0 / math.sqrt(rows * count * lax.axis_size("dp"))
     coeff_term = sums[:, : 2 * M].reshape(heads, 2, M, 128) * (weight[:, None, :, None] * norm_scale)
     coeff_term = coeff_term.transpose(1, 2, 0, 3).reshape(2, M, channels)
     skip_term = sums[:, 2 * M].reshape(channels) * norm_scale
-    proj_term = jnp.einsum("ld,klc->kdc", features, stacked, preferred_element_type=F32) * norm_scale
+    proj_terms = [
+        jnp.einsum("ld,lc->dc", features, stacked[k], preferred_element_type=F32) * norm_scale
+        for k in range(2)
+    ]
     partial_in = jnp.einsum("klc,kdc->ld", stacked, in_proj, preferred_element_type=F32)
     small = jnp.concatenate([coeff_term.reshape(2 * M, channels), skip_term[None]], axis=0)
-    proj_sum = lax.psum(proj_term.astype(BF16), ("tm", "dp")).astype(F32)
+    proj_sum = jnp.stack([summed_matrix(term) for term in proj_terms])
     small = summed_over(summed_over(small, "dp"), "tm")
     coeff_sum = small[: 2 * M].reshape(2, M, channels)
     skip_sum = small[2 * M]

time: 165 us -> 148 us (0.90)
  starting transfers between devices: 5.24 us -> 25.8 us
  blocking collectives: 13.9 us -> 0 us
  between operations: 22 us -> 8.8 us
  waiting for transfers between devices: 68.7 us -> 64.3 us
  matrix products: 6.62 us -> 3.83 us
  other arithmetic: 14.3 us -> 12.6 us
    ppermute x0 -> x19, waiting for transfers between devices: none -> 57.1 us  [the longest x6 24.8 us: summed_matrix(): value = kept + lax.ppermute(away, axis, pairs).astype(F32)]
    psum x1 -> x0, waiting for transfers between devices: 45.6 us -> none  [shards(): proj_sum = lax.psum(proj_term.astype(BF16), ('tm', 'dp')).astype(F32)]
    ppermute x0 -> x19, starting transfers between devices: none -> 23.4 us  [the longest x3 13.1 us: shards(): lax.ppermute(ends[:, :2 * M], 'tm', [(i, i + k) for i in range(count - k)])]
    all_gather x1 -> x0, blocking collectives: 13.9 us -> none  [shards(): gathered = lax.all_gather(ends, 'tm')]
    all_gather x1 -> x0, waiting for transfers between devices: 11.3 us -> none  [shards(): features = lax.all_gather(frames_in, 'tensor', axis=2, tiled=True)[0]]
    unnamed x6 -> x4, other arithmetic: 4.97 us -> 0.02 us
    ppermute x3, starting transfers between devices: 4.56 us -> 0.69 us  [summed_over(): lax.ppermute(value, axis, [(i, i ^ stride) for i in range(size)])]
    ppermute x1, waiting for transfers between devices: 3.67 us -> 0.01 us  [shards(): lax.ppermute(piece, 'tensor', [(i, (i + k) % size) for i in range(size)])]
  transfers between devices with their start and end apart: 6 -> 23, of which waited for: 6 -> 14; matrix products, arithmetic and copies ran while one was open for 11% -> 9% of each run, Pallas kernels for 0% -> 0%
where the time goes in v3:
time: 148 us; the launch traced here: 147 us
  waiting for transfers between devices  64.3 us (43%)
  starting transfers between devices  25.8 us (17%)
  Pallas kernels  24 us (16%)
  other arithmetic  12.6 us (9%)
  between operations  8.8 us (6%)
  local copies, waits for them, and re-layouts  7.83 us (5%)
  matrix products  3.83 us (3%)
    ppermute x6, waiting for transfers between devices, summed_matrix(): value = kept + lax.ppermute(away, axis, pairs).astype(F32)  24.8 us
    pallas_call x1, Pallas kernels, shards(): pl.pallas_call(functools.partial(conv_kernel, clips, M), grid_spec=pltpu....  20.8 us
    ppermute x6, waiting for transfers between devices, summed_matrix(): other = lax.ppermute(value, axis, pairs)  16.3 us
    ppermute x3, starting transfers between devices, shards(): lax.ppermute(ends[:, :2 * M], 'tm', [(i, i + k) for i in range(count - k)])  13.1 us
    ppermute x1, waiting for transfers between devices, widened(): lax.ppermute(value, axis, [(i, (i + k) % size) for i in range(size)])  11.8 us
    ppermute x3, waiting for transfers between devices, summed_over(): lax.ppermute(value, axis, [(i, i ^ stride) for i in range(size)])  7.26 us
    unnamed x28, local copies, waits for them, and re-layouts  5.38 us
    ppermute x3, waiting for transfers between devices, shards(): lax.ppermute(ends[:, 2 * M:], 'tm', [(i + k, i) for i in range(count - k)])  4.1 us
  transfers between devices with their start and end apart: 23, of which 14 were waited for; matrix products, arithmetic and copies ran while one was open for 9% of the time, Pallas kernels for 0%

profile of v3, /device:TPU:0, one launch (start us, length us, event | category | flops | bytes accessed | tf_op | source)
XLA Modules:
  0.0 147.1 jit_solution(1506418058037207028)
XLA Ops:
  0.6 3.0 %collective-permute-start = (bf16[768,512]{1,0:T(8,128)(2,1)}, bf16[768,512]{1,0:T(8,128)(2,1)S(1)}, u32[]{:S(2)}, u32[]{:S(2)}) collective-permute-start(bf16[768,512]{1,0:T(8,128)(2,1)} %bitcast.68), channel_id=1, source_target_pairs={{0,2},{2,0},{1,3},{3,1},{4,6},{6,4},{5,7},{7,5},{8,10},{10,8},{9,1... | collective-permute-start | bytes 2359304 | tf_op jit(solution)/shard_map/ppermute | solution.py:192
  3.7 0.8 reduce-window.9
  4.5 0.7 sqrt_bitcast_fusion
  5.3 0.1 pad.28.clone
  5.3 1.7 %fusion.6 = (f32[4,8,2048]{2,1,0:T(8,128)S(1)}, f32[4,8,2048]{2,1,0:T(8,128)S(1)}) fusion(f32[4,8]{1,0:T(4,128)} %bitcast.69, f32[2048]{0:T(1024)S(1)} %convert_element_type.116, f32[4,8]{1,0:T(4,128)S(1)} %get-tuple-element.65), kind=kLoop, calls=%fused_computation.29 | loop fusion | flops 262144 | bytes 532736 | tf_op jit(solution)/shard_map/mul | solution.py:222
  7.0 0.1 slice_reduce_fusion
  7.1 1.5 %fusion.24 = (s32[]{:T(128)}, s32[]{:T(128)}, s32[]{:T(128)}, s32[]{:T(128)}, s32[]{:T(128)}, /*index=5*/s32[]{:T(128)}, s32[]{:T(128)}, s32[]{:T(128)}, s32[]{:...) fusion(s32[]{:T(128)S(6)} %add.153, s32[]{:T(128)S(6)} %add.157, s32[]{:T(128)S(6)} %mul.369, ...), kind=kLoop, calls=%fused_computation.111 | loop fusion | flops 136 | bytes 144 | tf_op jit(solution)/shard_map/reduce_sum | solution.py:265
  8.8 0.8 maximum_maximum_fusion.w_ref
  9.6 11.8 %collective-permute-done = bf16[768,512]{1,0:T(8,128)(2,1)S(1)} collective-permute-done((bf16[768,512]{1,0:T(8,128)(2,1)}, bf16[768,512]{1,0:T(8,128)(2,1)S(1)}, u32[]{:S(2)}, u32[]{:S(2)}) %collective-permute-start) | collective-permute-done | bytes 786464 | tf_op jit(solution)/shard_map/ppermute | solution.py:192
  21.4 1.2 broadcast_select_fusion.1
  22.7 0.2 pad_maximum_fusion.feat_ref
  22.9 0.6 copy-done.8
  23.5 0.3 copy-done.10
  23.8 0.6 copy-done.1
  24.4 0.7 copy-done.2
  25.1 3.2 %project.1 = (bf16[768,512]{1,0:T(8,128)(2,1)S(1)}, bf16[768,512]{1,0:T(8,128)(2,1)S(1)}, f32[4,32,128]{2,1,0:T(8,128)S(1)}) custom-call(s32[5]{0:T(128)S(1)} %pad_add_fusion.starts_ref, bf16[768,1024]{1,0:T(8,128)(2,1)S(1)} %pad_maximum_fusion.feat_ref, bf16[2,1024,512]{2,1,0:T(8,128)(2,1)S(1)} %copy-done.2, bf16[768,512]{1,0:T(8,128)(2,1)S(1)} %bitcast.66, ...), custom_call_target="tpu_custom_call" | custom-call | tf_op jit(solution)/shard_map/project/pallas_call | solution.py:235
  28.3 0.9 copy-done.4
  29.2 1.3 collective-permute-start.6
  30.4 6.3 %collective-permute-start.3 = (f32[4,16,128]{2,1,0:T(8,128)S(1)}, f32[4,16,128]{2,1,0:T(8,128)S(1)}, u32[]{:S(2)}, u32[]{:S(2)}) collective-permute-start(f32[4,16,128]{2,1,0:T(8,128)S(1)} %get-tuple-element.45), channel_id=1, source_target_pairs={{0,12},{1,13},{2,14},{3,15},{16,28},{17,29},{18,30},{19,31}} | collective-permute-start | bytes 98312 | tf_op jit(solution)/shard_map/ppermute | solution.py:275
  36.9 0.3 copy.17.cre_ref
  37.2 0.3 copy.18.cim_ref
  45.0 1.3 collective-permute-start.1
  46.3 1.3 collective-permute-start.5
  47.6 5.4 %collective-permute-start.2 = (f32[4,16,128]{2,1,0:T(8,128)S(1)}, f32[4,16,128]{2,1,0:T(8,128)S(1)}, u32[]{:S(2)}, u32[]{:S(2)}) collective-permute-start(f32[4,16,128]{2,1,0:T(8,128)S(1)} %get-tuple-element.45), channel_id=1, source_target_pairs={{0,8},{4,12},{1,9},{5,13},{2,10},{6,14},{3,11},{7,15},{16,24},{20,... | collective-permute-start | bytes 98312 | tf_op jit(solution)/shard_map/ppermute | solution.py:275
  53.0 1.3 collective-permute-start.4
  54.5 0.1 multiply_subtract_fusion.1
  54.6 0.1 multiply_subtract_fusion
  54.7 4.1 %collective-permute-done.4 = f32[4,16,128]{2,1,0:T(8,128)S(1)} collective-permute-done((f32[4,16,128]{2,1,0:T(8,128)S(1)}, f32[4,16,128]{2,1,0:T(8,128)S(1)}, u32[]{:S(2)}, u32[]{:S(2)}) %collective-permute-start.4) | collective-permute-done | bytes 32800 | tf_op jit(solution)/shard_map/ppermute | solution.py:276
  58.8 1.1 copy-done.5
  60.0 1.1 copy-done.7
  61.1 20.8 %conv.1 = (bf16[768,512]{1,0:T(8,128)(2,1)}, bf16[2,768,512]{2,1,0:T(8,128)(2,1)S(1)}, f32[4,24,128]{2,1,0:T(8,128)S(1)}) custom-call(s32[5]{0:T(128)S(1)} %pad_add_fusion.starts_ref, f32[4,384,8]{2,1,0:T(8,128)S(1)} %copy.17.cre_ref, f32[4,384,8]{2,1,0:T(8,128)S(1)} %copy.18.cim_ref, f32[4,8,2048]{2,1,0:T(8,128)S(1)} %get-tuple-element.57.tre_ref, ...), custom_call_target="tpu_custom_call" | custom-call | tf_op jit(solution)/shard_map/conv/pallas_call | solution.py:294
  81.9 1.0 convolution_multiply_fusion
  82.9 1.0 convolution_multiply_fusion.1
  83.9 0.1 constant_dynamic-slice_fusion
  84.2 0.6 collective-permute-start.20
  84.8 0.1 collective-permute-start.8
  84.9 1.9 %collective-permute-done.20 = f32[17,512]{1,0:T(8,128)S(1)} collective-permute-done((f32[17,512]{1,0:T(8,128)S(1)}, f32[17,512]{1,0:T(8,128)S(1)}, u32[]{:S(2)}, u32[]{:S(2)}) %collective-permute-start.20) | collective-permute-done | bytes 34848 | tf_op jit(solution)/shard_map/ppermute | solution.py:161
  86.9 1.8 %convolution_bitcast_fusion = f32[768,1024]{1,0:T(8,128)S(1)} fusion(bf16[2,768,512]{2,1,0:T(8,128)(2,1)S(1)} %get-tuple-element.15, bf16[2,1024,512]{2,1,0:T(8,128)(2,1)S(1)} %copy-done.3), kind=kOutput, calls=%fused_computation.1 | convolution fusion | flops 1610612736 | bytes 6815744 | tf_op jit(solution)/shard_map/klc,kdc->ld/dot_general | solution.py:339
  88.7 2.2 %collective-permute-done.21 = f32[17,512]{1,0:T(8,128)S(1)} collective-permute-done((f32[17,512]{1,0:T(8,128)S(1)}, f32[17,512]{1,0:T(8,128)S(1)}, u32[]{:S(2)}, u32[]{:S(2)}) %collective-permute-start.21) | collective-permute-done | bytes 34848 | tf_op jit(solution)/shard_map/ppermute | solution.py:161
  91.1 0.1 dynamic-slice_convert_fusion
  91.2 1.7 %collective-permute-start.7 = (bf16[768,512]{1,0:T(8,128)(2,1)S(1)}, bf16[768,512]{1,0:T(8,128)(2,1)S(1)}, u32[]{:S(2)}, u32[]{:S(2)}) collective-permute-start(bf16[768,512]{1,0:T(8,128)(2,1)S(1)} %dynamic-slice_convert_fusion), channel_id=1, source_target_pairs={{0,2},{2,0},{1,3},{3,1},{4,6},{6,4},{5,7},{7,5},{8,10},{10,8},{9,1... | collective-permute-start | bytes 2359304 | tf_op jit(solution)/shard_map/ppermute | solution.py:351
  92.9 3.1 %collective-permute-done.22 = f32[17,512]{1,0:T(8,128)S(1)} collective-permute-done((f32[17,512]{1,0:T(8,128)S(1)}, f32[17,512]{1,0:T(8,128)S(1)}, u32[]{:S(2)}, u32[]{:S(2)}) %collective-permute-start.22) | collective-permute-done | bytes 34848 | tf_op jit(solution)/shard_map/ppermute | solution.py:161
  96.1 0.6 slice.97
  96.6 0.6 slice_bitcast_fusion.2
  97.3 0.2 dynamic-slice_add_fusion
  97.6 0.2 dynamic-slice_add_fusion.1
  97.9 2.1 %collective-permute-start.9 = (bf16[256,512]{1,0:T(8,128)(2,1)S(1)}, bf16[256,512]{1,0:T(8,128)(2,1)S(1)}, u32[]{:S(2)}, u32[]{:S(2)}) collective-permute-start(bf16[256,512]{1,0:T(8,128)(2,1)S(1)} %dynamic-slice_convert_fusion.2), channel_id=1, source_target_pairs={{0,4},{4,0},{8,12},{12,8},{1,5},{5,1},{9,13},{13,9},{2,6},{6,2},{1... | collective-permute-start | bytes 786440 | tf_op jit(solution)/shard_map/ppermute | solution.py:177
  100.0 8.3 %collective-permute-done.15 = bf16[256,512]{1,0:T(8,128)(2,1)S(1)} collective-permute-done((bf16[256,512]{1,0:T(8,128)(2,1)S(1)}, bf16[256,512]{1,0:T(8,128)(2,1)S(1)}, u32[]{:S(2)}, u32[]{:S(2)}) %collective-permute-start.15) | collective-permute-done | bytes 262176 | tf_op jit(solution)/shard_map/ppermute | solution.py:177
  108.4 2.8 %collective-permute-done.9 = bf16[256,512]{1,0:T(8,128)(2,1)S(1)} collective-permute-done((bf16[256,512]{1,0:T(8,128)(2,1)S(1)}, bf16[256,512]{1,0:T(8,128)(2,1)S(1)}, u32[]{:S(2)}, u32[]{:S(2)}) %collective-permute-start.9) | collective-permute-done | bytes 262176 | tf_op jit(solution)/shard_map/ppermute | solution.py:177
  111.3 0.2 collective-permute-start.10
  111.5 8.3 %collective-permute-done.16 = bf16[128,512]{1,0:T(8,128)(2,1)S(1)} collective-permute-done((bf16[128,512]{1,0:T(8,128)(2,1)S(1)}, bf16[128,512]{1,0:T(8,128)(2,1)S(1)}, u32[]{:S(2)}, u32[]{:S(2)}) %collective-permute-start.16) | collective-permute-done | bytes 131104 | tf_op jit(solution)/shard_map/ppermute | solution.py:177
  119.9 5.5 %collective-permute-done.10 = bf16[128,512]{1,0:T(8,128)(2,1)S(1)} collective-permute-done((bf16[128,512]{1,0:T(8,128)(2,1)S(1)}, bf16[128,512]{1,0:T(8,128)(2,1)S(1)}, u32[]{:S(2)}, u32[]{:S(2)}) %collective-permute-start.10) | collective-permute-done | bytes 131104 | tf_op jit(solution)/shard_map/ppermute | solution.py:177
  125.5 4.2 %collective-permute-done.17 = bf16[128,512]{1,0:T(8,128)(2,1)S(1)} collective-permute-done((bf16[128,512]{1,0:T(8,128)(2,1)S(1)}, bf16[128,512]{1,0:T(8,128)(2,1)S(1)}, u32[]{:S(2)}, u32[]{:S(2)}) %collective-permute-start.17) | collective-permute-done | bytes 131104 | tf_op jit(solution)/shard_map/ppermute | solution.py:182
  129.8 1.6 %collective-permute-done.11 = bf16[128,512]{1,0:T(8,128)(2,1)S(1)} collective-permute-done((bf16[128,512]{1,0:T(8,128)(2,1)S(1)}, bf16[128,512]{1,0:T(8,128)(2,1)S(1)}, u32[]{:S(2)}, u32[]{:S(2)}) %collective-permute-start.11) | collective-permute-done | bytes 131104 | tf_op jit(solution)/shard_map/ppermute | solution.py:182
  131.5 0.5 collective-permute-start.12
  132.0 7.1 %collective-permute-done.18 = bf16[256,512]{1,0:T(8,128)(2,1)S(1)} collective-permute-done((bf16[256,512]{1,0:T(8,128)(2,1)S(1)}, bf16[256,512]{1,0:T(8,128)(2,1)S(1)}, u32[]{:S(2)}, u32[]{:S(2)}) %collective-permute-start.18) | collective-permute-done | bytes 262176 | tf_op jit(solution)/shard_map/ppermute | solution.py:182
  139.1 0.1 broadcast_select_fusion.3
  139.3 3.0 %collective-permute-done.12 = bf16[256,512]{1,0:T(8,128)(2,1)S(1)} collective-permute-done((bf16[256,512]{1,0:T(8,128)(2,1)S(1)}, bf16[256,512]{1,0:T(8,128)(2,1)S(1)}, u32[]{:S(2)}, u32[]{:S(2)}) %collective-permute-start.12) | collective-permute-done | bytes 262176 | tf_op jit(solution)/shard_map/ppermute | solution.py:182
  142.2 0.1 broadcast_select_fusion.5
  142.4 1.2 fusion
  143.6 0.2 select_bitcast_fusion.1
  143.8 0.5 collective-permute-done.13
  144.3 0.2 select_bitcast_fusion.3
  144.5 2.6 %maximum_convert_fusion = f32[2,1024,512]{2,1,0:T(8,128)} fusion(bf16[1,512,512]{2,1,0:T(8,128)(2,1)S(1)} %get-tuple-element.35, bf16[1,512,512]{2,1,0:T(8,128)(2,1)S(1)} %get-tuple-element.34, bf16[1,512,512]{2,1,0:T(8,128)(2,1)S(1)} %get-tuple-element.33, bf16[1,512,512]{2,1,0:T(8,128)(2,1)S(1)} %get-tuple-element.32), kind=kLoop, calls=%fused_computation | loop fusion | flops 8388608 | bytes 6291456 | tf_op jit(solution)/shard_map/stack | solution.py:341
  (81 shorter events, 1.9 us)
Async XLA Ops:
  0.6 8.1 %copy-start = (f32[2,8,512]{2,1,0:T(8,128)S(1)}, f32[2,8,512]{2,1,0:T(8,128)}, u32[]{:S(2)}) copy-start(f32[2,8,512]{2,1,0:T(8,128)} %param.12) | copy-start | bytes 98308
  0.6 20.8 %collective-permute-start = (bf16[768,512]{1,0:T(8,128)(2,1)}, bf16[768,512]{1,0:T(8,128)(2,1)S(1)}, u32[]{:S(2)}, u32[]{:S(2)}) collective-permute-start(bf16[768,512]{1,0:T(8,128)(2,1)} %bitcast.68), channel_id=1, source_target_pairs={{0,2},{2,0},{1,3},{3,1},{4,6},{6,4},{5,7},{7,5},{8,10},{10,8},{9,1... | collective-permute-start | bytes 2359304 | tf_op jit(solution)/shard_map/ppermute | solution.py:192
  22.6 0.9 copy-start.8
  22.7 1.1 copy-start.10
  22.7 1.7 %copy-start.1 = (bf16[1,768,512]{2,1,0:T(8,128)(2,1)S(1)}, bf16[1,768,512]{2,1,0:T(8,128)(2,1)}, u32[]{:S(2)}) copy-start(bf16[1,768,512]{2,1,0:T(8,128)(2,1)} %param.15) | copy-start | bytes 2359300
  22.7 2.4 %copy-start.2 = (bf16[2,1024,512]{2,1,0:T(8,128)(2,1)S(1)}, bf16[2,1024,512]{2,1,0:T(8,128)(2,1)}, u32[]{:S(2)}) copy-start(bf16[2,1024,512]{2,1,0:T(8,128)(2,1)} %proj_ref.1) | copy-start | bytes 6291460
  25.1 11.7 %copy-start.12 = (f32[8,4]{0,1:T(4,128)S(1)}, f32[8,4]{0,1:T(4,128)}, u32[]{:S(2)}) copy-start(f32[8,4]{0,1:T(4,128)} %param.10) | copy-start | bytes 388
  28.3 0.9 copy-start.4
  29.1 8.0 %copy-start.6 = (bf16[768,512]{1,0:T(8,128)(2,1)}, bf16[768,512]{1,0:T(8,128)(2,1)S(1)}, u32[]{:S(2)}) copy-start(bf16[768,512]{1,0:T(8,128)(2,1)S(1)} %get-tuple-element.13.x_ref) | copy-start | bytes 2359300
  29.2 23.9 %collective-permute-start.6 = (f32[4,16,128]{2,1,0:T(8,128)S(1)}, f32[4,16,128]{2,1,0:T(8,128)S(1)}, u32[]{:S(2)}, u32[]{:S(2)}) collective-permute-start(f32[4,16,128]{2,1,0:T(8,128)S(1)} %get-tuple-element.44), channel_id=1, source_target_pairs={{12,0},{13,1},{14,2},{15,3},{28,16},{29,17},{30,18},{31,19}} | collective-permute-start | bytes 98312 | tf_op jit(solution)/shard_map/ppermute | solution.py:276
  30.4 23.9 %collective-permute-start.3 = (f32[4,16,128]{2,1,0:T(8,128)S(1)}, f32[4,16,128]{2,1,0:T(8,128)S(1)}, u32[]{:S(2)}, u32[]{:S(2)}) collective-permute-start(f32[4,16,128]{2,1,0:T(8,128)S(1)} %get-tuple-element.45), channel_id=1, source_target_pairs={{0,12},{1,13},{2,14},{3,15},{16,28},{17,29},{18,30},{19,31}} | collective-permute-start | bytes 98312 | tf_op jit(solution)/shard_map/ppermute | solution.py:275
  45.0 9.8 %collective-permute-start.1 = (f32[4,16,128]{2,1,0:T(8,128)S(1)}, f32[4,16,128]{2,1,0:T(8,128)S(1)}, u32[]{:S(2)}, u32[]{:S(2)}) collective-permute-start(f32[4,16,128]{2,1,0:T(8,128)S(1)} %get-tuple-element.45), channel_id=1, source_target_pairs={{0,4},{4,8},{8,12},{1,5},{5,9},{9,13},{2,6},{6,10},{10,14},{3,7},{... | collective-permute-start | bytes 98312 | tf_op jit(solution)/shard_map/ppermute | solution.py:275
  46.3 8.3 %collective-permute-start.5 = (f32[4,16,128]{2,1,0:T(8,128)S(1)}, f32[4,16,128]{2,1,0:T(8,128)S(1)}, u32[]{:S(2)}, u32[]{:S(2)}) collective-permute-start(f32[4,16,128]{2,1,0:T(8,128)S(1)} %get-tuple-element.44), channel_id=1, source_target_pairs={{8,0},{12,4},{9,1},{13,5},{10,2},{14,6},{11,3},{15,7},{24,16},{28,... | collective-permute-start | bytes 98312 | tf_op jit(solution)/shard_map/ppermute | solution.py:276
  47.6 7.0 %collective-permute-start.2 = (f32[4,16,128]{2,1,0:T(8,128)S(1)}, f32[4,16,128]{2,1,0:T(8,128)S(1)}, u32[]{:S(2)}, u32[]{:S(2)}) collective-permute-start(f32[4,16,128]{2,1,0:T(8,128)S(1)} %get-tuple-element.45), channel_id=1, source_target_pairs={{0,8},{4,12},{1,9},{5,13},{2,10},{6,14},{3,11},{7,15},{16,24},{20,... | collective-permute-start | bytes 98312 | tf_op jit(solution)/shard_map/ppermute | solution.py:275
  53.0 5.8 %collective-permute-start.4 = (f32[4,16,128]{2,1,0:T(8,128)S(1)}, f32[4,16,128]{2,1,0:T(8,128)S(1)}, u32[]{:S(2)}, u32[]{:S(2)}) collective-permute-start(f32[4,16,128]{2,1,0:T(8,128)S(1)} %get-tuple-element.44), channel_id=1, source_target_pairs={{4,0},{8,4},{12,8},{5,1},{9,5},{13,9},{6,2},{10,6},{14,10},{7,3},{... | collective-permute-start | bytes 98312 | tf_op jit(solution)/shard_map/ppermute | solution.py:276
  58.8 1.1 copy-start.5
  60.0 1.1 copy-start.7
  61.1 20.8 %copy-start.9 = (bf16[768,512]{1,0:T(8,128)(2,1)S(1)}, bf16[768,512]{1,0:T(8,128)(2,1)}, u32[]{:S(2)}) copy-start(bf16[768,512]{1,0:T(8,128)(2,1)} %copy-done.8) | copy-start | bytes 2359300
  61.1 20.8 %copy-start.11 = (bf16[768,512]{1,0:T(8,128)(2,1)S(1)}, bf16[768,512]{1,0:T(8,128)(2,1)}, u32[]{:S(2)}) copy-start(bf16[768,512]{1,0:T(8,128)(2,1)} %copy-done.10) | copy-start | bytes 2359300
  83.9 3.0 %copy-start.3 = (bf16[2,1024,512]{2,1,0:T(8,128)(2,1)S(1)}, bf16[2,1024,512]{2,1,0:T(8,128)(2,1)}, u32[]{:S(2)}) copy-start(bf16[2,1024,512]{2,1,0:T(8,128)(2,1)} %proj_ref.1) | copy-start | bytes 6291460
  84.0 13.2 %collective-permute-start.14 = (f32[512,512]{1,0:T(8,128)S(1)}, f32[512,512]{1,0:T(8,128)S(1)}, u32[]{:S(2)}, u32[]{:S(2)}) collective-permute-start(f32[512,512]{1,0:T(8,128)S(1)} %constant_dynamic-slice_fusion), channel_id=1, source_target_pairs={{0,1},{1,0},{2,3},{3,2},{4,5},{5,4},{6,7},{7,6},{8,9},{9,8},{10,11... | collective-permute-start | bytes 3145736 | tf_op jit(solution)/shard_map/ppermute | solution.py:177
  84.2 2.6 %collective-permute-start.20 = (f32[17,512]{1,0:T(8,128)S(1)}, f32[17,512]{1,0:T(8,128)S(1)}, u32[]{:S(2)}, u32[]{:S(2)}) collective-permute-start(f32[17,512]{1,0:T(8,128)S(1)} %pad_maximum_fusion.5), channel_id=1, source_target_pairs={{0,1},{1,0},{2,3},{3,2},{4,5},{5,4},{6,7},{7,6},{8,9},{9,8},{10,11... | collective-permute-start | bytes 104456 | tf_op jit(solution)/shard_map/ppermute | solution.py:161
  84.8 12.8 %collective-permute-start.8 = (f32[512,512]{1,0:T(8,128)S(1)}, f32[512,512]{1,0:T(8,128)S(1)}, u32[]{:S(2)}, u32[]{:S(2)}) collective-permute-start(f32[512,512]{1,0:T(8,128)S(1)} %constant_dynamic-slice_fusion.1), channel_id=1, source_target_pairs={{0,1},{1,0},{2,3},{3,2},{4,5},{5,4},{6,7},{7,6},{8,9},{9,8},{10,11... | collective-permute-start | bytes 3145736 | tf_op jit(solution)/shard_map/ppermute | solution.py:177
  86.8 4.2 %collective-permute-start.21 = (f32[17,512]{1,0:T(8,128)S(1)}, f32[17,512]{1,0:T(8,128)S(1)}, u32[]{:S(2)}, u32[]{:S(2)}) collective-permute-start(f32[17,512]{1,0:T(8,128)S(1)} %fusion.29), channel_id=1, source_target_pairs={{0,4},{4,0},{8,12},{12,8},{1,5},{5,1},{9,13},{13,9},{2,6},{6,2},{1... | collective-permute-start | bytes 104456 | tf_op jit(solution)/shard_map/ppermute | solution.py:161
  91.0 5.1 %collective-permute-start.22 = (f32[17,512]{1,0:T(8,128)S(1)}, f32[17,512]{1,0:T(8,128)S(1)}, u32[]{:S(2)}, u32[]{:S(2)}) collective-permute-start(f32[17,512]{1,0:T(8,128)S(1)} %add.179), channel_id=1, source_target_pairs={{0,8},{4,12},{8,0},{12,4},{1,9},{5,13},{9,1},{13,5},{2,10},{6,14},... | collective-permute-start | bytes 104456 | tf_op jit(solution)/shard_map/ppermute | solution.py:161
  91.2 51.2 %collective-permute-start.7 = (bf16[768,512]{1,0:T(8,128)(2,1)S(1)}, bf16[768,512]{1,0:T(8,128)(2,1)S(1)}, u32[]{:S(2)}, u32[]{:S(2)}) collective-permute-start(bf16[768,512]{1,0:T(8,128)(2,1)S(1)} %dynamic-slice_convert_fusion), channel_id=1, source_target_pairs={{0,2},{2,0},{1,3},{3,1},{4,6},{6,4},{5,7},{7,5},{8,10},{10,8},{9,1... | collective-permute-start | bytes 2359304 | tf_op jit(solution)/shard_map/ppermute | solution.py:351
  97.5 10.7 %collective-permute-start.15 = (bf16[256,512]{1,0:T(8,128)(2,1)S(1)}, bf16[256,512]{1,0:T(8,128)(2,1)S(1)}, u32[]{:S(2)}, u32[]{:S(2)}) collective-permute-start(bf16[256,512]{1,0:T(8,128)(2,1)S(1)} %dynamic-slice_convert_fusion.1), channel_id=1, source_target_pairs={{0,4},{4,0},{8,12},{12,8},{1,5},{5,1},{9,13},{13,9},{2,6},{6,2},{1... | collective-permute-start | bytes 786440 | tf_op jit(solution)/shard_map/ppermute | solution.py:177
  97.9 13.3 %collective-permute-start.9 = (bf16[256,512]{1,0:T(8,128)(2,1)S(1)}, bf16[256,512]{1,0:T(8,128)(2,1)S(1)}, u32[]{:S(2)}, u32[]{:S(2)}) collective-permute-start(bf16[256,512]{1,0:T(8,128)(2,1)S(1)} %dynamic-slice_convert_fusion.2), channel_id=1, source_target_pairs={{0,4},{4,0},{8,12},{12,8},{1,5},{5,1},{9,13},{13,9},{2,6},{6,2},{1... | collective-permute-start | bytes 786440 | tf_op jit(solution)/shard_map/ppermute | solution.py:177
  108.4 11.4 %collective-permute-start.16 = (bf16[128,512]{1,0:T(8,128)(2,1)S(1)}, bf16[128,512]{1,0:T(8,128)(2,1)S(1)}, u32[]{:S(2)}, u32[]{:S(2)}) collective-permute-start(bf16[128,512]{1,0:T(8,128)(2,1)S(1)} %dynamic-slice_convert_fusion.3), channel_id=1, source_target_pairs={{0,8},{4,12},{8,0},{12,4},{1,9},{5,13},{9,1},{13,5},{2,10},{6,14},... | collective-permute-start | bytes 393224 | tf_op jit(solution)/shard_map/ppermute | solution.py:177
  111.3 14.1 %collective-permute-start.10 = (bf16[128,512]{1,0:T(8,128)(2,1)S(1)}, bf16[128,512]{1,0:T(8,128)(2,1)S(1)}, u32[]{:S(2)}, u32[]{:S(2)}) collective-permute-start(bf16[128,512]{1,0:T(8,128)(2,1)S(1)} %dynamic-slice_convert_fusion.4), channel_id=1, source_target_pairs={{0,8},{4,12},{8,0},{12,4},{1,9},{5,13},{9,1},{13,5},{2,10},{6,14},... | collective-permute-start | bytes 393224 | tf_op jit(solution)/shard_map/ppermute | solution.py:177
  119.8 9.9 %collective-permute-start.17 = (bf16[128,512]{1,0:T(8,128)(2,1)S(1)}, bf16[128,512]{1,0:T(8,128)(2,1)S(1)}, u32[]{:S(2)}, u32[]{:S(2)}) collective-permute-start(bf16[128,512]{1,0:T(8,128)(2,1)S(1)} %add_convert_fusion.1), channel_id=1, source_target_pairs={{0,8},{4,12},{8,0},{12,4},{1,9},{5,13},{9,1},{13,5},{2,10},{6,14},... | collective-permute-start | bytes 393224 | tf_op jit(solution)/shard_map/ppermute | solution.py:182
  125.5 6.0 %collective-permute-start.11 = (bf16[128,512]{1,0:T(8,128)(2,1)S(1)}, bf16[128,512]{1,0:T(8,128)(2,1)S(1)}, u32[]{:S(2)}, u32[]{:S(2)}) collective-permute-start(bf16[128,512]{1,0:T(8,128)(2,1)S(1)} %add_convert_fusion.2), channel_id=1, source_target_pairs={{0,8},{4,12},{8,0},{12,4},{1,9},{5,13},{9,1},{13,5},{2,10},{6,14},... | collective-permute-start | bytes 393224 | tf_op jit(solution)/shard_map/ppermute | solution.py:182
  129.7 9.3 %collective-permute-start.18 = (bf16[256,512]{1,0:T(8,128)(2,1)S(1)}, bf16[256,512]{1,0:T(8,128)(2,1)S(1)}, u32[]{:S(2)}, u32[]{:S(2)}) collective-permute-start(bf16[256,512]{1,0:T(8,128)(2,1)S(1)} %pad_maximum_fusion.4), channel_id=1, source_target_pairs={{0,4},{4,0},{8,12},{12,8},{1,5},{5,1},{9,13},{13,9},{2,6},{6,2},{1... | collective-permute-start | bytes 786440 | tf_op jit(solution)/shard_map/ppermute | solution.py:182
  131.5 10.7 %collective-permute-start.12 = (bf16[256,512]{1,0:T(8,128)(2,1)S(1)}, bf16[256,512]{1,0:T(8,128)(2,1)S(1)}, u32[]{:S(2)}, u32[]{:S(2)}) collective-permute-start(bf16[256,512]{1,0:T(8,128)(2,1)S(1)} %pad_maximum_fusion.3), channel_id=1, source_target_pairs={{0,4},{4,0},{8,12},{12,8},{1,5},{5,1},{9,13},{13,9},{2,6},{6,2},{1... | collective-permute-start | bytes 786440 | tf_op jit(solution)/shard_map/ppermute | solution.py:182
  139.2 4.4 %collective-permute-start.19 = (bf16[512,512]{1,0:T(8,128)(2,1)S(1)}, bf16[512,512]{1,0:T(8,128)(2,1)S(1)}, u32[]{:S(2)}, u32[]{:S(2)}) collective-permute-start(bf16[512,512]{1,0:T(8,128)(2,1)S(1)} %pad_maximum_fusion.2), channel_id=1, source_target_pairs={{0,1},{1,0},{2,3},{3,2},{4,5},{5,4},{6,7},{7,6},{8,9},{9,8},{10,11... | collective-permute-start | bytes 1572872 | tf_op jit(solution)/shard_map/ppermute | solution.py:182
  142.4 2.0 %collective-permute-start.13 = (bf16[512,512]{1,0:T(8,128)(2,1)S(1)}, bf16[512,512]{1,0:T(8,128)(2,1)S(1)}, u32[]{:S(2)}, u32[]{:S(2)}) collective-permute-start(bf16[512,512]{1,0:T(8,128)(2,1)S(1)} %pad_maximum_fusion.1), channel_id=1, source_target_pairs={{0,1},{1,0},{2,3},{3,2},{4,5},{5,4},{6,7},{7,6},{8,9},{9,8},{10,11... | collective-permute-start | bytes 1572872 | tf_op jit(solution)/shard_map/ppermute | solution.py:182

commit v4 on v3

--- a/solution.py
+++ b/solution.py
@@ -270,24 +270,13 @@
         return own + keep.astype(F32) * turned
 
     entering = leaving = jnp.zeros((heads, 2 * M, 128), F32)
-    if count <= 8:
-        for k in range(count - 1, 0, -1):
-            before = lax.ppermute(ends[:, : 2 * M], "tm", [(i, i + k) for i in range(count - k)])
-            behind = lax.ppermute(ends[:, 2 * M :], "tm", [(i + k, i) for i in range(count - k)])
-            d = mine - k
-            entering = join(
-                entering, before, segment_at(d * rows - 1) == segment_at(d * rows + rows - 1)
-            )
-            d = mine + k
-            leaving = join(leaving, behind, segment_at(d * rows) == segment_at(d * rows + rows))
-    else:
-        gathered = lax.all_gather(ends, "tm")
-        for d in range(count - 1):
-            keep = segment_at(d * rows - 1) == segment_at(d * rows + rows - 1)
-            entering = jnp.where(d < mine, join(entering, gathered[d, :, : 2 * M], keep), entering)
-        for d in range(count - 1, 0, -1):
-            keep = segment_at(d * rows) == segment_at(d * rows + rows)
-            leaving = jnp.where(d > mine, join(leaving, gathered[d, :, 2 * M :], keep), leaving)
+    gathered = lax.all_gather(ends, "tm")
+    for d in range(count - 1):
+        keep = segment_at(d * rows - 1) == segment_at(d * rows + rows - 1)
+        entering = jnp.where(d < mine, join(entering, gathered[d, :, : 2 * M], keep), entering)
+    for d in range(count - 1, 0, -1):
+        keep = segment_at(d * rows) == segment_at(d * rows + rows)
+        leaving = jnp.where(d > mine, join(leaving, gathered[d, :, 2 * M :], keep), leaving)
 
     per_head = lambda i, s: (i, 0, 0)
     column = lambda i, s: (0, i)

time: 148 us -> 128 us (0.86)
  waiting for transfers between devices: 64.3 us -> 37.6 us
  blocking collectives: 0 us -> 14.4 us
  starting transfers between devices: 25.8 us -> 22 us
  local copies, waits for them, and re-layouts: 7.83 us -> 4.08 us
    ppermute x6 -> x0, starting transfers between devices: 17 us -> none  [the longest x3 13.1 us: shards(): lax.ppermute(ends[:, :2 * M], 'tm', [(i, i + k) for i in range(count - k)])]
    all_gather x0 -> x1, blocking collectives: none -> 14.4 us  [shards(): gathered = lax.all_gather(ends, 'tm')]
    ppermute x1, waiting for transfers between devices: 11.8 us -> 3.59 us  [widened(): lax.ppermute(value, axis, [(i, (i + k) % size) for i in range(size)])]
    ppermute x6, waiting for transfers between devices: 24.8 us -> 18 us  [summed_matrix(): value = kept + lax.ppermute(away, axis, pairs).astype(F32)]
    ppermute x6, starting transfers between devices: 0.81 us -> 6.61 us  [summed_matrix(): other = lax.ppermute(value, axis, pairs)]
    ppermute x6, waiting for transfers between devices: 16.3 us -> 11.7 us  [summed_matrix(): other = lax.ppermute(value, axis, pairs)]
    ppermute x6, starting transfers between devices: 2.59 us -> 6.84 us  [summed_matrix(): value = kept + lax.ppermute(away, axis, pairs).astype(F32)]
    ppermute x6 -> x0, waiting for transfers between devices: 4.11 us -> none  [the longest x3 4.1 us: shards(): lax.ppermute(ends[:, 2 * M:], 'tm', [(i + k, i) for i in range(count - k)])]
  transfers between devices with their start and end apart: 23 -> 17, of which waited for: 14 -> 12; matrix products, arithmetic and copies ran while one was open for 9% -> 10% of each run, Pallas kernels for 0% -> 0%
where the time goes in v4:
time: 128 us; the launch traced here: 127 us
  waiting for transfers between devices  37.6 us (29%)
  Pallas kernels  24 us (19%)
  starting transfers between devices  22 us (17%)
  blocking collectives  14.4 us (11%)
  other arithmetic  12.7 us (10%)
  between operations  8.81 us (7%)
  local copies, waits for them, and re-layouts  4.08 us (3%)
  matrix products  3.83 us (3%)
    pallas_call x1, Pallas kernels, shards(): pl.pallas_call(functools.partial(conv_kernel, clips, M), grid_spec=pltpu....  20.8 us
    ppermute x6, waiting for transfers between devices, summed_matrix(): value = kept + lax.ppermute(away, axis, pairs).astype(F32)  18 us
    all_gather x1, blocking collectives, shards(): gathered = lax.all_gather(ends, 'tm')  14.4 us
    ppermute x6, waiting for transfers between devices, summed_matrix(): other = lax.ppermute(value, axis, pairs)  11.7 us
    ppermute x6, starting transfers between devices, summed_matrix(): value = kept + lax.ppermute(away, axis, pairs).astype(F32)  6.84 us
    ppermute x6, starting transfers between devices, summed_matrix(): other = lax.ppermute(value, axis, pairs)  6.61 us
    ppermute x3, waiting for transfers between devices, summed_over(): lax.ppermute(value, axis, [(i, i ^ stride) for i in range(size)])  4.19 us
    ppermute x3, starting transfers between devices, summed_over(): lax.ppermute(value, axis, [(i, i ^ stride) for i in range(size)])  4.03 us
  transfers between devices with their start and end apart: 17, of which 12 were waited for; matrix products, arithmetic and copies ran while one was open for 10% of the time, Pallas kernels for 0%

profile of v4, /device:TPU:0, one launch (start us, length us, event | category | flops | bytes accessed | tf_op | source)
XLA Modules:
  0.0 127.4 jit_solution(5786639542784225413)
XLA Ops:
  0.7 3.0 %collective-permute-start = (bf16[768,512]{1,0:T(8,128)(2,1)}, bf16[768,512]{1,0:T(8,128)(2,1)}, u32[]{:S(2)}, u32[]{:S(2)}) collective-permute-start(bf16[768,512]{1,0:T(8,128)(2,1)} %bitcast.109), channel_id=1, source_target_pairs={{0,2},{2,0},{1,3},{3,1},{4,6},{6,4},{5,7},{7,5},{8,10},{10,8},{9,1... | collective-permute-start | bytes 2359304 | tf_op jit(solution)/shard_map/ppermute | solution.py:192
  3.7 0.7 sqrt_bitcast_fusion
  4.4 1.7 %fusion.6 = (f32[4,8,2048]{2,1,0:T(8,128)S(1)}, f32[4,8,2048]{2,1,0:T(8,128)S(1)}) fusion(f32[4,8]{1,0:T(4,128)} %bitcast.110, f32[2048]{0:T(1024)S(1)} %convert_element_type.108, f32[4,8]{1,0:T(4,128)S(1)} %get-tuple-element.59), kind=kLoop, calls=%fused_computation.29 | loop fusion | flops 262144 | bytes 532736 | tf_op jit(solution)/shard_map/mul | solution.py:222
  6.2 0.1 slice_reduce_fusion
  6.3 0.7 broadcast_multiply_fusion
  7.0 0.8 reduce-window.9
  7.8 1.5 %fusion.27 = (s32[]{:T(128)}, s32[]{:T(128)}, s32[]{:T(128)}, s32[]{:T(128)}, s32[]{:T(128)}, /*index=5*/s32[]{:T(128)}, s32[]{:T(128)}, s32[]{:T(128)}, s32[4]{0:T(128)S(1)}) fusion(s32[1,4]{1,0:T(1,128)} %param.14, s32[4,1]{0,1:T(1,128)S(1)} %reduce-window.9), kind=kLoop, calls=%fused_computation.116 | loop fusion | flops 92 | bytes 80 | tf_op jit(solution)/shard_map/reduce_sum | solution.py:265
  9.3 0.3 copy.21.cre_ref
  9.6 0.3 copy.22.cim_ref
  17.6 0.1 pad.28.clone
  17.7 0.1 pad_add_fusion.starts_ref
  17.8 0.1 fusion.21
  17.9 3.6 %collective-permute-done = bf16[768,512]{1,0:T(8,128)(2,1)} collective-permute-done((bf16[768,512]{1,0:T(8,128)(2,1)}, bf16[768,512]{1,0:T(8,128)(2,1)}, u32[]{:S(2)}, u32[]{:S(2)}) %collective-permute-start) | collective-permute-done | bytes 786464 | tf_op jit(solution)/shard_map/ppermute | solution.py:192
  21.5 1.2 broadcast_select_fusion.1
  22.8 0.2 pad_maximum_fusion.feat_ref
  23.0 0.9 copy-done.1
  23.9 0.7 copy-done.2
  24.6 3.2 %project.1 = (bf16[768,512]{1,0:T(8,128)(2,1)S(1)}, bf16[768,512]{1,0:T(8,128)(2,1)S(1)}, f32[4,32,128]{2,1,0:T(8,128)S(1)}) custom-call(s32[5]{0:T(128)S(1)} %pad_add_fusion.starts_ref, bf16[768,1024]{1,0:T(8,128)(2,1)S(1)} %pad_maximum_fusion.feat_ref, bf16[2,1024,512]{2,1,0:T(8,128)(2,1)S(1)} %copy-done.2, bf16[768,512]{1,0:T(8,128)(2,1)S(1)} %bitcast.103, ...), custom_call_target="tpu_custom_call" | custom-call | tf_op jit(solution)/shard_map/project/pallas_call | solution.py:235
  27.8 14.4 %all-gather = f32[16,32,128]{2,1,0:T(8,128)S(1)} all-gather(f32[4,32,128]{2,1,0:T(8,128)S(1)} %get-tuple-element.11), channel_id=2, replica_groups=mesh['group'=2,'tm'=4,'tensor'=2,'dp'=2] {'tm'}, dimensions={0}, use_global_device_ids=true | all-gather | bytes 327680 | tf_op jit(solution)/shard_map/all_gather | solution.py:273
  42.4 0.1 multiply_subtract_fusion.1
  42.5 0.1 multiply_subtract_fusion
  42.6 0.1 multiply_subtract_fusion.2
  42.7 20.8 %conv.1 = (bf16[768,512]{1,0:T(8,128)(2,1)}, bf16[2,768,512]{2,1,0:T(8,128)(2,1)S(1)}, f32[4,24,128]{2,1,0:T(8,128)S(1)}) custom-call(s32[5]{0:T(128)S(1)} %pad_add_fusion.starts_ref, f32[4,384,8]{2,1,0:T(8,128)S(1)} %copy.21.cre_ref, f32[4,384,8]{2,1,0:T(8,128)S(1)} %copy.22.cim_ref, f32[4,8,2048]{2,1,0:T(8,128)S(1)} %get-tuple-element.53.tre_ref, ...), custom_call_target="tpu_custom_call" | custom-call | tf_op jit(solution)/shard_map/conv/pallas_call | solution.py:283
  63.5 1.0 convolution_multiply_fusion
  64.5 1.0 convolution_multiply_fusion.1
  65.5 0.1 constant_dynamic-slice_fusion
  65.7 0.1 fusion.22
  65.8 0.6 collective-permute-start.14
  66.4 0.1 collective-permute-start.2
  66.5 1.9 %collective-permute-done.14 = f32[17,512]{1,0:T(8,128)S(1)} collective-permute-done((f32[17,512]{1,0:T(8,128)S(1)}, f32[17,512]{1,0:T(8,128)S(1)}, u32[]{:S(2)}, u32[]{:S(2)}) %collective-permute-start.14) | collective-permute-done | bytes 34848 | tf_op jit(solution)/shard_map/ppermute | solution.py:161
  68.4 1.5 %collective-permute-start.15 = (f32[17,512]{1,0:T(8,128)S(1)}, f32[17,512]{1,0:T(8,128)S(1)}, u32[]{:S(2)}, u32[]{:S(2)}) collective-permute-start(f32[17,512]{1,0:T(8,128)S(1)} %fusion.31), channel_id=1, source_target_pairs={{0,4},{4,0},{8,12},{12,8},{1,5},{5,1},{9,13},{13,9},{2,6},{6,2},{1... | collective-permute-start | bytes 104456 | tf_op jit(solution)/shard_map/ppermute | solution.py:161
  69.9 1.8 %convolution_bitcast_fusion = f32[768,1024]{1,0:T(8,128)S(1)} fusion(bf16[2,768,512]{2,1,0:T(8,128)(2,1)S(1)} %get-tuple-element.15, bf16[2,1024,512]{2,1,0:T(8,128)(2,1)S(1)} %copy-done.2), kind=kOutput, calls=%fused_computation.1 | convolution fusion | flops 1610612736 | bytes 6815744 | tf_op jit(solution)/shard_map/klc,kdc->ld/dot_general | solution.py:328
  71.8 0.8 collective-permute-done.15
  72.6 2.0 %collective-permute-start.16 = (f32[17,512]{1,0:T(8,128)S(1)}, f32[17,512]{1,0:T(8,128)S(1)}, u32[]{:S(2)}, u32[]{:S(2)}) collective-permute-start(f32[17,512]{1,0:T(8,128)S(1)} %add.137), channel_id=1, source_target_pairs={{0,8},{4,12},{8,0},{12,4},{1,9},{5,13},{9,1},{13,5},{2,10},{6,14},... | collective-permute-start | bytes 104456 | tf_op jit(solution)/shard_map/ppermute | solution.py:161
  74.5 0.1 dynamic-slice_convert_fusion
  74.6 1.5 %collective-permute-start.1 = (bf16[768,512]{1,0:T(8,128)(2,1)S(1)}, bf16[768,512]{1,0:T(8,128)(2,1)S(1)}, u32[]{:S(2)}, u32[]{:S(2)}) collective-permute-start(bf16[768,512]{1,0:T(8,128)(2,1)S(1)} %dynamic-slice_convert_fusion), channel_id=1, source_target_pairs={{0,2},{2,0},{1,3},{3,1},{4,6},{6,4},{5,7},{7,5},{8,10},{10,8},{9,1... | collective-permute-start | bytes 2359304 | tf_op jit(solution)/shard_map/ppermute | solution.py:340
  76.2 1.5 %collective-permute-done.16 = f32[17,512]{1,0:T(8,128)S(1)} collective-permute-done((f32[17,512]{1,0:T(8,128)S(1)}, f32[17,512]{1,0:T(8,128)S(1)}, u32[]{:S(2)}, u32[]{:S(2)}) %collective-permute-start.16) | collective-permute-done | bytes 34848 | tf_op jit(solution)/shard_map/ppermute | solution.py:161
  77.6 0.6 slice.115
  78.2 0.6 slice_bitcast_fusion.2
  78.8 0.2 dynamic-slice_add_fusion
  79.1 1.5 %collective-permute-start.9 = (bf16[256,512]{1,0:T(8,128)(2,1)S(1)}, bf16[256,512]{1,0:T(8,128)(2,1)S(1)}, u32[]{:S(2)}, u32[]{:S(2)}) collective-permute-start(bf16[256,512]{1,0:T(8,128)(2,1)S(1)} %dynamic-slice_convert_fusion.1), channel_id=1, source_target_pairs={{0,4},{4,0},{8,12},{12,8},{1,5},{5,1},{9,13},{13,9},{2,6},{6,2},{1... | collective-permute-start | bytes 786440 | tf_op jit(solution)/shard_map/ppermute | solution.py:177
  80.6 0.2 dynamic-slice_add_fusion.1
  80.9 0.6 collective-permute-start.3
  81.5 8.0 %collective-permute-done.9 = bf16[256,512]{1,0:T(8,128)(2,1)S(1)} collective-permute-done((bf16[256,512]{1,0:T(8,128)(2,1)S(1)}, bf16[256,512]{1,0:T(8,128)(2,1)S(1)}, u32[]{:S(2)}, u32[]{:S(2)}) %collective-permute-start.9) | collective-permute-done | bytes 262176 | tf_op jit(solution)/shard_map/ppermute | solution.py:177
  89.5 0.1 convert_add_fusion
  89.6 1.8 %collective-permute-start.10 = (bf16[128,512]{1,0:T(8,128)(2,1)S(1)}, bf16[128,512]{1,0:T(8,128)(2,1)S(1)}, u32[]{:S(2)}, u32[]{:S(2)}) collective-permute-start(bf16[128,512]{1,0:T(8,128)(2,1)S(1)} %dynamic-slice_convert_fusion.3), channel_id=1, source_target_pairs={{0,8},{4,12},{8,0},{12,4},{1,9},{5,13},{9,1},{13,5},{2,10},{6,14},... | collective-permute-start | bytes 393224 | tf_op jit(solution)/shard_map/ppermute | solution.py:177
  91.5 0.9 collective-permute-done.3
  92.3 0.1 convert_add_fusion.1
  92.4 2.7 %collective-permute-start.4 = (bf16[128,512]{1,0:T(8,128)(2,1)S(1)}, bf16[128,512]{1,0:T(8,128)(2,1)S(1)}, u32[]{:S(2)}, u32[]{:S(2)}) collective-permute-start(bf16[128,512]{1,0:T(8,128)(2,1)S(1)} %dynamic-slice_convert_fusion.4), channel_id=1, source_target_pairs={{0,8},{4,12},{8,0},{12,4},{1,9},{5,13},{9,1},{13,5},{2,10},{6,14},... | collective-permute-start | bytes 393224 | tf_op jit(solution)/shard_map/ppermute | solution.py:177
  95.1 7.5 %collective-permute-done.10 = bf16[128,512]{1,0:T(8,128)(2,1)S(1)} collective-permute-done((bf16[128,512]{1,0:T(8,128)(2,1)S(1)}, bf16[128,512]{1,0:T(8,128)(2,1)S(1)}, u32[]{:S(2)}, u32[]{:S(2)}) %collective-permute-start.10) | collective-permute-done | bytes 131104 | tf_op jit(solution)/shard_map/ppermute | solution.py:177
  102.7 1.7 %collective-permute-done.4 = bf16[128,512]{1,0:T(8,128)(2,1)S(1)} collective-permute-done((bf16[128,512]{1,0:T(8,128)(2,1)S(1)}, bf16[128,512]{1,0:T(8,128)(2,1)S(1)}, u32[]{:S(2)}, u32[]{:S(2)}) %collective-permute-start.4) | collective-permute-done | bytes 131104 | tf_op jit(solution)/shard_map/ppermute | solution.py:177
  104.5 1.3 collective-permute-start.5
  105.7 4.4 %collective-permute-done.11 = bf16[128,512]{1,0:T(8,128)(2,1)S(1)} collective-permute-done((bf16[128,512]{1,0:T(8,128)(2,1)S(1)}, bf16[128,512]{1,0:T(8,128)(2,1)S(1)}, u32[]{:S(2)}, u32[]{:S(2)}) %collective-permute-start.11) | collective-permute-done | bytes 131104 | tf_op jit(solution)/shard_map/ppermute | solution.py:182
  110.2 1.6 %collective-permute-start.12 = (bf16[256,512]{1,0:T(8,128)(2,1)S(1)}, bf16[256,512]{1,0:T(8,128)(2,1)S(1)}, u32[]{:S(2)}, u32[]{:S(2)}) collective-permute-start(bf16[256,512]{1,0:T(8,128)(2,1)S(1)} %pad_maximum_fusion.4), channel_id=1, source_target_pairs={{0,4},{4,0},{8,12},{12,8},{1,5},{5,1},{9,13},{13,9},{2,6},{6,2},{1... | collective-permute-start | bytes 786440 | tf_op jit(solution)/shard_map/ppermute | solution.py:182
  111.9 3.5 %collective-permute-start.6 = (bf16[256,512]{1,0:T(8,128)(2,1)S(1)}, bf16[256,512]{1,0:T(8,128)(2,1)S(1)}, u32[]{:S(2)}, u32[]{:S(2)}) collective-permute-start(bf16[256,512]{1,0:T(8,128)(2,1)S(1)} %pad_maximum_fusion.3), channel_id=1, source_target_pairs={{0,4},{4,0},{8,12},{12,8},{1,5},{5,1},{9,13},{13,9},{2,6},{6,2},{1... | collective-permute-start | bytes 786440 | tf_op jit(solution)/shard_map/ppermute | solution.py:182
  115.4 4.1 %collective-permute-done.12 = bf16[256,512]{1,0:T(8,128)(2,1)S(1)} collective-permute-done((bf16[256,512]{1,0:T(8,128)(2,1)S(1)}, bf16[256,512]{1,0:T(8,128)(2,1)S(1)}, u32[]{:S(2)}, u32[]{:S(2)}) %collective-permute-start.12) | collective-permute-done | bytes 262176 | tf_op jit(solution)/shard_map/ppermute | solution.py:182
  119.5 0.1 broadcast_select_fusion.3
  119.7 2.7 %collective-permute-done.6 = bf16[256,512]{1,0:T(8,128)(2,1)S(1)} collective-permute-done((bf16[256,512]{1,0:T(8,128)(2,1)S(1)}, bf16[256,512]{1,0:T(8,128)(2,1)S(1)}, u32[]{:S(2)}, u32[]{:S(2)}) %collective-permute-start.6) | collective-permute-done | bytes 262176 | tf_op jit(solution)/shard_map/ppermute | solution.py:182
  122.4 0.1 broadcast_select_fusion.5
  122.7 1.2 fusion
  123.8 0.2 select_bitcast_fusion.1
  124.0 0.5 collective-permute-done.7
  124.6 0.2 select_bitcast_fusion.3
  124.8 2.6 %maximum_convert_fusion = f32[2,1024,512]{2,1,0:T(8,128)} fusion(bf16[1,512,512]{2,1,0:T(8,128)(2,1)S(1)} %get-tuple-element.31, bf16[1,512,512]{2,1,0:T(8,128)(2,1)S(1)} %get-tuple-element.30, bf16[1,512,512]{2,1,0:T(8,128)(2,1)S(1)} %get-tuple-element.29, bf16[1,512,512]{2,1,0:T(8,128)(2,1)S(1)} %get-tuple-element.28), kind=kLoop, calls=%fused_computation | loop fusion | flops 8388608 | bytes 6291456 | tf_op jit(solution)/shard_map/stack | solution.py:330
  (53 shorter events, 1.1 us)
Async XLA Ops:
  0.6 17.2 %copy-start = (f32[2,8,512]{2,1,0:T(8,128)S(1)}, f32[2,8,512]{2,1,0:T(8,128)}, u32[]{:S(2)}) copy-start(f32[2,8,512]{2,1,0:T(8,128)} %param.12) | copy-start | bytes 98308
  0.6 20.9 %copy-start.3 = (bf16[1,768,512]{2,1,0:T(8,128)(2,1)S(1)}, bf16[1,768,512]{2,1,0:T(8,128)(2,1)}, u32[]{:S(2)}) copy-start(bf16[1,768,512]{2,1,0:T(8,128)(2,1)} %param.8) | copy-start | bytes 2359300
  0.7 17.2 %copy-start.4 = (f32[512]{0:T(512)S(1)}, f32[512]{0:T(512)}, u32[]{:S(2)}) copy-start(f32[512]{0:T(512)} %param.13) | copy-start | bytes 6148
  0.7 20.9 %collective-permute-start = (bf16[768,512]{1,0:T(8,128)(2,1)}, bf16[768,512]{1,0:T(8,128)(2,1)}, u32[]{:S(2)}, u32[]{:S(2)}) collective-permute-start(bf16[768,512]{1,0:T(8,128)(2,1)} %bitcast.109), channel_id=1, source_target_pairs={{0,2},{2,0},{1,3},{3,1},{4,6},{6,4},{5,7},{7,5},{8,10},{10,8},{9,1... | collective-permute-start | bytes 2359304 | tf_op jit(solution)/shard_map/ppermute | solution.py:192
  22.8 1.1 copy-start.1
  22.8 1.8 %copy-start.2 = (bf16[2,1024,512]{2,1,0:T(8,128)(2,1)S(1)}, bf16[2,1024,512]{2,1,0:T(8,128)(2,1)}, u32[]{:S(2)}) copy-start(bf16[2,1024,512]{2,1,0:T(8,128)(2,1)} %proj_ref.1) | copy-start | bytes 6291460
  65.6 13.2 %collective-permute-start.8 = (f32[512,512]{1,0:T(8,128)S(1)}, f32[512,512]{1,0:T(8,128)S(1)}, u32[]{:S(2)}, u32[]{:S(2)}) collective-permute-start(f32[512,512]{1,0:T(8,128)S(1)} %constant_dynamic-slice_fusion), channel_id=1, source_target_pairs={{0,1},{1,0},{2,3},{3,2},{4,5},{5,4},{6,7},{7,6},{8,9},{9,8},{10,11... | collective-permute-start | bytes 3145736 | tf_op jit(solution)/shard_map/ppermute | solution.py:177
  65.8 2.6 %collective-permute-start.14 = (f32[17,512]{1,0:T(8,128)S(1)}, f32[17,512]{1,0:T(8,128)S(1)}, u32[]{:S(2)}, u32[]{:S(2)}) collective-permute-start(f32[17,512]{1,0:T(8,128)S(1)} %pad_maximum_fusion.5), channel_id=1, source_target_pairs={{0,1},{1,0},{2,3},{3,2},{4,5},{5,4},{6,7},{7,6},{8,9},{9,8},{10,11... | collective-permute-start | bytes 104456 | tf_op jit(solution)/shard_map/ppermute | solution.py:161
  66.4 14.2 %collective-permute-start.2 = (f32[512,512]{1,0:T(8,128)S(1)}, f32[512,512]{1,0:T(8,128)S(1)}, u32[]{:S(2)}, u32[]{:S(2)}) collective-permute-start(f32[512,512]{1,0:T(8,128)S(1)} %constant_dynamic-slice_fusion.1), channel_id=1, source_target_pairs={{0,1},{1,0},{2,3},{3,2},{4,5},{5,4},{6,7},{7,6},{8,9},{9,8},{10,11... | collective-permute-start | bytes 3145736 | tf_op jit(solution)/shard_map/ppermute | solution.py:177
  68.4 4.2 %collective-permute-start.15 = (f32[17,512]{1,0:T(8,128)S(1)}, f32[17,512]{1,0:T(8,128)S(1)}, u32[]{:S(2)}, u32[]{:S(2)}) collective-permute-start(f32[17,512]{1,0:T(8,128)S(1)} %fusion.31), channel_id=1, source_target_pairs={{0,4},{4,0},{8,12},{12,8},{1,5},{5,1},{9,13},{13,9},{2,6},{6,2},{1... | collective-permute-start | bytes 104456 | tf_op jit(solution)/shard_map/ppermute | solution.py:161
  72.6 5.1 %collective-permute-start.16 = (f32[17,512]{1,0:T(8,128)S(1)}, f32[17,512]{1,0:T(8,128)S(1)}, u32[]{:S(2)}, u32[]{:S(2)}) collective-permute-start(f32[17,512]{1,0:T(8,128)S(1)} %add.137), channel_id=1, source_target_pairs={{0,8},{4,12},{8,0},{12,4},{1,9},{5,13},{9,1},{13,5},{2,10},{6,14},... | collective-permute-start | bytes 104456 | tf_op jit(solution)/shard_map/ppermute | solution.py:161
  74.6 48.0 %collective-permute-start.1 = (bf16[768,512]{1,0:T(8,128)(2,1)S(1)}, bf16[768,512]{1,0:T(8,128)(2,1)S(1)}, u32[]{:S(2)}, u32[]{:S(2)}) collective-permute-start(bf16[768,512]{1,0:T(8,128)(2,1)S(1)} %dynamic-slice_convert_fusion), channel_id=1, source_target_pairs={{0,2},{2,0},{1,3},{3,1},{4,6},{6,4},{5,7},{7,5},{8,10},{10,8},{9,1... | collective-permute-start | bytes 2359304 | tf_op jit(solution)/shard_map/ppermute | solution.py:340
  79.1 10.4 %collective-permute-start.9 = (bf16[256,512]{1,0:T(8,128)(2,1)S(1)}, bf16[256,512]{1,0:T(8,128)(2,1)S(1)}, u32[]{:S(2)}, u32[]{:S(2)}) collective-permute-start(bf16[256,512]{1,0:T(8,128)(2,1)S(1)} %dynamic-slice_convert_fusion.1), channel_id=1, source_target_pairs={{0,4},{4,0},{8,12},{12,8},{1,5},{5,1},{9,13},{13,9},{2,6},{6,2},{1... | collective-permute-start | bytes 786440 | tf_op jit(solution)/shard_map/ppermute | solution.py:177
  80.9 11.4 %collective-permute-start.3 = (bf16[256,512]{1,0:T(8,128)(2,1)S(1)}, bf16[256,512]{1,0:T(8,128)(2,1)S(1)}, u32[]{:S(2)}, u32[]{:S(2)}) collective-permute-start(bf16[256,512]{1,0:T(8,128)(2,1)S(1)} %dynamic-slice_convert_fusion.2), channel_id=1, source_target_pairs={{0,4},{4,0},{8,12},{12,8},{1,5},{5,1},{9,13},{13,9},{2,6},{6,2},{1... | collective-permute-start | bytes 786440 | tf_op jit(solution)/shard_map/ppermute | solution.py:177
  89.6 13.0 %collective-permute-start.10 = (bf16[128,512]{1,0:T(8,128)(2,1)S(1)}, bf16[128,512]{1,0:T(8,128)(2,1)S(1)}, u32[]{:S(2)}, u32[]{:S(2)}) collective-permute-start(bf16[128,512]{1,0:T(8,128)(2,1)S(1)} %dynamic-slice_convert_fusion.3), channel_id=1, source_target_pairs={{0,8},{4,12},{8,0},{12,4},{1,9},{5,13},{9,1},{13,5},{2,10},{6,14},... | collective-permute-start | bytes 393224 | tf_op jit(solution)/shard_map/ppermute | solution.py:177
  92.4 12.0 %collective-permute-start.4 = (bf16[128,512]{1,0:T(8,128)(2,1)S(1)}, bf16[128,512]{1,0:T(8,128)(2,1)S(1)}, u32[]{:S(2)}, u32[]{:S(2)}) collective-permute-start(bf16[128,512]{1,0:T(8,128)(2,1)S(1)} %dynamic-slice_convert_fusion.4), channel_id=1, source_target_pairs={{0,8},{4,12},{8,0},{12,4},{1,9},{5,13},{9,1},{13,5},{2,10},{6,14},... | collective-permute-start | bytes 393224 | tf_op jit(solution)/shard_map/ppermute | solution.py:177
  102.6 7.5 %collective-permute-start.11 = (bf16[128,512]{1,0:T(8,128)(2,1)S(1)}, bf16[128,512]{1,0:T(8,128)(2,1)S(1)}, u32[]{:S(2)}, u32[]{:S(2)}) collective-permute-start(bf16[128,512]{1,0:T(8,128)(2,1)S(1)} %add_convert_fusion.1), channel_id=1, source_target_pairs={{0,8},{4,12},{8,0},{12,4},{1,9},{5,13},{9,1},{13,5},{2,10},{6,14},... | collective-permute-start | bytes 393224 | tf_op jit(solution)/shard_map/ppermute | solution.py:182
  104.5 7.4 %collective-permute-start.5 = (bf16[128,512]{1,0:T(8,128)(2,1)S(1)}, bf16[128,512]{1,0:T(8,128)(2,1)S(1)}, u32[]{:S(2)}, u32[]{:S(2)}) collective-permute-start(bf16[128,512]{1,0:T(8,128)(2,1)S(1)} %add_convert_fusion.2), channel_id=1, source_target_pairs={{0,8},{4,12},{8,0},{12,4},{1,9},{5,13},{9,1},{13,5},{2,10},{6,14},... | collective-permute-start | bytes 393224 | tf_op jit(solution)/shard_map/ppermute | solution.py:182
  110.2 9.3 %collective-permute-start.12 = (bf16[256,512]{1,0:T(8,128)(2,1)S(1)}, bf16[256,512]{1,0:T(8,128)(2,1)S(1)}, u32[]{:S(2)}, u32[]{:S(2)}) collective-permute-start(bf16[256,512]{1,0:T(8,128)(2,1)S(1)} %pad_maximum_fusion.4), channel_id=1, source_target_pairs={{0,4},{4,0},{8,12},{12,8},{1,5},{5,1},{9,13},{13,9},{2,6},{6,2},{1... | collective-permute-start | bytes 786440 | tf_op jit(solution)/shard_map/ppermute | solution.py:182
  111.9 10.6 %collective-permute-start.6 = (bf16[256,512]{1,0:T(8,128)(2,1)S(1)}, bf16[256,512]{1,0:T(8,128)(2,1)S(1)}, u32[]{:S(2)}, u32[]{:S(2)}) collective-permute-start(bf16[256,512]{1,0:T(8,128)(2,1)S(1)} %pad_maximum_fusion.3), channel_id=1, source_target_pairs={{0,4},{4,0},{8,12},{12,8},{1,5},{5,1},{9,13},{13,9},{2,6},{6,2},{1... | collective-permute-start | bytes 786440 | tf_op jit(solution)/shard_map/ppermute | solution.py:182
  119.6 4.2 %collective-permute-start.13 = (bf16[512,512]{1,0:T(8,128)(2,1)S(1)}, bf16[512,512]{1,0:T(8,128)(2,1)S(1)}, u32[]{:S(2)}, u32[]{:S(2)}) collective-permute-start(bf16[512,512]{1,0:T(8,128)(2,1)S(1)} %pad_maximum_fusion.2), channel_id=1, source_target_pairs={{0,1},{1,0},{2,3},{3,2},{4,5},{5,4},{6,7},{7,6},{8,9},{9,8},{10,11... | collective-permute-start | bytes 1572872 | tf_op jit(solution)/shard_map/ppermute | solution.py:182
  122.6 2.0 %collective-permute-start.7 = (bf16[512,512]{1,0:T(8,128)(2,1)S(1)}, bf16[512,512]{1,0:T(8,128)(2,1)S(1)}, u32[]{:S(2)}, u32[]{:S(2)}) collective-permute-start(bf16[512,512]{1,0:T(8,128)(2,1)S(1)} %pad_maximum_fusion.1), channel_id=1, source_target_pairs={{0,1},{1,0},{2,3},{3,2},{4,5},{5,4},{6,7},{7,6},{8,9},{9,8},{10,11... | collective-permute-start | bytes 1572872 | tf_op jit(solution)/shard_map/ppermute | solution.py:182

commit v5 on v4

--- a/solution.py
+++ b/solution.py
@@ -46,9 +46,9 @@
         ends_ref[h, 2 * modes :, :] = dot(bwd, grad[:, cols])
 
 
-def conv_kernel(
-    clips, modes, starts_ref, cre_ref, cim_ref, tre_ref, tim_ref, w_ref, u_ref, g_ref, q_ref, x_ref, up_ref,
-    mixed_ref, stack_ref, sums_ref, kf, kb, tx,
+def forward_kernel(
+    clips, modes, starts_ref, cre_ref, cim_ref, tre_ref, tim_ref, w_ref, u_ref, q_ref, x_ref, up_ref,
+    mixed_ref, grad_ref, tx, kf,
 ):
     rows = q_ref.shape[0]
     blocks = rows // BLOCK_LEN
@@ -63,10 +63,6 @@
         fr, fi = tre_ref[0, m : m + 1, L + 128 : L + 256], tim_ref[0, m : m + 1, L + 128 : L + 256]
         kf[:, re * 128 : re * 128 + 128] = jnp.where(i0 >= i1, er * fr - ei * fi, 0.0).astype(BF16)
         kf[:, im * 128 : im * 128 + 128] = jnp.where(i0 >= i1, -(er * fi + ei * fr), 0.0).astype(BF16)
-        fr, fi = cre_ref[0, 128:256, m : m + 1], cim_ref[0, 128:256, m : m + 1]
-        er, ei = tre_ref[0, m : m + 1, L : L + 128], tim_ref[0, m : m + 1, L : L + 128]
-        kb[re * 128 : re * 128 + 128, :] = jnp.where(i1 >= i0, er * fr - ei * fi, 0.0).astype(BF16)
-        kb[im * 128 : im * 128 + 128, :] = jnp.where(i1 >= i0, -(er * fi + ei * fr), 0.0).astype(BF16)
 
     w = w_ref[0, : 2 * M, :]
     wr, wi = w[:M], w[M:]
@@ -109,10 +105,10 @@
             acc = acc + dot(kf[:, j * 256 : j * 256 + 256] * same2, scaled)
         out = skip * xf + acc
         mixed_ref[at, :] = (q_ref[at, :].astype(F32) * out).astype(BF16)
-        stack_ref[0, at, :] = (up_ref[at, :].astype(F32) * out).astype(BF16)
+        grad_ref[at, :] = (up_ref[at, :].astype(F32) * out).astype(BF16)
         reach = (row_h * flag(seg1[: 2 * M] == last)).astype(BF16)
         total = dot(reach, x)
-        tx[b] = total
+        tx[0, b] = total
         keep = flag(last == prior)
         return (
             total[:M] + keep * (pr * ur - pi * ui),
@@ -120,6 +116,52 @@
         )
 
     lax.fori_loop(0, blocks, forward, (u_ref[0, :M, :], u_ref[0, M:, :]))
+
+
+def backward_kernel(
+    clips, modes, starts_ref, cre_ref, cim_ref, tre_ref, tim_ref, w_ref, g_ref, q_ref, x_ref, up_ref, tx,
+    grad_ref, sums_ref, kb,
+):
+    rows = q_ref.shape[0]
+    blocks = rows // BLOCK_LEN
+    M = modes
+    L = 2 * rows
+    first = starts_ref[0]
+    i0 = lax.broadcasted_iota(jnp.int32, (BLOCK_LEN, BLOCK_LEN), 0)
+    i1 = lax.broadcasted_iota(jnp.int32, (BLOCK_LEN, BLOCK_LEN), 1)
+    for m in range(M):
+        re, im = m, M + m
+        fr, fi = cre_ref[0, 128:256, m : m + 1], cim_ref[0, 128:256, m : m + 1]
+        er, ei = tre_ref[0, m : m + 1, L : L + 128], tim_ref[0, m : m + 1, L : L + 128]
+        kb[re * 128 : re * 128 + 128, :] = jnp.where(i1 >= i0, er * fr - ei * fi, 0.0).astype(BF16)
+        kb[im * 128 : im * 128 + 128, :] = jnp.where(i1 >= i0, -(er * fi + ei * fr), 0.0).astype(BF16)
+
+    w = w_ref[0, : 2 * M, :]
+    wr, wi = w[:M], w[M:]
+    skip = w_ref[0, 2 * M : 2 * M + 1, :]
+    pr = tre_ref[0, :, L + 384 : L + 512]
+    pi = tim_ref[0, :, L + 384 : L + 512]
+    col_p = jnp.concatenate([cre_ref[0, :128, :], cim_ref[0, :128, :]], axis=1).astype(BF16)
+    col_h = jnp.concatenate([cre_ref[0, 256:, :], cim_ref[0, 256:, :]], axis=1).astype(BF16)
+    row_h = jnp.concatenate([tre_ref[0, :, L + 256 : L + 384], tim_ref[0, :, L + 256 : L + 384]], axis=0)
+    row_p = jnp.concatenate([tre_ref[0, :, L : L + 128], tim_ref[0, :, L : L + 128]], axis=0)
+
+    def flag(cond):
+        return jnp.where(cond, 1.0, 0.0).astype(F32)
+
+    def weigh(sr, si):
+        return jnp.concatenate([wr * sr - wi * si, -(wr * si + wi * sr)], axis=0).astype(BF16)
+
+    def masks(b):
+        begin = first + b * BLOCK_LEN
+        seg0 = segment_of(starts_ref, clips, i0 + begin)
+        seg1 = segment_of(starts_ref, clips, i1 + begin)
+        prior = segment_of(starts_ref, clips, begin - 1)
+        head = segment_of(starts_ref, clips, begin)
+        last = segment_of(starts_ref, clips, begin + BLOCK_LEN - 1)
+        after = segment_of(starts_ref, clips, begin + BLOCK_LEN)
+        return seg0, seg1, flag(seg0 == seg1).astype(BF16), prior, head, last, after
+
     sums_ref[...] = jnp.zeros_like(sums_ref)
 
     def backward(step, carried):
@@ -135,9 +177,9 @@
             part = dot(kb[m * 128 : m * 128 + 128, :] * same, gb)
             gx = gx + w[m : m + 1] * part
             sums_ref[0, m : m + 1, :] += jnp.sum(xf * part, axis=0, keepdims=True)
-        stack_ref[1, at, :] = gx.astype(BF16)
+        grad_ref[at, :] = gx.astype(BF16)
         sums_ref[0, 2 * M : 2 * M + 1, :] += jnp.sum(xf * g, axis=0, keepdims=True)
-        total = tx[b]
+        total = tx[0, b]
         join = flag(last == after)
         sums_ref[0, :M, :] += join * (total[:M] * gr - total[M:] * gi)
         sums_ref[0, M : 2 * M, :] -= join * (total[:M] * gi + total[M:] * gr)
@@ -163,9 +205,8 @@
     return value
 
 
-def summed_matrix(value):
-    stages = []
-    for axis, kind in (("dp", F32), ("tm", BF16)):
+def halved(value, axes, stages):
+    for axis, kind in axes:
         size, place = lax.axis_size(axis), lax.axis_index(axis)
         stride = 1
         while stride < size:
@@ -177,6 +218,10 @@
             value = kept + lax.ppermute(away, axis, pairs).astype(F32)
             stages.append((axis, pairs, upper))
             stride *= 2
+    return value
+
+
+def doubled(value, stages):
     value = value.astype(BF16)
     for axis, pairs, upper in reversed(stages):
         other = lax.ppermute(value, axis, pairs)
@@ -280,54 +325,72 @@
 
     per_head = lambda i, s: (i, 0, 0)
     column = lambda i, s: (0, i)
-    mixed, stacked, sums = pl.pallas_call(
-        functools.partial(conv_kernel, clips, M),
+    blocks = rows // BLOCK_LEN
+    shared = [
+        pl.BlockSpec((1, 3 * BLOCK_LEN, M), per_head),
+        pl.BlockSpec((1, 3 * BLOCK_LEN, M), per_head),
+        pl.BlockSpec((1, M, steps.size), per_head),
+        pl.BlockSpec((1, M, steps.size), per_head),
+        pl.BlockSpec((1, 2 * M + 8, 128), per_head),
+        pl.BlockSpec((1, 2 * M, 128), per_head),
+        pl.BlockSpec((rows, 128), column),
+        pl.BlockSpec((rows, 128), column),
+        pl.BlockSpec((rows, 128), column),
+    ]
+    totals_spec = pl.BlockSpec((1, blocks, 2 * M, 128), lambda i, s: (i, 0, 0, 0))
+    cost = pl.CostEstimate(
+        flops=4 * M * BLOCK_LEN * rows * channels * 4, bytes_accessed=10 * rows * channels, transcendentals=0
+    )
+    mixed, grad_query, totals = pl.pallas_call(
+        functools.partial(forward_kernel, clips, M),
         grid_spec=pltpu.PrefetchScalarGridSpec(
             num_scalar_prefetch=1,
             grid=(heads,),
-            in_specs=[
-                pl.BlockSpec((1, 3 * BLOCK_LEN, M), per_head),
-                pl.BlockSpec((1, 3 * BLOCK_LEN, M), per_head),
-                pl.BlockSpec((1, M, steps.size), per_head),
-                pl.BlockSpec((1, M, steps.size), per_head),
-                pl.BlockSpec((1, 2 * M + 8, 128), per_head),
-                pl.BlockSpec((1, 2 * M, 128), per_head),
-                pl.BlockSpec((1, 2 * M, 128), per_head),
-                pl.BlockSpec((rows, 128), column),
-                pl.BlockSpec((rows, 128), column),
-                pl.BlockSpec((rows, 128), column),
-            ],
-            out_specs=[
-                pl.BlockSpec((rows, 128), column),
-                pl.BlockSpec((2, rows, 128), lambda i, s: (0, 0, i)),
-                pl.BlockSpec((1, 2 * M + 8, 128), per_head),
-            ],
-            scratch_shapes=[
-                pltpu.VMEM((BLOCK_LEN, 2 * M * BLOCK_LEN), BF16),
-                pltpu.VMEM((2 * M * BLOCK_LEN, BLOCK_LEN), BF16),
-                pltpu.VMEM((rows // BLOCK_LEN, 2 * M, 128), F32),
-            ],
+            in_specs=shared,
+            out_specs=[pl.BlockSpec((rows, 128), column), pl.BlockSpec((rows, 128), column), totals_spec],
+            scratch_shapes=[pltpu.VMEM((BLOCK_LEN, 2 * M * BLOCK_LEN), BF16)],
         ),
         out_shape=[
             jax.ShapeDtypeStruct((rows, channels), BF16),
-            jax.ShapeDtypeStruct((2, rows, channels), BF16),
+            jax.ShapeDtypeStruct((rows, channels), BF16),
+            jax.ShapeDtypeStruct((heads, blocks, 2 * M, 128), F32),
+        ],
+        compiler_params=pltpu.CompilerParams(vmem_limit_bytes=40 << 20),
+        cost_estimate=cost,
+        name="conv_forward",
+    )(starts, col_re, col_im, table_re, table_im, w_table, entering, query_rows, signal, upstream)
+    norm_scale = 1.0 / math.sqrt(rows * count * lax.axis_size("dp"))
+    query_stages, value_stages = [], []
+    query_term = jnp.einsum("ld,lc->dc", features, grad_query, preferred_element_type=F32) * norm_scale
+    query_term = halved(query_term, [("dp", F32), ("tm", BF16)], query_stages)
+    grad_value, sums = pl.pallas_call(
+        functools.partial(backward_kernel, clips, M),
+        grid_spec=pltpu.PrefetchScalarGridSpec(
+            num_scalar_prefetch=1,
+            grid=(heads,),
+            in_specs=shared + [totals_spec],
+            out_specs=[pl.BlockSpec((rows, 128), column), pl.BlockSpec((1, 2 * M + 8, 128), per_head)],
+            scratch_shapes=[pltpu.VMEM((2 * M * BLOCK_LEN, BLOCK_LEN), BF16)],
+        ),
+        out_shape=[
+            jax.ShapeDtypeStruct((rows, channels), BF16),
             jax.ShapeDtypeStruct((heads, 2 * M + 8, 128), F32),
         ],
         compiler_params=pltpu.CompilerParams(vmem_limit_bytes=40 << 20),
-        name="conv",
-    )(starts, col_re, col_im, table_re, table_im, w_table, entering, leaving, query_rows, signal, upstream)
-
-    norm_scale = 1.0 / math.sqrt(rows * count * lax.axis_size("dp"))
+        cost_estimate=cost,
+        name="conv_backward",
+    )(starts, col_re, col_im, table_re, table_im, w_table, leaving, query_rows, signal, upstream, totals)
+
     coeff_term = sums[:, : 2 * M].reshape(heads, 2, M, 128) * (weight[:, None, :, None] * norm_scale)
     coeff_term = coeff_term.transpose(1, 2, 0, 3).reshape(2, M, channels)
     skip_term = sums[:, 2 * M].reshape(channels) * norm_scale
-    proj_terms = [
-        jnp.einsum("ld,lc->dc", features, stacked[k], preferred_element_type=F32) * norm_scale
-        for k in range(2)
-    ]
-    partial_in = jnp.einsum("klc,kdc->ld", stacked, in_proj, preferred_element_type=F32)
+    value_term = jnp.einsum("ld,lc->dc", features, grad_value, preferred_element_type=F32) * norm_scale
+    query_term, value_term = lax.optimization_barrier((query_term, value_term))
+    value_term = halved(value_term, [("dp", F32), ("tm", BF16)], value_stages)
+    partial_in = jnp.einsum("lc,dc->ld", grad_query, in_proj[0], preferred_element_type=F32)
+    partial_in += jnp.einsum("lc,dc->ld", grad_value, in_proj[1], preferred_element_type=F32)
     small = jnp.concatenate([coeff_term.reshape(2 * M, channels), skip_term[None]], axis=0)
-    proj_sum = jnp.stack([summed_matrix(term) for term in proj_terms])
+    proj_sum = jnp.stack([doubled(query_term, query_stages), doubled(value_term, value_stages)])
     small = summed_over(summed_over(small, "dp"), "tm")
     coeff_sum = small[: 2 * M].reshape(2, M, channels)
     skip_sum = small[2 * M]

time: 128 us -> 130 us (1.016)
  starting transfers between devices: 22 us -> 16.3 us
  local copies, waits for them, and re-layouts: 4.08 us -> 7.99 us
  waiting for transfers between devices: 37.6 us -> 40.4 us
  Pallas kernels: 24 us -> 25.3 us
    ppermute x3, starting transfers between devices: 4.03 us -> 1 us  [summed_over(): lax.ppermute(value, axis, [(i, i ^ stride) for i in range(size)])]
    ppermute x12, waiting for transfers between devices: 29.8 us -> 32.6 us  [the longest x6 17.3 us: halved(): value = kept + lax.ppermute(away, axis, pairs).astype(F32)]
    ppermute x12, starting transfers between devices: 13.4 us -> 10.7 us  [the longest x6 8.8 us: halved(): value = kept + lax.ppermute(away, axis, pairs).astype(F32)]
    add x4 -> x5, other arithmetic: 0.56 us -> 2.13 us  [halved(): value = kept + lax.ppermute(away, axis, pairs).astype(F32)]
    pallas_call x1 -> x2, Pallas kernels: 20.8 us -> 22.1 us  [the longest x1 11.1 us: shards(): pl.pallas_call(functools.partial(backward_kernel, clips, M), grid_spec=pl...]
    unnamed x12 -> x48, local copies, waits for them, and re-layouts: 1.64 us -> 2.66 us
    dot_general x3 -> x4, matrix products: 3.83 us -> 4.03 us  [the longest x1 1.01 us: shards(): jnp.einsum('lc,dc->ld', grad_query, in_proj[0], preferred_element_type=F32)]
  transfers between devices with their start and end apart: 17 -> 17, of which waited for: 12 -> 13; matrix products, arithmetic and copies ran while one was open for 10% -> 11% of each run, Pallas kernels for 0% -> 9%
where the time goes in v5:
time: 130 us
  waiting for transfers between devices  40.4 us (31%)
  Pallas kernels  25.3 us (19%)
  starting transfers between devices  16.3 us (13%)
  blocking collectives  14.4 us (11%)
  other arithmetic  12.5 us (10%)
  between operations  9.04 us (7%)
  local copies, waits for them, and re-layouts  7.99 us (6%)
  matrix products  4.03 us (3%)
    ppermute x6, waiting for transfers between devices, halved(): value = kept + lax.ppermute(away, axis, pairs).astype(F32)  17.3 us
    ppermute x6, waiting for transfers between devices, doubled(): other = lax.ppermute(value, axis, pairs)  15.3 us
    all_gather x1, blocking collectives, shards(): gathered = lax.all_gather(ends, 'tm')  14.4 us
    pallas_call x1, Pallas kernels, shards(): pl.pallas_call(functools.partial(backward_kernel, clips, M), grid_spec=pl...  11.1 us
    pallas_call x1, Pallas kernels, shards(): pl.pallas_call(functools.partial(forward_kernel, clips, M), grid_spec=plt...  11 us
    ppermute x6, starting transfers between devices, halved(): value = kept + lax.ppermute(away, axis, pairs).astype(F32)  8.8 us
    ppermute x3, waiting for transfers between devices, summed_over(): lax.ppermute(value, axis, [(i, i ^ stride) for i in range(size)])  5.43 us
    pallas_call x1, Pallas kernels, shards(): pl.pallas_call(functools.partial(project_kernel, clips, M), grid_spec=plt...  3.18 us
  transfers between devices with their start and end apart: 17, of which 13 were waited for; matrix products, arithmetic and copies ran while one was open for 11% of the time, Pallas kernels for 9%

profile of v5, /device:TPU:0, one launch (start us, length us, event | category | flops | bytes accessed | tf_op | source)
XLA Modules:
  0.0 129.9 jit_solution(15090295328167203606)
XLA Ops:
  0.7 3.0 %collective-permute-start = (bf16[768,512]{1,0:T(8,128)(2,1)}, bf16[768,512]{1,0:T(8,128)(2,1)S(1)}, u32[]{:S(2)}, u32[]{:S(2)}) collective-permute-start(bf16[768,512]{1,0:T(8,128)(2,1)} %bitcast.110), channel_id=1, source_target_pairs={{0,2},{2,0},{1,3},{3,1},{4,6},{6,4},{5,7},{7,5},{8,10},{10,8},{9,1... | collective-permute-start | bytes 2359304 | tf_op jit(solution)/shard_map/ppermute | solution.py:237
  3.7 0.7 sqrt_bitcast_fusion
  4.5 1.7 %fusion.7 = (f32[4,8,2048]{2,1,0:T(8,128)S(1)}, f32[4,8,2048]{2,1,0:T(8,128)S(1)}) fusion(f32[4,8]{1,0:T(4,128)} %bitcast.111, f32[2048]{0:T(1024)S(1)} %convert_element_type.108, f32[4,8]{1,0:T(4,128)S(1)} %get-tuple-element.67), kind=kLoop, calls=%fused_computation.30 | loop fusion | flops 262144 | bytes 532736 | tf_op jit(solution)/shard_map/mul | solution.py:267
  6.2 0.1 slice_reduce_fusion
  6.3 0.8 reduce-window.9
  7.1 1.5 %fusion.28 = (s32[]{:T(128)}, s32[]{:T(128)}, s32[]{:T(128)}, s32[]{:T(128)}, s32[]{:T(128)}, /*index=5*/s32[]{:T(128)}, s32[]{:T(128)}, s32[]{:T(128)}, s32[4]{0:T(128)S(1)}) fusion(s32[1,4]{1,0:T(1,128)} %param.14, s32[4,1]{0,1:T(1,128)S(1)} %reduce-window.9), kind=kLoop, calls=%fused_computation.117 | loop fusion | flops 92 | bytes 80 | tf_op jit(solution)/shard_map/reduce_sum | solution.py:310
  16.4 1.2 copy.26.cim_ref
  17.6 1.2 copy.25.cre_ref
  18.7 0.1 pad.28.clone
  18.8 0.1 pad_add_fusion.starts_ref
  18.9 0.1 fusion.22
  19.0 0.1 maximum_maximum_fusion.w_ref
  19.0 2.4 %collective-permute-done = bf16[768,512]{1,0:T(8,128)(2,1)S(1)} collective-permute-done((bf16[768,512]{1,0:T(8,128)(2,1)}, bf16[768,512]{1,0:T(8,128)(2,1)S(1)}, u32[]{:S(2)}, u32[]{:S(2)}) %collective-permute-start) | collective-permute-done | bytes 786464 | tf_op jit(solution)/shard_map/ppermute | solution.py:237
  21.4 0.1 broadcast_select_fusion.1
  21.6 0.2 pad_maximum_fusion.feat_ref
  21.8 1.9 %copy-done.1 = bf16[2,1024,512]{2,1,0:T(8,128)(2,1)S(1)} copy-done((bf16[2,1024,512]{2,1,0:T(8,128)(2,1)S(1)}, bf16[2,1024,512]{2,1,0:T(8,128)(2,1)}, u32[]{:S(2)}) %copy-start.1) | copy-done | bytes 2097176
  23.7 0.2 copy-done.2
  23.9 3.2 %project.1 = (bf16[768,512]{1,0:T(8,128)(2,1)S(1)}, bf16[768,512]{1,0:T(8,128)(2,1)S(1)}, f32[4,32,128]{2,1,0:T(8,128)S(1)}) custom-call(s32[5]{0:T(128)S(1)} %pad_add_fusion.starts_ref, bf16[768,1024]{1,0:T(8,128)(2,1)S(1)} %pad_maximum_fusion.feat_ref, bf16[2,1024,512]{2,1,0:T(8,128)(2,1)S(1)} %copy-done.1, bf16[768,512]{1,0:T(8,128)(2,1)S(1)} %bitcast.103, ...), custom_call_target="tpu_custom_call" | custom-call | tf_op jit(solution)/shard_map/project/pallas_call | solution.py:280
  27.1 14.4 %all-gather = f32[16,32,128]{2,1,0:T(8,128)S(1)} all-gather(f32[4,32,128]{2,1,0:T(8,128)S(1)} %get-tuple-element.15), channel_id=2, replica_groups=mesh['group'=2,'tm'=4,'tensor'=2,'dp'=2] {'tm'}, dimensions={0}, use_global_device_ids=true | all-gather | bytes 327680 | tf_op jit(solution)/shard_map/all_gather | solution.py:318
  41.7 0.1 multiply_subtract_fusion.1
  41.7 0.1 multiply_subtract_fusion
  41.9 0.1 multiply_subtract_fusion.2
  42.0 11.0 %conv_forward.1 = (bf16[768,512]{1,0:T(8,128)(2,1)}, bf16[768,512]{1,0:T(8,128)(2,1)S(1)}, f32[4,6,16,128]{3,2,1,0:T(8,128)S(1)}) custom-call(s32[5]{0:T(128)S(1)} %pad_add_fusion.starts_ref, f32[4,384,8]{2,1,0:T(8,128)S(1)} %copy-done.7, f32[4,384,8]{2,1,0:T(8,128)S(1)} %copy-done.5, f32[4,8,2048]{2,1,0:T(8,128)S(1)} %get-tuple-element.61.tre_ref, ...), custom_call_target="tpu_custom_call" | custom-call | flops 6442450944 | bytes 3932160 | tf_op jit(solution)/shard_map/conv_forward/pallas_call | solution.py:344
  53.0 1.0 convolution_multiply_fusion.1
  54.1 1.2 constant_dynamic-slice_fusion.1
  55.2 0.5 copy-done.19
  55.8 2.9 %collective-permute-done.2 = f32[512,512]{1,0:T(8,128)} collective-permute-done((f32[512,512]{1,0:T(8,128)}, f32[512,512]{1,0:T(8,128)}, u32[]{:S(2)}, u32[]{:S(2)}) %collective-permute-start.2) | collective-permute-done | bytes 1048608 | tf_op jit(solution)/shard_map/ppermute | solution.py:218
  58.7 1.7 %dynamic-slice_add_fusion.1 = f32[512,512]{1,0:T(8,128)S(1)} fusion(f32[512,512]{1,0:T(8,128)} %collective-permute-done.2, f32[1024,512]{1,0:T(8,128)} %copy-done.19, s32[]{:T(128)S(6)} %select_n.174), kind=kLoop, calls=%fused_computation.11 | loop fusion | flops 262144 | bytes 3145732 | tf_op jit(solution)/shard_map/add | solution.py:218
  60.5 1.6 %collective-permute-start.3 = (bf16[256,512]{1,0:T(8,128)(2,1)S(1)}, bf16[256,512]{1,0:T(8,128)(2,1)S(1)}, u32[]{:S(2)}, u32[]{:S(2)}) collective-permute-start(bf16[256,512]{1,0:T(8,128)(2,1)S(1)} %dynamic-slice_convert_fusion.2), channel_id=1, source_target_pairs={{0,4},{4,0},{8,12},{12,8},{1,5},{5,1},{9,13},{13,9},{2,6},{6,2},{1... | collective-permute-start | bytes 786440 | tf_op jit(solution)/shard_map/ppermute | solution.py:218
  62.1 11.1 %conv_backward.1 = (bf16[768,512]{1,0:T(8,128)(2,1)S(1)}, f32[4,24,128]{2,1,0:T(8,128)S(1)}) custom-call(s32[5]{0:T(128)S(1)} %pad_add_fusion.starts_ref, f32[4,384,8]{2,1,0:T(8,128)S(1)} %copy-done.8, f32[4,384,8]{2,1,0:T(8,128)S(1)} %copy-done.6, f32[4,8,2048]{2,1,0:T(8,128)S(1)} %get-tuple-element.61.tre_ref, ...), custom_call_target="tpu_custom_call" | custom-call | flops 6442450944 | bytes 3932160 | tf_op jit(solution)/shard_map/conv_backward/pallas_call | solution.py:366
  73.3 2.5 %collective-permute-start.4 = (bf16[128,512]{1,0:T(8,128)(2,1)S(1)}, bf16[128,512]{1,0:T(8,128)(2,1)S(1)}, u32[]{:S(2)}, u32[]{:S(2)}) collective-permute-start(bf16[128,512]{1,0:T(8,128)(2,1)S(1)} %dynamic-slice_convert_fusion.4), channel_id=1, source_target_pairs={{0,8},{4,12},{8,0},{12,4},{1,9},{5,13},{9,1},{13,5},{2,10},{6,14},... | collective-permute-start | bytes 393224 | tf_op jit(solution)/shard_map/ppermute | solution.py:218
  75.9 1.0 convolution_multiply_fusion
  76.9 5.5 %collective-permute-done.4 = bf16[128,512]{1,0:T(8,128)(2,1)S(1)} collective-permute-done((bf16[128,512]{1,0:T(8,128)(2,1)S(1)}, bf16[128,512]{1,0:T(8,128)(2,1)S(1)}, u32[]{:S(2)}, u32[]{:S(2)}) %collective-permute-start.4) | collective-permute-done | bytes 131104 | tf_op jit(solution)/shard_map/ppermute | solution.py:218
  82.4 0.1 constant_dynamic-slice_fusion
  82.5 0.1 collective-permute-start.8
  82.6 0.1 fusion.23
  82.6 0.6 collective-permute-start.14
  83.2 1.0 fusion.1
  84.2 1.1 collective-permute-done.14
  85.4 0.2 dynamic-slice_add_fusion
  85.6 2.1 %collective-permute-start.9 = (bf16[256,512]{1,0:T(8,128)(2,1)S(1)}, bf16[256,512]{1,0:T(8,128)(2,1)S(1)}, u32[]{:S(2)}, u32[]{:S(2)}) collective-permute-start(bf16[256,512]{1,0:T(8,128)(2,1)S(1)} %dynamic-slice_convert_fusion.1), channel_id=1, source_target_pairs={{0,4},{4,0},{8,12},{12,8},{1,5},{5,1},{9,13},{13,9},{2,6},{6,2},{1... | collective-permute-start | bytes 786440 | tf_op jit(solution)/shard_map/ppermute | solution.py:218
  87.7 1.0 convolution_add_fusion
  88.7 1.2 collective-permute-done.15
  89.9 0.4 collective-permute-start.16
  90.3 0.1 dynamic-slice_convert_fusion
  90.4 1.5 %collective-permute-start.1 = (bf16[768,512]{1,0:T(8,128)(2,1)S(1)}, bf16[768,512]{1,0:T(8,128)(2,1)S(1)}, u32[]{:S(2)}, u32[]{:S(2)}) collective-permute-start(bf16[768,512]{1,0:T(8,128)(2,1)S(1)} %dynamic-slice_convert_fusion), channel_id=1, source_target_pairs={{0,2},{2,0},{1,3},{3,1},{4,6},{6,4},{5,7},{7,5},{8,10},{10,8},{9,1... | collective-permute-start | bytes 2359304 | tf_op jit(solution)/shard_map/ppermute | solution.py:403
  92.0 3.2 %collective-permute-done.16 = f32[17,512]{1,0:T(8,128)S(1)} collective-permute-done((f32[17,512]{1,0:T(8,128)S(1)}, f32[17,512]{1,0:T(8,128)S(1)}, u32[]{:S(2)}, u32[]{:S(2)}) %collective-permute-start.16) | collective-permute-done | bytes 34848 | tf_op jit(solution)/shard_map/ppermute | solution.py:203
  95.1 0.6 slice.115
  95.9 2.6 %collective-permute-start.10 = (bf16[128,512]{1,0:T(8,128)(2,1)S(1)}, bf16[128,512]{1,0:T(8,128)(2,1)S(1)}, u32[]{:S(2)}, u32[]{:S(2)}) collective-permute-start(bf16[128,512]{1,0:T(8,128)(2,1)S(1)} %dynamic-slice_convert_fusion.3), channel_id=1, source_target_pairs={{0,8},{4,12},{8,0},{12,4},{1,9},{5,13},{9,1},{13,5},{2,10},{6,14},... | collective-permute-start | bytes 393224 | tf_op jit(solution)/shard_map/ppermute | solution.py:218
  98.5 0.6 slice_bitcast_fusion.2
  99.1 0.4 collective-permute-start.5
  99.5 8.8 %collective-permute-done.10 = bf16[128,512]{1,0:T(8,128)(2,1)S(1)} collective-permute-done((bf16[128,512]{1,0:T(8,128)(2,1)S(1)}, bf16[128,512]{1,0:T(8,128)(2,1)S(1)}, u32[]{:S(2)}, u32[]{:S(2)}) %collective-permute-start.10) | collective-permute-done | bytes 131104 | tf_op jit(solution)/shard_map/ppermute | solution.py:218
  108.5 4.2 %collective-permute-done.5 = bf16[128,512]{1,0:T(8,128)(2,1)S(1)} collective-permute-done((bf16[128,512]{1,0:T(8,128)(2,1)S(1)}, bf16[128,512]{1,0:T(8,128)(2,1)S(1)}, u32[]{:S(2)}, u32[]{:S(2)}) %collective-permute-start.5) | collective-permute-done | bytes 131104 | tf_op jit(solution)/shard_map/ppermute | solution.py:227
  112.8 2.6 %collective-permute-done.11 = bf16[128,512]{1,0:T(8,128)(2,1)S(1)} collective-permute-done((bf16[128,512]{1,0:T(8,128)(2,1)S(1)}, bf16[128,512]{1,0:T(8,128)(2,1)S(1)}, u32[]{:S(2)}, u32[]{:S(2)}) %collective-permute-start.11) | collective-permute-done | bytes 131104 | tf_op jit(solution)/shard_map/ppermute | solution.py:227
  115.5 1.2 collective-permute-start.12
  116.7 5.3 %collective-permute-done.6 = bf16[256,512]{1,0:T(8,128)(2,1)S(1)} collective-permute-done((bf16[256,512]{1,0:T(8,128)(2,1)S(1)}, bf16[256,512]{1,0:T(8,128)(2,1)S(1)}, u32[]{:S(2)}, u32[]{:S(2)}) %collective-permute-start.6) | collective-permute-done | bytes 262176 | tf_op jit(solution)/shard_map/ppermute | solution.py:227
  122.0 0.1 broadcast_select_fusion.5
  122.3 2.7 %collective-permute-done.12 = bf16[256,512]{1,0:T(8,128)(2,1)S(1)} collective-permute-done((bf16[256,512]{1,0:T(8,128)(2,1)S(1)}, bf16[256,512]{1,0:T(8,128)(2,1)S(1)}, u32[]{:S(2)}, u32[]{:S(2)}) %collective-permute-start.12) | collective-permute-done | bytes 262176 | tf_op jit(solution)/shard_map/ppermute | solution.py:227
  124.9 0.1 broadcast_select_fusion.3
  125.2 1.2 fusion.5
  126.4 0.2 select_bitcast_fusion.3
  126.6 0.5 collective-permute-done.13
  127.0 0.2 select_bitcast_fusion.1
  127.3 2.6 %maximum_convert_fusion = f32[2,1024,512]{2,1,0:T(8,128)} fusion(bf16[1,512,512]{2,1,0:T(8,128)(2,1)S(1)} %get-tuple-element.39, bf16[1,512,512]{2,1,0:T(8,128)(2,1)S(1)} %get-tuple-element.38, bf16[1,512,512]{2,1,0:T(8,128)(2,1)S(1)} %get-tuple-element.37, bf16[1,512,512]{2,1,0:T(8,128)(2,1)S(1)} %get-tuple-element.36), kind=kLoop, calls=%fused_computation | loop fusion | flops 8388608 | bytes 6291456 | tf_op jit(solution)/shard_map/stack | solution.py:393
  (91 shorter events, 1.3 us)
Async XLA Ops:
  0.6 18.3 %copy-start = (f32[2,8,512]{2,1,0:T(8,128)S(1)}, f32[2,8,512]{2,1,0:T(8,128)}, u32[]{:S(2)}) copy-start(f32[2,8,512]{2,1,0:T(8,128)} %param.12) | copy-start | bytes 98308
  0.6 20.8 %copy-start.20 = (bf16[1,768,512]{2,1,0:T(8,128)(2,1)S(1)}, bf16[1,768,512]{2,1,0:T(8,128)(2,1)}, u32[]{:S(2)}) copy-start(bf16[1,768,512]{2,1,0:T(8,128)(2,1)} %param.8) | copy-start | bytes 2359300
  0.7 18.3 %copy-start.22 = (f32[512]{0:T(512)S(1)}, f32[512]{0:T(512)}, u32[]{:S(2)}) copy-start(f32[512]{0:T(512)} %param.13) | copy-start | bytes 6148
  0.7 20.8 %collective-permute-start = (bf16[768,512]{1,0:T(8,128)(2,1)}, bf16[768,512]{1,0:T(8,128)(2,1)S(1)}, u32[]{:S(2)}, u32[]{:S(2)}) collective-permute-start(bf16[768,512]{1,0:T(8,128)(2,1)} %bitcast.110), channel_id=1, source_target_pairs={{0,2},{2,0},{1,3},{3,1},{4,6},{6,4},{5,7},{7,5},{8,10},{10,8},{9,1... | collective-permute-start | bytes 2359304 | tf_op jit(solution)/shard_map/ppermute | solution.py:237
  21.5 31.4 %copy-start.15 = (bf16[768,512]{1,0:T(8,128)(2,1)}, bf16[768,512]{1,0:T(8,128)(2,1)S(1)}, u32[]{:S(2)}) copy-start(bf16[768,512]{1,0:T(8,128)(2,1)S(1)} %get-tuple-element.34) | copy-start | bytes 2359300
  21.5 31.4 %copy-start.17 = (bf16[768,512]{1,0:T(8,128)(2,1)}, bf16[768,512]{1,0:T(8,128)(2,1)S(1)}, u32[]{:S(2)}) copy-start(bf16[768,512]{1,0:T(8,128)(2,1)S(1)} %get-tuple-element.35) | copy-start | bytes 2359300
  21.6 2.2 %copy-start.1 = (bf16[2,1024,512]{2,1,0:T(8,128)(2,1)S(1)}, bf16[2,1024,512]{2,1,0:T(8,128)(2,1)}, u32[]{:S(2)}) copy-start(bf16[2,1024,512]{2,1,0:T(8,128)(2,1)} %proj_ref.1) | copy-start | bytes 6291460
  21.6 2.3 %copy-start.2 = (bf16[1,768,512]{2,1,0:T(8,128)(2,1)S(1)}, bf16[1,768,512]{2,1,0:T(8,128)(2,1)}, u32[]{:S(2)}) copy-start(bf16[1,768,512]{2,1,0:T(8,128)(2,1)} %param.15) | copy-start | bytes 2359300
  23.9 18.1 %copy-start.5 = (f32[4,384,8]{2,1,0:T(8,128)S(1)}, f32[4,384,8]{2,1,0:T(8,128)}, u32[]{:S(2)}) copy-start(f32[4,384,8]{2,1,0:T(8,128)} %copy.26.cim_ref) | copy-start | bytes 147460
  23.9 18.1 %copy-start.7 = (f32[4,384,8]{2,1,0:T(8,128)S(1)}, f32[4,384,8]{2,1,0:T(8,128)}, u32[]{:S(2)}) copy-start(f32[4,384,8]{2,1,0:T(8,128)} %copy.25.cre_ref) | copy-start | bytes 147460
  27.1 25.9 %copy-start.9 = (bf16[768,512]{1,0:T(8,128)(2,1)}, bf16[768,512]{1,0:T(8,128)(2,1)S(1)}, u32[]{:S(2)}) copy-start(bf16[768,512]{1,0:T(8,128)(2,1)S(1)} %get-tuple-element.16.q_ref) | copy-start | bytes 2359300
  27.1 25.9 %copy-start.11 = (bf16[768,512]{1,0:T(8,128)(2,1)}, bf16[768,512]{1,0:T(8,128)(2,1)S(1)}, u32[]{:S(2)}) copy-start(bf16[768,512]{1,0:T(8,128)(2,1)S(1)} %get-tuple-element.17.x_ref) | copy-start | bytes 2359300
  53.0 1.0 copy-start.3
  53.0 1.0 copy-start.13
  54.0 1.7 %copy-start.19 = (f32[1024,512]{1,0:T(8,128)}, f32[1024,512]{1,0:T(8,128)S(1)}, u32[]{:S(2)}) copy-start(f32[1024,512]{1,0:T(8,128)S(1)} %convolution_multiply_fusion.1) | copy-start | bytes 6291460
  54.0 1.7 %copy-start.21 = (f32[8,4]{0,1:T(4,128)S(1)}, f32[8,4]{0,1:T(4,128)}, u32[]{:S(2)}) copy-start(f32[8,4]{0,1:T(4,128)} %param.10) | copy-start | bytes 388
  55.7 3.0 %collective-permute-start.2 = (f32[512,512]{1,0:T(8,128)}, f32[512,512]{1,0:T(8,128)}, u32[]{:S(2)}, u32[]{:S(2)}) collective-permute-start(f32[512,512]{1,0:T(8,128)} %constant_dynamic-slice_fusion.1), channel_id=1, source_target_pairs={{0,1},{1,0},{2,3},{3,2},{4,5},{5,4},{6,7},{7,6},{8,9},{9,8},{10,11... | collective-permute-start | bytes 3145736 | tf_op jit(solution)/shard_map/ppermute | solution.py:218
  55.7 6.4 %copy-start.6 = (f32[4,384,8]{2,1,0:T(8,128)S(1)}, f32[4,384,8]{2,1,0:T(8,128)}, u32[]{:S(2)}) copy-start(f32[4,384,8]{2,1,0:T(8,128)} %copy.26.cim_ref) | copy-start | bytes 147460
  55.7 6.4 %copy-start.8 = (f32[4,384,8]{2,1,0:T(8,128)S(1)}, f32[4,384,8]{2,1,0:T(8,128)}, u32[]{:S(2)}) copy-start(f32[4,384,8]{2,1,0:T(8,128)} %copy.25.cre_ref) | copy-start | bytes 147460
  55.7 6.4 %copy-start.10 = (bf16[768,512]{1,0:T(8,128)(2,1)S(1)}, bf16[768,512]{1,0:T(8,128)(2,1)}, u32[]{:S(2)}) copy-start(bf16[768,512]{1,0:T(8,128)(2,1)} %copy-done.9) | copy-start | bytes 2359300
  55.7 6.3 %copy-start.12 = (bf16[768,512]{1,0:T(8,128)(2,1)S(1)}, bf16[768,512]{1,0:T(8,128)(2,1)}, u32[]{:S(2)}) copy-start(bf16[768,512]{1,0:T(8,128)(2,1)} %copy-done.11) | copy-start | bytes 2359300
  55.7 6.3 %copy-start.14 = (f32[4,6,16,128]{3,2,1,0:T(8,128)S(1)}, f32[4,6,16,128]{3,2,1,0:T(8,128)}, u32[]{:S(2)}) copy-start(f32[4,6,16,128]{3,2,1,0:T(8,128)} %copy-done.13) | copy-start | bytes 589828
  60.5 12.7 %collective-permute-start.3 = (bf16[256,512]{1,0:T(8,128)(2,1)S(1)}, bf16[256,512]{1,0:T(8,128)(2,1)S(1)}, u32[]{:S(2)}, u32[]{:S(2)}) collective-permute-start(bf16[256,512]{1,0:T(8,128)(2,1)S(1)} %dynamic-slice_convert_fusion.2), channel_id=1, source_target_pairs={{0,4},{4,0},{8,12},{12,8},{1,5},{5,1},{9,13},{13,9},{2,6},{6,2},{1... | collective-permute-start | bytes 786440 | tf_op jit(solution)/shard_map/ppermute | solution.py:218
  62.1 13.8 %copy-start.16 = (bf16[768,512]{1,0:T(8,128)(2,1)S(1)}, bf16[768,512]{1,0:T(8,128)(2,1)}, u32[]{:S(2)}) copy-start(bf16[768,512]{1,0:T(8,128)(2,1)} %copy-done.15) | copy-start | bytes 2359300
  62.1 13.8 %copy-start.18 = (bf16[768,512]{1,0:T(8,128)(2,1)S(1)}, bf16[768,512]{1,0:T(8,128)(2,1)}, u32[]{:S(2)}) copy-start(bf16[768,512]{1,0:T(8,128)(2,1)} %copy-done.17) | copy-start | bytes 2359300
  73.3 9.0 %collective-permute-start.4 = (bf16[128,512]{1,0:T(8,128)(2,1)S(1)}, bf16[128,512]{1,0:T(8,128)(2,1)S(1)}, u32[]{:S(2)}, u32[]{:S(2)}) collective-permute-start(bf16[128,512]{1,0:T(8,128)(2,1)S(1)} %dynamic-slice_convert_fusion.4), channel_id=1, source_target_pairs={{0,8},{4,12},{8,0},{12,4},{1,9},{5,13},{9,1},{13,5},{2,10},{6,14},... | collective-permute-start | bytes 393224 | tf_op jit(solution)/shard_map/ppermute | solution.py:218
  76.9 6.3 %copy-start.4 = (bf16[768,512]{1,0:T(8,128)(2,1)S(1)}, bf16[768,512]{1,0:T(8,128)(2,1)}, u32[]{:S(2)}) copy-start(bf16[768,512]{1,0:T(8,128)(2,1)} %copy-done.3) | copy-start | bytes 2359300
  82.5 2.9 %collective-permute-start.8 = (f32[512,512]{1,0:T(8,128)S(1)}, f32[512,512]{1,0:T(8,128)S(1)}, u32[]{:S(2)}, u32[]{:S(2)}) collective-permute-start(f32[512,512]{1,0:T(8,128)S(1)} %constant_dynamic-slice_fusion), channel_id=1, source_target_pairs={{0,1},{1,0},{2,3},{3,2},{4,5},{5,4},{6,7},{7,6},{8,9},{9,8},{10,11... | collective-permute-start | bytes 3145736 | tf_op jit(solution)/shard_map/ppermute | solution.py:218
  82.6 2.6 %collective-permute-start.14 = (f32[17,512]{1,0:T(8,128)S(1)}, f32[17,512]{1,0:T(8,128)S(1)}, u32[]{:S(2)}, u32[]{:S(2)}) collective-permute-start(f32[17,512]{1,0:T(8,128)S(1)} %pad_maximum_fusion.5), channel_id=1, source_target_pairs={{0,1},{1,0},{2,3},{3,2},{4,5},{5,4},{6,7},{7,6},{8,9},{9,8},{10,11... | collective-permute-start | bytes 104456 | tf_op jit(solution)/shard_map/ppermute | solution.py:203
  85.3 4.6 %collective-permute-start.15 = (f32[17,512]{1,0:T(8,128)S(1)}, f32[17,512]{1,0:T(8,128)S(1)}, u32[]{:S(2)}, u32[]{:S(2)}) collective-permute-start(f32[17,512]{1,0:T(8,128)S(1)} %fusion.32), channel_id=1, source_target_pairs={{0,4},{4,0},{8,12},{12,8},{1,5},{5,1},{9,13},{13,9},{2,6},{6,2},{1... | collective-permute-start | bytes 104456 | tf_op jit(solution)/shard_map/ppermute | solution.py:203
  85.6 10.2 %collective-permute-start.9 = (bf16[256,512]{1,0:T(8,128)(2,1)S(1)}, bf16[256,512]{1,0:T(8,128)(2,1)S(1)}, u32[]{:S(2)}, u32[]{:S(2)}) collective-permute-start(bf16[256,512]{1,0:T(8,128)(2,1)S(1)} %dynamic-slice_convert_fusion.1), channel_id=1, source_target_pairs={{0,4},{4,0},{8,12},{12,8},{1,5},{5,1},{9,13},{13,9},{2,6},{6,2},{1... | collective-permute-start | bytes 786440 | tf_op jit(solution)/shard_map/ppermute | solution.py:218
  89.9 5.2 %collective-permute-start.16 = (f32[17,512]{1,0:T(8,128)S(1)}, f32[17,512]{1,0:T(8,128)S(1)}, u32[]{:S(2)}, u32[]{:S(2)}) collective-permute-start(f32[17,512]{1,0:T(8,128)S(1)} %add.141), channel_id=1, source_target_pairs={{0,8},{4,12},{8,0},{12,4},{1,9},{5,13},{9,1},{13,5},{2,10},{6,14},... | collective-permute-start | bytes 104456 | tf_op jit(solution)/shard_map/ppermute | solution.py:203
  90.4 34.7 %collective-permute-start.1 = (bf16[768,512]{1,0:T(8,128)(2,1)S(1)}, bf16[768,512]{1,0:T(8,128)(2,1)S(1)}, u32[]{:S(2)}, u32[]{:S(2)}) collective-permute-start(bf16[768,512]{1,0:T(8,128)(2,1)S(1)} %dynamic-slice_convert_fusion), channel_id=1, source_target_pairs={{0,2},{2,0},{1,3},{3,1},{4,6},{6,4},{5,7},{7,5},{8,10},{10,8},{9,1... | collective-permute-start | bytes 2359304 | tf_op jit(solution)/shard_map/ppermute | solution.py:403
  95.9 12.4 %collective-permute-start.10 = (bf16[128,512]{1,0:T(8,128)(2,1)S(1)}, bf16[128,512]{1,0:T(8,128)(2,1)S(1)}, u32[]{:S(2)}, u32[]{:S(2)}) collective-permute-start(bf16[128,512]{1,0:T(8,128)(2,1)S(1)} %dynamic-slice_convert_fusion.3), channel_id=1, source_target_pairs={{0,8},{4,12},{8,0},{12,4},{1,9},{5,13},{9,1},{13,5},{2,10},{6,14},... | collective-permute-start | bytes 393224 | tf_op jit(solution)/shard_map/ppermute | solution.py:218
  99.1 13.6 %collective-permute-start.5 = (bf16[128,512]{1,0:T(8,128)(2,1)S(1)}, bf16[128,512]{1,0:T(8,128)(2,1)S(1)}, u32[]{:S(2)}, u32[]{:S(2)}) collective-permute-start(bf16[128,512]{1,0:T(8,128)(2,1)S(1)} %convert_add_fusion.2), channel_id=1, source_target_pairs={{0,8},{4,12},{8,0},{12,4},{1,9},{5,13},{9,1},{13,5},{2,10},{6,14},... | collective-permute-start | bytes 393224 | tf_op jit(solution)/shard_map/ppermute | solution.py:227
  108.4 7.0 %collective-permute-start.11 = (bf16[128,512]{1,0:T(8,128)(2,1)S(1)}, bf16[128,512]{1,0:T(8,128)(2,1)S(1)}, u32[]{:S(2)}, u32[]{:S(2)}) collective-permute-start(bf16[128,512]{1,0:T(8,128)(2,1)S(1)} %add_convert_fusion.1), channel_id=1, source_target_pairs={{0,8},{4,12},{8,0},{12,4},{1,9},{5,13},{9,1},{13,5},{2,10},{6,14},... | collective-permute-start | bytes 393224 | tf_op jit(solution)/shard_map/ppermute | solution.py:227
  112.7 9.3 %collective-permute-start.6 = (bf16[256,512]{1,0:T(8,128)(2,1)S(1)}, bf16[256,512]{1,0:T(8,128)(2,1)S(1)}, u32[]{:S(2)}, u32[]{:S(2)}) collective-permute-start(bf16[256,512]{1,0:T(8,128)(2,1)S(1)} %pad_maximum_fusion.3), channel_id=1, source_target_pairs={{0,4},{4,0},{8,12},{12,8},{1,5},{5,1},{9,13},{13,9},{2,6},{6,2},{1... | collective-permute-start | bytes 786440 | tf_op jit(solution)/shard_map/ppermute | solution.py:227
  115.5 9.4 %collective-permute-start.12 = (bf16[256,512]{1,0:T(8,128)(2,1)S(1)}, bf16[256,512]{1,0:T(8,128)(2,1)S(1)}, u32[]{:S(2)}, u32[]{:S(2)}) collective-permute-start(bf16[256,512]{1,0:T(8,128)(2,1)S(1)} %pad_maximum_fusion.4), channel_id=1, source_target_pairs={{0,4},{4,0},{8,12},{12,8},{1,5},{5,1},{9,13},{13,9},{2,6},{6,2},{1... | collective-permute-start | bytes 786440 | tf_op jit(solution)/shard_map/ppermute | solution.py:227
  122.2 4.2 %collective-permute-start.7 = (bf16[512,512]{1,0:T(8,128)(2,1)S(1)}, bf16[512,512]{1,0:T(8,128)(2,1)S(1)}, u32[]{:S(2)}, u32[]{:S(2)}) collective-permute-start(bf16[512,512]{1,0:T(8,128)(2,1)S(1)} %pad_maximum_fusion.1), channel_id=1, source_target_pairs={{0,1},{1,0},{2,3},{3,2},{4,5},{5,4},{6,7},{7,6},{8,9},{9,8},{10,11... | collective-permute-start | bytes 1572872 | tf_op jit(solution)/shard_map/ppermute | solution.py:227
  125.1 2.0 %collective-permute-start.13 = (bf16[512,512]{1,0:T(8,128)(2,1)S(1)}, bf16[512,512]{1,0:T(8,128)(2,1)S(1)}, u32[]{:S(2)}, u32[]{:S(2)}) collective-permute-start(bf16[512,512]{1,0:T(8,128)(2,1)S(1)} %pad_maximum_fusion.2), channel_id=1, source_target_pairs={{0,1},{1,0},{2,3},{3,2},{4,5},{5,4},{6,7},{7,6},{8,9},{9,8},{10,11... | collective-permute-start | bytes 1572872 | tf_op jit(solution)/shard_map/ppermute | solution.py:227
